TPU v7x, 256 devices: a whole 4x4x8 slice. The times are simulated.
256 devices in a mesh: section: 8 (over z_hi, y), dp: 4 (over x), expert: 8 (over z_lo, core).
Axes of the slice: x: 4, y: 4, z: 8 (z_hi: 2, z_lo: 4; z = z_hi * 4 + z_lo), core: 2. Of those that a mesh axis runs over, the one named last changes fastest.
Arguments:
- tokens: bfloat16 [4, 1024, 2048], P(None, ('dp', 'expert')), may hold values from -6 to 6
- cotangent: bfloat16 [4, 1024, 2048], P(None, ('dp', 'expert')), may hold values from -0.29882812 to 0.29882812
- up_proj: bfloat16 [8, 8, 2048, 512], P('section', 'expert'), may hold values from -0.125 to 0.125
- down_proj: bfloat16 [8, 8, 512, 2048], P('section', 'expert'), may hold values from -0.25 to 0.25
- gate_proj: bfloat16 [8, 2048, 8], P('section'), may hold values from -0.125 to 0.125
- routes: int32 [8, 4, 1024, 4], P('section', None, ('dp', 'expert')), may hold values from 0 to 7, all different within a row; in each aligned block of 32 rows (0 to 31, 32 to 63, ..., all dimensions but the last counted through in order) at most 17 rows name the same one
Outputs:
- up_grad: bfloat16 [8, 8, 2048, 512], P('section', 'expert')
- down_grad: bfloat16 [8, 8, 512, 2048], P('section', 'expert')
Inputs may be any that keep to these rules, and one draw needn't show every extreme that they name: `routes`: each row names 4 different experts. Within one layer and micro-batch, the 32 rows of one device name any one expert at most 17 times, a bound that some block reaches.
All inputs are finite; a program needn't handle non-finite values.
Results may differ from a plain program's by a relative error of at most 0.025.
Values may be sent and summed in bfloat16 or wider, within the bound.
A program may use at most 128 MiB of HBM per device.

v0:
```python
import jax
import jax.numpy as jnp
from jax import lax
from jax.sharding import PartitionSpec as P

CAP = 17


epsilon = 1e-06


def from_behind(block, axis, distance):
    devices = range(lax.axis_size(axis))
    route = [(i - distance, i) for i in devices if i - distance in devices]
    return lax.ppermute(block, axis, route)


def normalize(section_in):
    as_f32 = section_in.astype(jnp.float32)
    rscale = lax.rsqrt(jnp.mean(as_f32 * as_f32, axis=-1, keepdims=True) + epsilon)
    return (as_f32, rscale, (as_f32 * rscale).astype(jnp.bfloat16))


def local(tokens, cotangent, up_proj, down_proj, gate_proj, routes):
    section_pos = lax.axis_index("section")
    section_count = lax.axis_size("section")
    expert_devs = lax.axis_size("expert")
    local_experts = up_proj.shape[1]
    experts_all = local_experts * expert_devs
    micro_count, tok_rows, features = tokens.shape
    top_count = routes.shape[3]
    capacity = CAP
    w_up = up_proj[0]
    w_down = down_proj[0]
    gate_cols = gate_proj[0]
    route_all = routes[0]
    step_count = micro_count + section_count - 1
    expert_ids = jnp.arange(experts_all, dtype=jnp.int32)

    def slot_rows(route_rows):
        flat_ids = route_rows.reshape(-1)
        onehot = (flat_ids[:, None] == expert_ids[None, :]).astype(jnp.int32)
        ranks = jnp.cumsum(onehot, axis=0) - onehot
        slots = jnp.sum(ranks * onehot, axis=1)
        return flat_ids * capacity + slots

    def to_buffer(row_values, dest_rows):
        filled = (
            jnp.zeros((experts_all * capacity, features), row_values.dtype)
            .at[dest_rows]
            .set(row_values)
        )
        return filled.reshape(expert_devs, local_experts, capacity, features)

    def from_buffer(buffer, dest_rows):
        return buffer.reshape(experts_all * capacity, features)[dest_rows].reshape(
            tok_rows, top_count, features
        )

    def repeated(normed):
        return jnp.broadcast_to(normed[:, None, :], (tok_rows, top_count, features)).reshape(
            tok_rows * top_count, features
        )

    def gate_values(normed, route_rows):
        logits = jnp.dot(normed, gate_cols, preferred_element_type=jnp.float32)
        return jax.nn.sigmoid(jnp.take_along_axis(logits, route_rows, axis=1))

    def expert_forward(received):
        preact = jnp.einsum("secd,edh->sech", received, w_up, preferred_element_type=jnp.float32)
        hidden = jax.nn.gelu(preact).astype(jnp.bfloat16)
        outbuf = jnp.einsum(
            "sech,ehd->secd", hidden, w_down, preferred_element_type=jnp.float32
        ).astype(jnp.bfloat16)
        return (preact, outbuf)

    def expert_skip(received):
        preact = jnp.zeros(received.shape[:3] + (w_up.shape[2],), jnp.float32)
        return (preact, jnp.zeros_like(received))

    def forward_step(incoming, step_index):
        micro_raw = step_index - section_pos
        live_step = (micro_raw >= 0) & (micro_raw < micro_count)
        micro = jnp.clip(micro_raw, 0, micro_count - 1)
        first_in = lax.dynamic_index_in_dim(tokens, micro, 0, keepdims=False)
        section_in = jnp.where(section_pos == 0, first_in, incoming)
        route_rows = lax.dynamic_index_in_dim(route_all, micro, 0, keepdims=False)
        as_f32, rscale, normed = normalize(section_in)
        gatev = gate_values(normed, route_rows)
        wgt = gatev / jnp.sum(gatev, axis=-1, keepdims=True)
        dest_rows = slot_rows(route_rows)
        received = lax.all_to_all(
            to_buffer(repeated(normed), dest_rows),
            "expert",
            split_axis=0,
            concat_axis=0,
            tiled=True,
        )
        preact, outbuf = lax.cond(live_step, expert_forward, expert_skip, received)
        returned = lax.all_to_all(outbuf, "expert", split_axis=0, concat_axis=0, tiled=True)
        expout = from_buffer(returned, dest_rows)
        section_out = (
            as_f32 + jnp.sum(wgt[..., None] * expout.astype(jnp.float32), axis=1)
        ).astype(jnp.bfloat16)
        passed = from_behind(section_out, "section", 1)
        stored = (section_in, gatev, expout, received, preact)
        return (passed, stored)

    start_act = jnp.zeros((tok_rows, features), jnp.bfloat16)
    _, saved = lax.scan(forward_step, start_act, jnp.arange(step_count))

    def expert_backward(received, dreceived, preact):
        hidden = jax.nn.gelu(preact).astype(jnp.bfloat16)
        down_inc = jnp.einsum(
            "sech,secd->ehd", hidden, dreceived, preferred_element_type=jnp.float32
        )
        dhidden = jnp.einsum(
            "secd,ehd->sech", dreceived, w_down, preferred_element_type=jnp.float32
        )
        _, pullback = jax.vjp(jax.nn.gelu, preact)
        dpre = pullback(dhidden)[0].astype(jnp.bfloat16)
        up_inc = jnp.einsum("secd,sech->edh", received, dpre, preferred_element_type=jnp.float32)
        dinbuf = jnp.einsum(
            "sech,edh->secd", dpre, w_up, preferred_element_type=jnp.float32
        ).astype(jnp.bfloat16)
        return (up_inc, down_inc, dinbuf)

    def backward_skip(operands):
        received = operands[0]
        return (
            jnp.zeros(w_up.shape, jnp.float32),
            jnp.zeros(w_down.shape, jnp.float32),
            jnp.zeros_like(received),
        )

    def backward_step(carry, step_index):
        incoming, acc_up, acc_down = carry
        micro_raw = step_index - (section_count - 1 - section_pos)
        live_step = (micro_raw >= 0) & (micro_raw < micro_count)
        micro = jnp.clip(micro_raw, 0, micro_count - 1)
        fwd_index = micro + section_pos
        section_in = lax.dynamic_index_in_dim(saved[0], fwd_index, 0, keepdims=False)
        gatev = lax.dynamic_index_in_dim(saved[1], fwd_index, 0, keepdims=False)
        expout = lax.dynamic_index_in_dim(saved[2], fwd_index, 0, keepdims=False)
        last_in = lax.dynamic_index_in_dim(cotangent, micro, 0, keepdims=False)
        grad_out = jnp.where(section_pos == section_count - 1, last_in, incoming)
        route_rows = lax.dynamic_index_in_dim(route_all, micro, 0, keepdims=False)
        dest_rows = slot_rows(route_rows)
        as_f32, rscale, normed = normalize(section_in)
        total = jnp.sum(gatev, axis=-1, keepdims=True)
        wgt = gatev / total
        grad_f32 = grad_out.astype(jnp.float32)
        dwgt = jnp.sum(expout.astype(jnp.float32) * grad_f32[:, None, :], axis=-1)
        dout = (
            (wgt[..., None] * grad_f32[:, None, :])
            .astype(jnp.bfloat16)
            .reshape(tok_rows * top_count, features)
        )
        dsend = to_buffer(dout, dest_rows)
        dreceived = lax.all_to_all(dsend, "expert", split_axis=0, concat_axis=0, tiled=True)
        received = lax.dynamic_index_in_dim(saved[3], fwd_index, 0, keepdims=False)
        preact = lax.dynamic_index_in_dim(saved[4], fwd_index, 0, keepdims=False)

        def backward_live(operands):
            return expert_backward(operands[0], operands[1], operands[2])

        up_inc, down_inc, dinbuf = lax.cond(
            live_step, backward_live, backward_skip, (received, dreceived, preact)
        )
        dreturned = lax.all_to_all(dinbuf, "expert", split_axis=0, concat_axis=0, tiled=True)
        dexp = jnp.sum(from_buffer(dreturned, dest_rows).astype(jnp.float32), axis=1)
        dgate = (dwgt - jnp.sum(wgt * dwgt, axis=-1, keepdims=True)) / total
        dlogit = dgate * gatev * (1.0 - gatev)
        onehot = (route_rows[..., None] == expert_ids).astype(jnp.float32)
        dfull = jnp.sum(dlogit[..., None] * onehot, axis=1)
        drouter = jnp.dot(dfull, gate_cols.astype(jnp.float32).T, precision=lax.Precision.HIGHEST)
        dnorm = dexp + drouter
        grad_in = (
            grad_f32
            + rscale * dnorm
            - as_f32 * rscale**3 * jnp.mean(dnorm * as_f32, axis=-1, keepdims=True)
        ).astype(jnp.bfloat16)
        passed = from_behind(grad_in, "section", -1)
        return ((passed, acc_up + up_inc, acc_down + down_inc), None)

    start_carry = (
        jnp.zeros((tok_rows, features), jnp.bfloat16),
        jnp.zeros(w_up.shape, jnp.float32),
        jnp.zeros(w_down.shape, jnp.float32),
    )
    final_carry, _ = lax.scan(backward_step, start_carry, jnp.arange(step_count))
    acc_up = final_carry[1]
    acc_down = final_carry[2]
    sum_up, sum_down = lax.psum((acc_up, acc_down), "dp")
    up_out = sum_up.astype(jnp.bfloat16)
    down_out = sum_down.astype(jnp.bfloat16)
    return (up_out[None], down_out[None])


def solution(mesh):
    in_specs = (
        P(None, ("dp", "expert"), None),
        P(None, ("dp", "expert"), None),
        P("section", "expert", None, None),
        P("section", "expert", None, None),
        P("section", None, None),
        P("section", None, ("dp", "expert"), None),
    )
    out_specs = (P("section", "expert", None, None), P("section", "expert", None, None))
    return jax.shard_map(local, mesh=mesh, in_specs=in_specs, out_specs=out_specs, check_vma=False)
```

profile of v0, /device:TPU:62, one launch (start us, length us, event | category | flops | bytes accessed | tf_op | source)
XLA Modules:
  0.0 1871.0 jit_solution(8187474157075311391)
XLA Ops:
  0.7 817.2 %while.39 = (s32[]{:T(128)}, bf16[32,2048]{1,0:T(8,128)(2,1)S(1)}, bf16[11,32,2048]{2,1,0:T(8,128)(2,1)}, f32[11,32,4]{1,2,0:T(4,128)S(1)}, bf16[11,32,4,2048]{3...) while((s32[]{:T(128)}, bf16[32,2048]{1,0:T(8,128)(2,1)S(1)}, ...), condition=%wide.region_9.10_spmd.clone, body=%wide.region_0.9_spmd.clone.sunk | while | flops 573637120 | bytes 41864460 | solution.py:110
  15.9 15.9 all-to-all-done
  85.6 15.9 all-to-all-done
  159.4 15.9 all-to-all-done
  233.1 15.9 all-to-all-done
  306.9 15.9 all-to-all-done
  383.2 15.9 all-to-all-done
  459.5 15.9 all-to-all-done
  535.8 15.9 all-to-all-done
  612.1 15.9 all-to-all-done
  759.7 15.9 all-to-all-done
  817.9 907.4 %while.40 = (s32[]{:T(128)}, bf16[32,2048]{1,0:T(8,128)(2,1)S(1)}, f32[1,2048,512]{2,1,0:T(8,128)}, f32[1,512,2048]{2,1,0:T(8,128)}, pred[]{:T(512)}, /*index=5*...) while((s32[]{:T(128)}, bf16[32,2048]{1,0:T(8,128)(2,1)S(1)}, ...), condition=%wide.region_23.24_spmd.clone.clone, body=%wide.region_10.23_spmd.clone.clone.sunk | while | flops 1156267392 | bytes 68606576 | solution.py:191
  833.5 16.0 all-to-all-done.2
  914.3 16.0 all-to-all-done.2
  994.4 16.0 all-to-all-done.2
  1074.4 16.0 all-to-all-done.2
  1156.4 16.0 all-to-all-done.2
  1242.5 16.0 all-to-all-done.2
  1328.7 16.0 all-to-all-done.2
  1414.8 16.0 all-to-all-done.2
  1501.0 16.0 all-to-all-done.2
  1581.0 16.0 all-to-all-done.2
  1661.0 16.0 all-to-all-done.2
  1725.3 145.7 %all-reduce.2 = (bf16[1,2048,512]{2,1,0:T(8,128)(2,1)}, bf16[1,512,2048]{2,1,0:T(8,128)(2,1)}) all-reduce(f32[1,2048,512]{2,1,0:T(8,128)} %get-tuple-element.388, f32[1,512,2048]{2,1,0:T(8,128)} %get-tuple-element.389), channel_id=1, replica_groups=mesh['section'=8,'dp'=4,'expert'=8] {'dp'}, use_global_device_ids=true, to_apply=%region_24.25 | all-reduce | flops 2097152 | bytes 12582912 | tf_op jit(solution)/shard_map/psum | solution.py:194
  (1132 shorter events, 1491.8 us)
Async XLA Ops:
  33.6 24.4 %all-to-all-start.1 = ((bf16[8,1,17,2048]{3,2,1,0:T(8,128)(2,1)}), bf16[8,1,17,2048]{3,2,1,0:T(8,128)(2,1)S(1)}, u32[]{:S(2)}, u32[]{:S(2)}) async-start(bf16[8,1,17,2048]{3,2,1,0:T(8,128)(2,1)} %bitcast.207), calls=%async_computation.1 | async-start | bytes 1572864 | tf_op jit(solution)/shard_map/while/body/eval_jaxpr/all_to_all | solution.py:100
  103.2 24.5 %all-to-all-start.1 = ((bf16[8,1,17,2048]{3,2,1,0:T(8,128)(2,1)}), bf16[8,1,17,2048]{3,2,1,0:T(8,128)(2,1)S(1)}, u32[]{:S(2)}, u32[]{:S(2)}) async-start(bf16[8,1,17,2048]{3,2,1,0:T(8,128)(2,1)} %bitcast.207), calls=%async_computation.1 | async-start | bytes 1572864 | tf_op jit(solution)/shard_map/while/body/eval_jaxpr/all_to_all | solution.py:100
  177.0 24.5 %all-to-all-start.1 = ((bf16[8,1,17,2048]{3,2,1,0:T(8,128)(2,1)}), bf16[8,1,17,2048]{3,2,1,0:T(8,128)(2,1)S(1)}, u32[]{:S(2)}, u32[]{:S(2)}) async-start(bf16[8,1,17,2048]{3,2,1,0:T(8,128)(2,1)} %bitcast.207), calls=%async_computation.1 | async-start | bytes 1572864 | tf_op jit(solution)/shard_map/while/body/eval_jaxpr/all_to_all | solution.py:100
  253.3 24.5 %all-to-all-start.1 = ((bf16[8,1,17,2048]{3,2,1,0:T(8,128)(2,1)}), bf16[8,1,17,2048]{3,2,1,0:T(8,128)(2,1)S(1)}, u32[]{:S(2)}, u32[]{:S(2)}) async-start(bf16[8,1,17,2048]{3,2,1,0:T(8,128)(2,1)} %bitcast.207), calls=%async_computation.1 | async-start | bytes 1572864 | tf_op jit(solution)/shard_map/while/body/eval_jaxpr/all_to_all | solution.py:100
  327.1 24.5 %all-to-all-start.1 = ((bf16[8,1,17,2048]{3,2,1,0:T(8,128)(2,1)}), bf16[8,1,17,2048]{3,2,1,0:T(8,128)(2,1)S(1)}, u32[]{:S(2)}, u32[]{:S(2)}) async-start(bf16[8,1,17,2048]{3,2,1,0:T(8,128)(2,1)} %bitcast.207), calls=%async_computation.1 | async-start | bytes 1572864 | tf_op jit(solution)/shard_map/while/body/eval_jaxpr/all_to_all | solution.py:100
  403.3 24.5 %all-to-all-start.1 = ((bf16[8,1,17,2048]{3,2,1,0:T(8,128)(2,1)}), bf16[8,1,17,2048]{3,2,1,0:T(8,128)(2,1)S(1)}, u32[]{:S(2)}, u32[]{:S(2)}) async-start(bf16[8,1,17,2048]{3,2,1,0:T(8,128)(2,1)} %bitcast.207), calls=%async_computation.1 | async-start | bytes 1572864 | tf_op jit(solution)/shard_map/while/body/eval_jaxpr/all_to_all | solution.py:100
  479.6 24.5 %all-to-all-start.1 = ((bf16[8,1,17,2048]{3,2,1,0:T(8,128)(2,1)}), bf16[8,1,17,2048]{3,2,1,0:T(8,128)(2,1)S(1)}, u32[]{:S(2)}, u32[]{:S(2)}) async-start(bf16[8,1,17,2048]{3,2,1,0:T(8,128)(2,1)} %bitcast.207), calls=%async_computation.1 | async-start | bytes 1572864 | tf_op jit(solution)/shard_map/while/body/eval_jaxpr/all_to_all | solution.py:100
  553.5 24.5 %all-to-all-start.1 = ((bf16[8,1,17,2048]{3,2,1,0:T(8,128)(2,1)}), bf16[8,1,17,2048]{3,2,1,0:T(8,128)(2,1)S(1)}, u32[]{:S(2)}, u32[]{:S(2)}) async-start(bf16[8,1,17,2048]{3,2,1,0:T(8,128)(2,1)} %bitcast.207), calls=%async_computation.1 | async-start | bytes 1572864 | tf_op jit(solution)/shard_map/while/body/eval_jaxpr/all_to_all | solution.py:100
  629.7 24.5 %all-to-all-start.1 = ((bf16[8,1,17,2048]{3,2,1,0:T(8,128)(2,1)}), bf16[8,1,17,2048]{3,2,1,0:T(8,128)(2,1)S(1)}, u32[]{:S(2)}, u32[]{:S(2)}) async-start(bf16[8,1,17,2048]{3,2,1,0:T(8,128)(2,1)} %bitcast.207), calls=%async_computation.1 | async-start | bytes 1572864 | tf_op jit(solution)/shard_map/while/body/eval_jaxpr/all_to_all | solution.py:100
  703.6 24.5 %all-to-all-start.1 = ((bf16[8,1,17,2048]{3,2,1,0:T(8,128)(2,1)}), bf16[8,1,17,2048]{3,2,1,0:T(8,128)(2,1)S(1)}, u32[]{:S(2)}, u32[]{:S(2)}) async-start(bf16[8,1,17,2048]{3,2,1,0:T(8,128)(2,1)} %bitcast.207), calls=%async_computation.1 | async-start | bytes 1572864 | tf_op jit(solution)/shard_map/while/body/eval_jaxpr/all_to_all | solution.py:100
  777.4 24.5 %all-to-all-start.1 = ((bf16[8,1,17,2048]{3,2,1,0:T(8,128)(2,1)}), bf16[8,1,17,2048]{3,2,1,0:T(8,128)(2,1)S(1)}, u32[]{:S(2)}, u32[]{:S(2)}) async-start(bf16[8,1,17,2048]{3,2,1,0:T(8,128)(2,1)} %bitcast.207), calls=%async_computation.1 | async-start | bytes 1572864 | tf_op jit(solution)/shard_map/while/body/eval_jaxpr/all_to_all | solution.py:100
  855.5 24.5 %all-to-all-start.3 = ((bf16[8,1,17,2048]{3,2,1,0:T(8,128)(2,1)}), bf16[8,1,17,2048]{3,2,1,0:T(8,128)(2,1)S(1)}, u32[]{:S(2)}, u32[]{:S(2)}) async-start(bf16[8,1,17,2048]{3,2,1,0:T(8,128)(2,1)} %bitcast.220), calls=%async_computation.3 | async-start | bytes 1572864 | tf_op jit(solution)/shard_map/while/body/eval_jaxpr/all_to_all | solution.py:170
  936.3 24.5 %all-to-all-start.3 = ((bf16[8,1,17,2048]{3,2,1,0:T(8,128)(2,1)}), bf16[8,1,17,2048]{3,2,1,0:T(8,128)(2,1)S(1)}, u32[]{:S(2)}, u32[]{:S(2)}) async-start(bf16[8,1,17,2048]{3,2,1,0:T(8,128)(2,1)} %bitcast.220), calls=%async_computation.3 | async-start | bytes 1572864 | tf_op jit(solution)/shard_map/while/body/eval_jaxpr/all_to_all | solution.py:170
  1016.4 24.5 %all-to-all-start.3 = ((bf16[8,1,17,2048]{3,2,1,0:T(8,128)(2,1)}), bf16[8,1,17,2048]{3,2,1,0:T(8,128)(2,1)S(1)}, u32[]{:S(2)}, u32[]{:S(2)}) async-start(bf16[8,1,17,2048]{3,2,1,0:T(8,128)(2,1)} %bitcast.220), calls=%async_computation.3 | async-start | bytes 1572864 | tf_op jit(solution)/shard_map/while/body/eval_jaxpr/all_to_all | solution.py:170
  1096.4 24.5 %all-to-all-start.3 = ((bf16[8,1,17,2048]{3,2,1,0:T(8,128)(2,1)}), bf16[8,1,17,2048]{3,2,1,0:T(8,128)(2,1)S(1)}, u32[]{:S(2)}, u32[]{:S(2)}) async-start(bf16[8,1,17,2048]{3,2,1,0:T(8,128)(2,1)} %bitcast.220), calls=%async_computation.3 | async-start | bytes 1572864 | tf_op jit(solution)/shard_map/while/body/eval_jaxpr/all_to_all | solution.py:170
  1184.5 24.5 %all-to-all-start.3 = ((bf16[8,1,17,2048]{3,2,1,0:T(8,128)(2,1)}), bf16[8,1,17,2048]{3,2,1,0:T(8,128)(2,1)S(1)}, u32[]{:S(2)}, u32[]{:S(2)}) async-start(bf16[8,1,17,2048]{3,2,1,0:T(8,128)(2,1)} %bitcast.220), calls=%async_computation.3 | async-start | bytes 1572864 | tf_op jit(solution)/shard_map/while/body/eval_jaxpr/all_to_all | solution.py:170
  1270.7 24.5 %all-to-all-start.3 = ((bf16[8,1,17,2048]{3,2,1,0:T(8,128)(2,1)}), bf16[8,1,17,2048]{3,2,1,0:T(8,128)(2,1)S(1)}, u32[]{:S(2)}, u32[]{:S(2)}) async-start(bf16[8,1,17,2048]{3,2,1,0:T(8,128)(2,1)} %bitcast.220), calls=%async_computation.3 | async-start | bytes 1572864 | tf_op jit(solution)/shard_map/while/body/eval_jaxpr/all_to_all | solution.py:170
  1356.8 24.5 %all-to-all-start.3 = ((bf16[8,1,17,2048]{3,2,1,0:T(8,128)(2,1)}), bf16[8,1,17,2048]{3,2,1,0:T(8,128)(2,1)S(1)}, u32[]{:S(2)}, u32[]{:S(2)}) async-start(bf16[8,1,17,2048]{3,2,1,0:T(8,128)(2,1)} %bitcast.220), calls=%async_computation.3 | async-start | bytes 1572864 | tf_op jit(solution)/shard_map/while/body/eval_jaxpr/all_to_all | solution.py:170
  1443.0 24.5 %all-to-all-start.3 = ((bf16[8,1,17,2048]{3,2,1,0:T(8,128)(2,1)}), bf16[8,1,17,2048]{3,2,1,0:T(8,128)(2,1)S(1)}, u32[]{:S(2)}, u32[]{:S(2)}) async-start(bf16[8,1,17,2048]{3,2,1,0:T(8,128)(2,1)} %bitcast.220), calls=%async_computation.3 | async-start | bytes 1572864 | tf_op jit(solution)/shard_map/while/body/eval_jaxpr/all_to_all | solution.py:170
  1523.0 24.5 %all-to-all-start.3 = ((bf16[8,1,17,2048]{3,2,1,0:T(8,128)(2,1)}), bf16[8,1,17,2048]{3,2,1,0:T(8,128)(2,1)S(1)}, u32[]{:S(2)}, u32[]{:S(2)}) async-start(bf16[8,1,17,2048]{3,2,1,0:T(8,128)(2,1)} %bitcast.220), calls=%async_computation.3 | async-start | bytes 1572864 | tf_op jit(solution)/shard_map/while/body/eval_jaxpr/all_to_all | solution.py:170
  1572.9 24.1 %all-to-all-start.2 = ((bf16[8,1,17,2048]{3,2,1,0:T(8,128)(2,1)}), bf16[8,1,17,2048]{3,2,1,0:T(8,128)(2,1)S(1)}, u32[]{:S(2)}, u32[]{:S(2)}) async-start(bf16[8,1,17,2048]{3,2,1,0:T(8,128)(2,1)} %bitcast.219), calls=%async_computation.2 | async-start | bytes 1572864 | tf_op jit(solution)/shard_map/while/body/eval_jaxpr/all_to_all | solution.py:160
  1603.0 24.5 %all-to-all-start.3 = ((bf16[8,1,17,2048]{3,2,1,0:T(8,128)(2,1)}), bf16[8,1,17,2048]{3,2,1,0:T(8,128)(2,1)S(1)}, u32[]{:S(2)}, u32[]{:S(2)}) async-start(bf16[8,1,17,2048]{3,2,1,0:T(8,128)(2,1)} %bitcast.220), calls=%async_computation.3 | async-start | bytes 1572864 | tf_op jit(solution)/shard_map/while/body/eval_jaxpr/all_to_all | solution.py:170
  1652.8 24.1 %all-to-all-start.2 = ((bf16[8,1,17,2048]{3,2,1,0:T(8,128)(2,1)}), bf16[8,1,17,2048]{3,2,1,0:T(8,128)(2,1)S(1)}, u32[]{:S(2)}, u32[]{:S(2)}) async-start(bf16[8,1,17,2048]{3,2,1,0:T(8,128)(2,1)} %bitcast.219), calls=%async_computation.2 | async-start | bytes 1572864 | tf_op jit(solution)/shard_map/while/body/eval_jaxpr/all_to_all | solution.py:160
  1683.0 24.5 %all-to-all-start.3 = ((bf16[8,1,17,2048]{3,2,1,0:T(8,128)(2,1)}), bf16[8,1,17,2048]{3,2,1,0:T(8,128)(2,1)S(1)}, u32[]{:S(2)}, u32[]{:S(2)}) async-start(bf16[8,1,17,2048]{3,2,1,0:T(8,128)(2,1)} %bitcast.220), calls=%async_computation.3 | async-start | bytes 1572864 | tf_op jit(solution)/shard_map/while/body/eval_jaxpr/all_to_all | solution.py:170
  (83 other events, 1288.5 us)
where the time goes:
time: 1880 us; the launch traced here: 1870 us
  waiting for transfers between devices  711 us (38%)
  starting transfers between devices  428 us (23%)
  other arithmetic  259 us (14%)
  local copies, waits for them, and re-layouts  228 us (12%)
  blocking collectives  146 us (8%)
  matrix products  80.3 us (4%)
    all_to_all x11, waiting for transfers between devices, backward_step(): lax.all_to_all(dsend, 'expert', split_axis=0, concat_axis=0, tiled=True)  176 us
    all_to_all x11, waiting for transfers between devices, forward_step(): lax.all_to_all(to_buffer(repeated(normed), dest_rows), 'expert', split_ax...  175 us
    all_to_all x11, waiting for transfers between devices, forward_step(): lax.all_to_all(outbuf, 'expert', split_axis=0, concat_axis=0, tiled=True)  159 us
    psum x1, blocking collectives, local(): sum_up, sum_down = lax.psum((acc_up, acc_down), 'dp')  146 us
    add x22, other arithmetic, backward_step(): return ((passed, acc_up + up_inc, acc_down + down_inc), None)  143 us
    ppermute x22, starting transfers between devices, from_behind(): return lax.ppermute(block, axis, route)  133 us
    all_to_all x11, waiting for transfers between devices, backward_step(): lax.all_to_all(dinbuf, 'expert', split_axis=0, concat_axis=0, tiled=True)  122 us
    ppermute x22, waiting for transfers between devices, from_behind(): return lax.ppermute(block, axis, route)  79.6 us
  transfers between devices with their start and end apart: 66, of which 66 were waited for; matrix products, arithmetic and copies ran while one was open for 12% of the time, Pallas kernels for 0%

commit v1 on v0

--- a/solution.py
+++ b/solution.py
@@ -1,7 +1,13 @@
+import functools
+
 import jax
 import jax.numpy as jnp
 from jax import lax
+from jax.experimental import pallas as pl
+from jax.experimental.pallas import tpu as pltpu
 from jax.sharding import PartitionSpec as P
+
+MESH = pl.DeviceIdType.MESH
 
 CAP = 17
 
@@ -13,6 +19,52 @@
     devices = range(lax.axis_size(axis))
     route = [(i - distance, i) for i in devices if i - distance in devices]
     return lax.ppermute(block, axis, route)
+
+
+def exchange_kernel(n, x_ref, o_ref, copy_sem, send_sem, recv_sem):
+    me = lax.axis_index("expert")
+    barrier = pltpu.get_barrier_semaphore()
+    for j in range(1, n):
+        pl.semaphore_signal(
+            barrier, inc=1, device_id={"expert": lax.rem(me + j, n)}, device_id_type=MESH
+        )
+    pl.semaphore_wait(barrier, n - 1)
+    local = pltpu.make_async_copy(x_ref.at[me], o_ref.at[me], copy_sem)
+    local.start()
+    copies = []
+    for j in range(1, n):
+        peer = lax.rem(me + j, n)
+        copy = pltpu.make_async_remote_copy(
+            src_ref=x_ref.at[peer],
+            dst_ref=o_ref.at[me],
+            send_sem=send_sem.at[j],
+            recv_sem=recv_sem.at[j],
+            device_id={"expert": peer},
+            device_id_type=MESH,
+        )
+        copy.start()
+        copies.append(copy)
+    local.wait()
+    for copy in copies:
+        copy.wait()
+
+
+def expert_exchange(block, site):
+    n = block.shape[0]
+    nbytes = block.size * block.dtype.itemsize
+    return pl.pallas_call(
+        functools.partial(exchange_kernel, n),
+        out_shape=jax.ShapeDtypeStruct(block.shape, block.dtype),
+        in_specs=[pl.BlockSpec(memory_space=pl.ANY)],
+        out_specs=pl.BlockSpec(memory_space=pl.ANY),
+        scratch_shapes=[
+            pltpu.SemaphoreType.DMA(()),
+            pltpu.SemaphoreType.DMA((n,)),
+            pltpu.SemaphoreType.DMA((n,)),
+        ],
+        compiler_params=pltpu.CompilerParams(collective_id=site, has_side_effects=True),
+        cost_estimate=pl.CostEstimate(flops=0, bytes_accessed=2 * nbytes, transcendentals=0),
+    )(block)
 
 
 def normalize(section_in):
@@ -89,15 +141,9 @@
         gatev = gate_values(normed, route_rows)
         wgt = gatev / jnp.sum(gatev, axis=-1, keepdims=True)
         dest_rows = slot_rows(route_rows)
-        received = lax.all_to_all(
-            to_buffer(repeated(normed), dest_rows),
-            "expert",
-            split_axis=0,
-            concat_axis=0,
-            tiled=True,
-        )
+        received = expert_exchange(to_buffer(repeated(normed), dest_rows), 3)
         preact, outbuf = lax.cond(live_step, expert_forward, expert_skip, received)
-        returned = lax.all_to_all(outbuf, "expert", split_axis=0, concat_axis=0, tiled=True)
+        returned = expert_exchange(outbuf, 0)
         expout = from_buffer(returned, dest_rows)
         section_out = (
             as_f32 + jnp.sum(wgt[..., None] * expout.astype(jnp.float32), axis=1)
@@ -157,7 +203,7 @@
             .reshape(tok_rows * top_count, features)
         )
         dsend = to_buffer(dout, dest_rows)
-        dreceived = lax.all_to_all(dsend, "expert", split_axis=0, concat_axis=0, tiled=True)
+        dreceived = expert_exchange(dsend, 1)
         received = lax.dynamic_index_in_dim(saved[3], fwd_index, 0, keepdims=False)
         preact = lax.dynamic_index_in_dim(saved[4], fwd_index, 0, keepdims=False)
 
@@ -167,7 +213,7 @@
         up_inc, down_inc, dinbuf = lax.cond(
             live_step, backward_live, backward_skip, (received, dreceived, preact)
         )
-        dreturned = lax.all_to_all(dinbuf, "expert", split_axis=0, concat_axis=0, tiled=True)
+        dreturned = expert_exchange(dinbuf, 2)
         dexp = jnp.sum(from_buffer(dreturned, dest_rows).astype(jnp.float32), axis=1)
         dgate = (dwgt - jnp.sum(wgt * dwgt, axis=-1, keepdims=True)) / total
         dlogit = dgate * gatev * (1.0 - gatev)

time: 1880 us -> 1800 us (0.957)
  Pallas kernels: 0 us -> 855 us
  waiting for transfers between devices: 711 us -> 56.6 us
  starting transfers between devices: 428 us -> 132 us
    pallas_call x0 -> x44, Pallas kernels: none -> 855 us  [expert_exchange(): pl.pallas_call(functools.partial(exchange_kernel, n), out_shape=jax.Shape...]
    all_to_all x44 -> x0, waiting for transfers between devices: 632 us -> none  [the longest x11 176 us: backward_step(): lax.all_to_all(dsend, 'expert', split_axis=0, concat_axis=0, tiled=True)]
    all_to_all x44 -> x0, starting transfers between devices: 295 us -> none  [the longest x11 76.5 us: backward_step(): lax.all_to_all(dinbuf, 'expert', split_axis=0, concat_axis=0, tiled=True)]
    reshape x22, local copies, waits for them, and re-layouts: 4.59 us -> 29.6 us  [from_buffer(): buffer.reshape(experts_all * capacity, features)[dest_rows]]
    ppermute x22, waiting for transfers between devices: 79.6 us -> 56.6 us  [from_behind(): return lax.ppermute(block, axis, route)]
  transfers between devices with their start and end apart: 66 -> 22, of which waited for: 66 -> 22; matrix products, arithmetic and copies ran while one was open for 12% -> 11% of each run, Pallas kernels for 0% -> 0%
where the time goes in v1:
time: 1800 us; the launch traced here: 1790 us
  Pallas kernels  855 us (48%)
  other arithmetic  260 us (14%)
  local copies, waits for them, and re-layouts  239 us (13%)
  blocking collectives  148 us (8%)
  starting transfers between devices  132 us (7%)
  matrix products  81.3 us (5%)
  waiting for transfers between devices  56.6 us (3%)
  loops' own time  19.5 us (1%)
    pallas_call x44, Pallas kernels, expert_exchange(): pl.pallas_call(functools.partial(exchange_kernel, n), out_shape=jax.Shape...  855 us
    psum x1, blocking collectives, local(): sum_up, sum_down = lax.psum((acc_up, acc_down), 'dp')  148 us
    add x22, other arithmetic, backward_step(): return ((passed, acc_up + up_inc, acc_down + down_inc), None)  143 us
    ppermute x22, starting transfers between devices, from_behind(): return lax.ppermute(block, axis, route)  132 us
    ppermute x22, waiting for transfers between devices, from_behind(): return lax.ppermute(block, axis, route)  56.6 us
    dynamic_update_slice x33, local copies, waits for them, and re-layouts, local(): _, saved = lax.scan(forward_step, start_act, jnp.arange(step_count))  41.5 us
    another operation x30, local copies, waits for them, and re-layouts  36.5 us
  transfers between devices with their start and end apart: 22, of which 22 were waited for; matrix products, arithmetic and copies ran while one was open for 11% of the time, Pallas kernels for 0%

profile of v1, /device:TPU:62, one launch (start us, length us, event | category | flops | bytes accessed | tf_op | source)
XLA Modules:
  0.0 1791.8 jit_solution(994197975681552875)
XLA Ops:
  0.7 775.1 %while.39 = (s32[]{:T(128)}, bf16[32,2048]{1,0:T(8,128)(2,1)S(1)}, bf16[11,32,2048]{2,1,0:T(8,128)(2,1)}, f32[11,32,4]{1,2,0:T(4,128)S(1)}, bf16[11,32,4,2048]{3...) while((s32[]{:T(128)}, bf16[32,2048]{1,0:T(8,128)(2,1)S(1)}, ...), condition=%wide.region_9.10_spmd.clone, body=%wide.region_0.9_spmd.clone.sunk | while | flops 573637120 | bytes 31444144 | solution.py:156
  8.3 21.1 %eval_jaxpr.8 = bf16[8,1,17,2048]{3,2,1,0:T(8,128)(2,1)S(1)} custom-call(bf16[8,1,17,2048]{3,2,1,0:T(8,128)(2,1)} %bitcast.224), custom_call_target="tpu_custom_call" | custom-call | bytes 1114112 | tf_op jit(solution)/shard_map/while/body/eval_jaxpr/pallas_call | solution.py:55
  30.4 20.3 %eval_jaxpr.9 = bf16[8,1,17,2048]{3,2,1,0:T(8,128)(2,1)} custom-call(bf16[8,1,17,2048]{3,2,1,0:T(8,128)(2,1)S(1)} %bitcast.222), custom_call_target="tpu_custom_call" | custom-call | bytes 1114112 | tf_op jit(solution)/shard_map/while/body/eval_jaxpr/pallas_call | solution.py:55
  95.7 19.8 %eval_jaxpr.9 = bf16[8,1,17,2048]{3,2,1,0:T(8,128)(2,1)} custom-call(bf16[8,1,17,2048]{3,2,1,0:T(8,128)(2,1)S(1)} %bitcast.222), custom_call_target="tpu_custom_call" | custom-call | bytes 1114112 | tf_op jit(solution)/shard_map/while/body/eval_jaxpr/pallas_call | solution.py:55
  164.7 19.8 %eval_jaxpr.9 = bf16[8,1,17,2048]{3,2,1,0:T(8,128)(2,1)} custom-call(bf16[8,1,17,2048]{3,2,1,0:T(8,128)(2,1)S(1)} %bitcast.222), custom_call_target="tpu_custom_call" | custom-call | bytes 1114112 | tf_op jit(solution)/shard_map/while/body/eval_jaxpr/pallas_call | solution.py:55
  237.8 20.0 %eval_jaxpr.9 = bf16[8,1,17,2048]{3,2,1,0:T(8,128)(2,1)} custom-call(bf16[8,1,17,2048]{3,2,1,0:T(8,128)(2,1)S(1)} %bitcast.222), custom_call_target="tpu_custom_call" | custom-call | bytes 1114112 | tf_op jit(solution)/shard_map/while/body/eval_jaxpr/pallas_call | solution.py:55
  307.0 20.0 %eval_jaxpr.9 = bf16[8,1,17,2048]{3,2,1,0:T(8,128)(2,1)} custom-call(bf16[8,1,17,2048]{3,2,1,0:T(8,128)(2,1)S(1)} %bitcast.222), custom_call_target="tpu_custom_call" | custom-call | bytes 1114112 | tf_op jit(solution)/shard_map/while/body/eval_jaxpr/pallas_call | solution.py:55
  380.1 20.0 %eval_jaxpr.9 = bf16[8,1,17,2048]{3,2,1,0:T(8,128)(2,1)} custom-call(bf16[8,1,17,2048]{3,2,1,0:T(8,128)(2,1)S(1)} %bitcast.222), custom_call_target="tpu_custom_call" | custom-call | bytes 1114112 | tf_op jit(solution)/shard_map/while/body/eval_jaxpr/pallas_call | solution.py:55
  453.1 20.0 %eval_jaxpr.9 = bf16[8,1,17,2048]{3,2,1,0:T(8,128)(2,1)} custom-call(bf16[8,1,17,2048]{3,2,1,0:T(8,128)(2,1)S(1)} %bitcast.222), custom_call_target="tpu_custom_call" | custom-call | bytes 1114112 | tf_op jit(solution)/shard_map/while/body/eval_jaxpr/pallas_call | solution.py:55
  595.6 19.8 %eval_jaxpr.9 = bf16[8,1,17,2048]{3,2,1,0:T(8,128)(2,1)} custom-call(bf16[8,1,17,2048]{3,2,1,0:T(8,128)(2,1)S(1)} %bitcast.222), custom_call_target="tpu_custom_call" | custom-call | bytes 1114112 | tf_op jit(solution)/shard_map/while/body/eval_jaxpr/pallas_call | solution.py:55
  664.7 19.8 %eval_jaxpr.9 = bf16[8,1,17,2048]{3,2,1,0:T(8,128)(2,1)} custom-call(bf16[8,1,17,2048]{3,2,1,0:T(8,128)(2,1)S(1)} %bitcast.222), custom_call_target="tpu_custom_call" | custom-call | bytes 1114112 | tf_op jit(solution)/shard_map/while/body/eval_jaxpr/pallas_call | solution.py:55
  775.8 868.4 %while.40 = (s32[]{:T(128)}, bf16[32,2048]{1,0:T(8,128)(2,1)S(1)}, f32[1,2048,512]{2,1,0:T(8,128)}, f32[1,512,2048]{2,1,0:T(8,128)}, pred[]{:T(512)}, /*index=5*...) while((s32[]{:T(128)}, bf16[32,2048]{1,0:T(8,128)(2,1)S(1)}, ...), condition=%wide.region_23.24_spmd.clone.clone, body=%wide.region_10.23_spmd.clone.clone.sunk | while | flops 1156267392 | bytes 71031400 | solution.py:237
  807.3 20.0 %eval_jaxpr.11 = bf16[8,1,17,2048]{3,2,1,0:T(8,128)(2,1)} custom-call(bf16[8,1,17,2048]{3,2,1,0:T(8,128)(2,1)S(1)} %bitcast.223), custom_call_target="tpu_custom_call" | custom-call | bytes 1114112 | tf_op jit(solution)/shard_map/while/body/eval_jaxpr/pallas_call | solution.py:55
  883.2 20.0 %eval_jaxpr.11 = bf16[8,1,17,2048]{3,2,1,0:T(8,128)(2,1)} custom-call(bf16[8,1,17,2048]{3,2,1,0:T(8,128)(2,1)S(1)} %bitcast.223), custom_call_target="tpu_custom_call" | custom-call | bytes 1114112 | tf_op jit(solution)/shard_map/while/body/eval_jaxpr/pallas_call | solution.py:55
  959.0 20.4 %eval_jaxpr.11 = bf16[8,1,17,2048]{3,2,1,0:T(8,128)(2,1)} custom-call(bf16[8,1,17,2048]{3,2,1,0:T(8,128)(2,1)S(1)} %bitcast.223), custom_call_target="tpu_custom_call" | custom-call | bytes 1114112 | tf_op jit(solution)/shard_map/while/body/eval_jaxpr/pallas_call | solution.py:55
  1035.3 20.4 %eval_jaxpr.11 = bf16[8,1,17,2048]{3,2,1,0:T(8,128)(2,1)} custom-call(bf16[8,1,17,2048]{3,2,1,0:T(8,128)(2,1)S(1)} %bitcast.223), custom_call_target="tpu_custom_call" | custom-call | bytes 1114112 | tf_op jit(solution)/shard_map/while/body/eval_jaxpr/pallas_call | solution.py:55
  1123.7 19.8 %eval_jaxpr.11 = bf16[8,1,17,2048]{3,2,1,0:T(8,128)(2,1)} custom-call(bf16[8,1,17,2048]{3,2,1,0:T(8,128)(2,1)S(1)} %bitcast.223), custom_call_target="tpu_custom_call" | custom-call | bytes 1114112 | tf_op jit(solution)/shard_map/while/body/eval_jaxpr/pallas_call | solution.py:55
  1206.2 19.8 %eval_jaxpr.11 = bf16[8,1,17,2048]{3,2,1,0:T(8,128)(2,1)} custom-call(bf16[8,1,17,2048]{3,2,1,0:T(8,128)(2,1)S(1)} %bitcast.223), custom_call_target="tpu_custom_call" | custom-call | bytes 1114112 | tf_op jit(solution)/shard_map/while/body/eval_jaxpr/pallas_call | solution.py:55
  1288.7 19.9 %eval_jaxpr.11 = bf16[8,1,17,2048]{3,2,1,0:T(8,128)(2,1)} custom-call(bf16[8,1,17,2048]{3,2,1,0:T(8,128)(2,1)S(1)} %bitcast.223), custom_call_target="tpu_custom_call" | custom-call | bytes 1114112 | tf_op jit(solution)/shard_map/while/body/eval_jaxpr/pallas_call | solution.py:55
  1371.4 19.8 %eval_jaxpr.11 = bf16[8,1,17,2048]{3,2,1,0:T(8,128)(2,1)} custom-call(bf16[8,1,17,2048]{3,2,1,0:T(8,128)(2,1)S(1)} %bitcast.223), custom_call_target="tpu_custom_call" | custom-call | bytes 1114112 | tf_op jit(solution)/shard_map/while/body/eval_jaxpr/pallas_call | solution.py:55
  1447.0 20.4 %eval_jaxpr.11 = bf16[8,1,17,2048]{3,2,1,0:T(8,128)(2,1)} custom-call(bf16[8,1,17,2048]{3,2,1,0:T(8,128)(2,1)S(1)} %bitcast.223), custom_call_target="tpu_custom_call" | custom-call | bytes 1114112 | tf_op jit(solution)/shard_map/while/body/eval_jaxpr/pallas_call | solution.py:55
  1523.2 20.4 %eval_jaxpr.11 = bf16[8,1,17,2048]{3,2,1,0:T(8,128)(2,1)} custom-call(bf16[8,1,17,2048]{3,2,1,0:T(8,128)(2,1)S(1)} %bitcast.223), custom_call_target="tpu_custom_call" | custom-call | bytes 1114112 | tf_op jit(solution)/shard_map/while/body/eval_jaxpr/pallas_call | solution.py:55
  1599.5 20.4 %eval_jaxpr.11 = bf16[8,1,17,2048]{3,2,1,0:T(8,128)(2,1)} custom-call(bf16[8,1,17,2048]{3,2,1,0:T(8,128)(2,1)S(1)} %bitcast.223), custom_call_target="tpu_custom_call" | custom-call | bytes 1114112 | tf_op jit(solution)/shard_map/while/body/eval_jaxpr/pallas_call | solution.py:55
  1644.2 147.6 %all-reduce.2 = (bf16[1,2048,512]{2,1,0:T(8,128)(2,1)}, bf16[1,512,2048]{2,1,0:T(8,128)(2,1)}) all-reduce(f32[1,2048,512]{2,1,0:T(8,128)} %get-tuple-element.388, f32[1,512,2048]{2,1,0:T(8,128)} %get-tuple-element.389), channel_id=1, replica_groups=mesh['section'=8,'dp'=4,'expert'=8] {'dp'}, use_global_device_ids=true, to_apply=%region_24.25 | all-reduce | flops 2097152 | bytes 12582912 | tf_op jit(solution)/shard_map/psum | solution.py:240
  (1082 shorter events, 1309.4 us)
Async XLA Ops:
  55.8 12.7 collective-permute-start
  120.7 16.8 collective-permute-start
  189.7 17.0 collective-permute-start
  262.9 13.0 collective-permute-start
  332.1 16.9 collective-permute-start
  405.2 16.9 collective-permute-start
  478.3 17.1 collective-permute-start
  547.5 21.0 %collective-permute-start = (bf16[32,2048]{1,0:T(8,128)(2,1)S(1)}, bf16[32,2048]{1,0:T(8,128)(2,1)S(1)}, u32[]{:S(2)}, u32[]{:S(2)}) collective-permute-start(bf16[32,2048]{1,0:T(8,128)(2,1)S(1)} %fusion.144), channel_id=1, source_target_pairs={{0,32},{32,64},{64,96},{96,128},{128,160},{160,192},{192,224},{1,3... | collective-permute-start | bytes 393224 | tf_op jit(solution)/shard_map/while/body/eval_jaxpr/ppermute | solution.py:21
  620.6 16.9 collective-permute-start
  689.7 16.9 collective-permute-start
  758.8 17.0 collective-permute-start
  834.6 17.3 collective-permute-start.1
  910.5 17.0 collective-permute-start.1
  986.7 17.2 collective-permute-start.1
  1062.9 22.9 %collective-permute-start.1 = (bf16[32,2048]{1,0:T(8,128)(2,1)S(1)}, bf16[32,2048]{1,0:T(8,128)(2,1)S(1)}, u32[]{:S(2)}, u32[]{:S(2)}) collective-permute-start(bf16[32,2048]{1,0:T(8,128)(2,1)S(1)} %fusion.157), channel_id=1, source_target_pairs={{32,0},{64,32},{96,64},{128,96},{160,128},{192,160},{224,192},{33,... | collective-permute-start | bytes 393224 | tf_op jit(solution)/shard_map/while/body/eval_jaxpr/ppermute | solution.py:21
  1115.0 5.0 copy-start.3
  1150.7 17.7 collective-permute-start.1
  1233.3 17.6 collective-permute-start.1
  1280.0 5.0 copy-start.3
  1315.8 17.7 collective-permute-start.1
  1398.4 16.9 collective-permute-start.1
  1474.6 17.2 collective-permute-start.1
  1550.9 17.0 collective-permute-start.1
  1627.1 17.1 collective-permute-start.1
  (36 other events, 117.6 us)

commit v2 on v1

--- a/solution.py
+++ b/solution.py
@@ -172,12 +172,8 @@
         return (up_inc, down_inc, dinbuf)
 
     def backward_skip(operands):
-        received = operands[0]
-        return (
-            jnp.zeros(w_up.shape, jnp.float32),
-            jnp.zeros(w_down.shape, jnp.float32),
-            jnp.zeros_like(received),
-        )
+        received, acc_up, acc_down = operands[0], operands[3], operands[4]
+        return (acc_up, acc_down, jnp.zeros_like(received))
 
     def backward_step(carry, step_index):
         incoming, acc_up, acc_down = carry
@@ -208,10 +204,14 @@
         preact = lax.dynamic_index_in_dim(saved[4], fwd_index, 0, keepdims=False)
 
         def backward_live(operands):
-            return expert_backward(operands[0], operands[1], operands[2])
-
-        up_inc, down_inc, dinbuf = lax.cond(
-            live_step, backward_live, backward_skip, (received, dreceived, preact)
+            up_inc, down_inc, dinbuf = expert_backward(operands[0], operands[1], operands[2])
+            return (operands[3] + up_inc, operands[4] + down_inc, dinbuf)
+
+        new_up, new_down, dinbuf = lax.cond(
+            live_step,
+            backward_live,
+            backward_skip,
+            (received, dreceived, preact, acc_up, acc_down),
         )
         dreturned = expert_exchange(dinbuf, 2)
         dexp = jnp.sum(from_buffer(dreturned, dest_rows).astype(jnp.float32), axis=1)
@@ -227,7 +227,7 @@
             - as_f32 * rscale**3 * jnp.mean(dnorm * as_f32, axis=-1, keepdims=True)
         ).astype(jnp.bfloat16)
         passed = from_behind(grad_in, "section", -1)
-        return ((passed, acc_up + up_inc, acc_down + down_inc), None)
+        return ((passed, new_up, new_down), None)
 
     start_carry = (
         jnp.zeros((tok_rows, features), jnp.bfloat16),
@@ -237,7 +237,9 @@
     final_carry, _ = lax.scan(backward_step, start_carry, jnp.arange(step_count))
     acc_up = final_carry[1]
     acc_down = final_carry[2]
-    sum_up, sum_down = lax.psum((acc_up, acc_down), "dp")
+    sum_up, sum_down = lax.psum(
+        (acc_up.astype(jnp.bfloat16), acc_down.astype(jnp.bfloat16)), "dp"
+    )
     up_out = sum_up.astype(jnp.bfloat16)
     down_out = sum_down.astype(jnp.bfloat16)
     return (up_out[None], down_out[None])

time: 1800 us -> 1720 us (0.956)
  waiting for transfers between devices: 56.6 us -> 283 us
  blocking collectives: 148 us -> 0 us
  other arithmetic: 260 us -> 123 us
    psum x1 -> x0, blocking collectives: 148 us -> none  [local(): sum_up, sum_down = lax.psum((acc_up, acc_down), 'dp')]
    add x22 -> x0, other arithmetic: 143 us -> none  [backward_step(): return ((passed, acc_up + up_inc, acc_down + down_inc), None)]
    ppermute x22, waiting for transfers between devices: 56.6 us -> 189 us  [from_behind(): return lax.ppermute(block, axis, route)]
    psum x0 -> x1, waiting for transfers between devices: none -> 93.3 us  [local(): lax.psum((acc_up.astype(jnp.bfloat16), acc_down.astype(jnp.bfloat16)), 'dp')]
    another operation x30 -> x16, local copies, waits for them, and re-layouts: 36.5 us -> 1.11 us
  transfers between devices with their start and end apart: 22 -> 23, of which waited for: 22 -> 23; matrix products, arithmetic and copies ran while one was open for 11% -> 3% of each run, Pallas kernels for 0% -> 0%
where the time goes in v2:
time: 1720 us; the launch traced here: 1710 us
  Pallas kernels  852 us (50%)
  waiting for transfers between devices  283 us (16%)
  local copies, waits for them, and re-layouts  222 us (13%)
  starting transfers between devices  135 us (8%)
  other arithmetic  123 us (7%)
  matrix products  67.2 us (4%)
  loops' own time  19.4 us (1%)
    pallas_call x44, Pallas kernels, expert_exchange(): pl.pallas_call(functools.partial(exchange_kernel, n), out_shape=jax.Shape...  852 us
    ppermute x22, waiting for transfers between devices, from_behind(): return lax.ppermute(block, axis, route)  189 us
    ppermute x22, starting transfers between devices, from_behind(): return lax.ppermute(block, axis, route)  135 us
    psum x1, waiting for transfers between devices, local(): lax.psum((acc_up.astype(jnp.bfloat16), acc_down.astype(jnp.bfloat16)), 'dp')  93.3 us
    dynamic_update_slice x33, local copies, waits for them, and re-layouts, local(): _, saved = lax.scan(forward_step, start_act, jnp.arange(step_count))  41.5 us
  transfers between devices with their start and end apart: 23, of which 23 were waited for; matrix products, arithmetic and copies ran while one was open for 3% of the time, Pallas kernels for 0%

profile of v2, /device:TPU:62, one launch (start us, length us, event | category | flops | bytes accessed | tf_op | source)
XLA Modules:
  0.0 1714.4 jit_solution(6520618879283231371)
XLA Ops:
  7.3 775.1 %while.39 = (s32[]{:T(128)}, bf16[32,2048]{1,0:T(8,128)(2,1)S(1)}, bf16[11,32,2048]{2,1,0:T(8,128)(2,1)}, f32[11,32,4]{1,2,0:T(4,128)S(1)}, bf16[11,32,4,2048]{3...) while((s32[]{:T(128)}, bf16[32,2048]{1,0:T(8,128)(2,1)S(1)}, ...), condition=%wide.region_9.10_spmd.clone, body=%wide.region_0.9_spmd.clone.sunk | while | flops 573637120 | bytes 31444144 | solution.py:156
  14.9 21.1 %eval_jaxpr.8 = bf16[8,1,17,2048]{3,2,1,0:T(8,128)(2,1)S(1)} custom-call(bf16[8,1,17,2048]{3,2,1,0:T(8,128)(2,1)} %bitcast.222), custom_call_target="tpu_custom_call" | custom-call | bytes 1114112 | tf_op jit(solution)/shard_map/while/body/eval_jaxpr/pallas_call | solution.py:55
  37.0 20.3 %eval_jaxpr.9 = bf16[8,1,17,2048]{3,2,1,0:T(8,128)(2,1)} custom-call(bf16[8,1,17,2048]{3,2,1,0:T(8,128)(2,1)S(1)} %bitcast.220), custom_call_target="tpu_custom_call" | custom-call | bytes 1114112 | tf_op jit(solution)/shard_map/while/body/eval_jaxpr/pallas_call | solution.py:55
  102.3 19.8 %eval_jaxpr.9 = bf16[8,1,17,2048]{3,2,1,0:T(8,128)(2,1)} custom-call(bf16[8,1,17,2048]{3,2,1,0:T(8,128)(2,1)S(1)} %bitcast.220), custom_call_target="tpu_custom_call" | custom-call | bytes 1114112 | tf_op jit(solution)/shard_map/while/body/eval_jaxpr/pallas_call | solution.py:55
  171.3 19.8 %eval_jaxpr.9 = bf16[8,1,17,2048]{3,2,1,0:T(8,128)(2,1)} custom-call(bf16[8,1,17,2048]{3,2,1,0:T(8,128)(2,1)S(1)} %bitcast.220), custom_call_target="tpu_custom_call" | custom-call | bytes 1114112 | tf_op jit(solution)/shard_map/while/body/eval_jaxpr/pallas_call | solution.py:55
  244.4 20.0 %eval_jaxpr.9 = bf16[8,1,17,2048]{3,2,1,0:T(8,128)(2,1)} custom-call(bf16[8,1,17,2048]{3,2,1,0:T(8,128)(2,1)S(1)} %bitcast.220), custom_call_target="tpu_custom_call" | custom-call | bytes 1114112 | tf_op jit(solution)/shard_map/while/body/eval_jaxpr/pallas_call | solution.py:55
  313.5 20.0 %eval_jaxpr.9 = bf16[8,1,17,2048]{3,2,1,0:T(8,128)(2,1)} custom-call(bf16[8,1,17,2048]{3,2,1,0:T(8,128)(2,1)S(1)} %bitcast.220), custom_call_target="tpu_custom_call" | custom-call | bytes 1114112 | tf_op jit(solution)/shard_map/while/body/eval_jaxpr/pallas_call | solution.py:55
  386.7 20.0 %eval_jaxpr.9 = bf16[8,1,17,2048]{3,2,1,0:T(8,128)(2,1)} custom-call(bf16[8,1,17,2048]{3,2,1,0:T(8,128)(2,1)S(1)} %bitcast.220), custom_call_target="tpu_custom_call" | custom-call | bytes 1114112 | tf_op jit(solution)/shard_map/while/body/eval_jaxpr/pallas_call | solution.py:55
  459.7 20.0 %eval_jaxpr.9 = bf16[8,1,17,2048]{3,2,1,0:T(8,128)(2,1)} custom-call(bf16[8,1,17,2048]{3,2,1,0:T(8,128)(2,1)S(1)} %bitcast.220), custom_call_target="tpu_custom_call" | custom-call | bytes 1114112 | tf_op jit(solution)/shard_map/while/body/eval_jaxpr/pallas_call | solution.py:55
  602.2 19.8 %eval_jaxpr.9 = bf16[8,1,17,2048]{3,2,1,0:T(8,128)(2,1)} custom-call(bf16[8,1,17,2048]{3,2,1,0:T(8,128)(2,1)S(1)} %bitcast.220), custom_call_target="tpu_custom_call" | custom-call | bytes 1114112 | tf_op jit(solution)/shard_map/while/body/eval_jaxpr/pallas_call | solution.py:55
  671.3 19.8 %eval_jaxpr.9 = bf16[8,1,17,2048]{3,2,1,0:T(8,128)(2,1)} custom-call(bf16[8,1,17,2048]{3,2,1,0:T(8,128)(2,1)S(1)} %bitcast.220), custom_call_target="tpu_custom_call" | custom-call | bytes 1114112 | tf_op jit(solution)/shard_map/while/body/eval_jaxpr/pallas_call | solution.py:55
  787.5 816.7 %while.40 = (s32[]{:T(128)}, bf16[32,2048]{1,0:T(8,128)(2,1)S(1)}, f32[1,2048,512]{2,1,0:T(8,128)}, f32[1,512,2048]{2,1,0:T(8,128)}, pred[]{:T(512)}, /*index=5*...) while((s32[]{:T(128)}, bf16[32,2048]{1,0:T(8,128)(2,1)S(1)}, ...), condition=%wide.region_23.24_spmd.clone.clone, body=%wide.region_10.23_spmd.clone.clone.sunk | while | flops 1154170240 | bytes 116775576 | solution.py:237
  814.0 20.0 %eval_jaxpr.11 = bf16[8,1,17,2048]{3,2,1,0:T(8,128)(2,1)} custom-call(bf16[8,1,17,2048]{3,2,1,0:T(8,128)(2,1)S(1)} %bitcast.221), custom_call_target="tpu_custom_call" | custom-call | bytes 1114112 | tf_op jit(solution)/shard_map/while/body/eval_jaxpr/pallas_call | solution.py:55
  884.9 20.0 %eval_jaxpr.11 = bf16[8,1,17,2048]{3,2,1,0:T(8,128)(2,1)} custom-call(bf16[8,1,17,2048]{3,2,1,0:T(8,128)(2,1)S(1)} %bitcast.221), custom_call_target="tpu_custom_call" | custom-call | bytes 1114112 | tf_op jit(solution)/shard_map/while/body/eval_jaxpr/pallas_call | solution.py:55
  955.3 20.0 %eval_jaxpr.11 = bf16[8,1,17,2048]{3,2,1,0:T(8,128)(2,1)} custom-call(bf16[8,1,17,2048]{3,2,1,0:T(8,128)(2,1)S(1)} %bitcast.221), custom_call_target="tpu_custom_call" | custom-call | bytes 1114112 | tf_op jit(solution)/shard_map/while/body/eval_jaxpr/pallas_call | solution.py:55
  1025.8 20.0 %eval_jaxpr.11 = bf16[8,1,17,2048]{3,2,1,0:T(8,128)(2,1)} custom-call(bf16[8,1,17,2048]{3,2,1,0:T(8,128)(2,1)S(1)} %bitcast.221), custom_call_target="tpu_custom_call" | custom-call | bytes 1114112 | tf_op jit(solution)/shard_map/while/body/eval_jaxpr/pallas_call | solution.py:55
  1107.6 19.8 %eval_jaxpr.11 = bf16[8,1,17,2048]{3,2,1,0:T(8,128)(2,1)} custom-call(bf16[8,1,17,2048]{3,2,1,0:T(8,128)(2,1)S(1)} %bitcast.221), custom_call_target="tpu_custom_call" | custom-call | bytes 1114112 | tf_op jit(solution)/shard_map/while/body/eval_jaxpr/pallas_call | solution.py:55
  1188.1 19.8 %eval_jaxpr.11 = bf16[8,1,17,2048]{3,2,1,0:T(8,128)(2,1)} custom-call(bf16[8,1,17,2048]{3,2,1,0:T(8,128)(2,1)S(1)} %bitcast.221), custom_call_target="tpu_custom_call" | custom-call | bytes 1114112 | tf_op jit(solution)/shard_map/while/body/eval_jaxpr/pallas_call | solution.py:55
  1268.6 19.8 %eval_jaxpr.11 = bf16[8,1,17,2048]{3,2,1,0:T(8,128)(2,1)} custom-call(bf16[8,1,17,2048]{3,2,1,0:T(8,128)(2,1)S(1)} %bitcast.221), custom_call_target="tpu_custom_call" | custom-call | bytes 1114112 | tf_op jit(solution)/shard_map/while/body/eval_jaxpr/pallas_call | solution.py:55
  1349.0 19.8 %eval_jaxpr.11 = bf16[8,1,17,2048]{3,2,1,0:T(8,128)(2,1)} custom-call(bf16[8,1,17,2048]{3,2,1,0:T(8,128)(2,1)S(1)} %bitcast.221), custom_call_target="tpu_custom_call" | custom-call | bytes 1114112 | tf_op jit(solution)/shard_map/while/body/eval_jaxpr/pallas_call | solution.py:55
  1419.2 20.0 %eval_jaxpr.11 = bf16[8,1,17,2048]{3,2,1,0:T(8,128)(2,1)} custom-call(bf16[8,1,17,2048]{3,2,1,0:T(8,128)(2,1)S(1)} %bitcast.221), custom_call_target="tpu_custom_call" | custom-call | bytes 1114112 | tf_op jit(solution)/shard_map/while/body/eval_jaxpr/pallas_call | solution.py:55
  1489.7 20.0 %eval_jaxpr.11 = bf16[8,1,17,2048]{3,2,1,0:T(8,128)(2,1)} custom-call(bf16[8,1,17,2048]{3,2,1,0:T(8,128)(2,1)S(1)} %bitcast.221), custom_call_target="tpu_custom_call" | custom-call | bytes 1114112 | tf_op jit(solution)/shard_map/while/body/eval_jaxpr/pallas_call | solution.py:55
  1560.1 20.0 %eval_jaxpr.11 = bf16[8,1,17,2048]{3,2,1,0:T(8,128)(2,1)} custom-call(bf16[8,1,17,2048]{3,2,1,0:T(8,128)(2,1)S(1)} %bitcast.221), custom_call_target="tpu_custom_call" | custom-call | bytes 1114112 | tf_op jit(solution)/shard_map/while/body/eval_jaxpr/pallas_call | solution.py:55
  1609.7 93.3 %all-reduce.3.cloned.1.call-done = (bf16[1,1,2048,512]{3,2,1,0:T(8,128)(2,1)}, bf16[1,1,512,2048]{3,2,1,0:T(8,128)(2,1)}) async-done(((bf16[1,1,2048,512]{3,2,1,0:T(8,128)(2,1)}, bf16[1,1,512,2048]{3,2,1,0:T(8,128)(2,1)}), (bf16[1,1,2048,512]{3,2,1,0:T(8,128)(2,1)}, bf16[1,1,512,2048]{3,2,1,0:T(8,128)(2,1)})) %all-reduce.3.cloned.1.call-update) | async-done | bytes 4194320 | tf_op jit(solution)/shard_map/psum | solution.py:240
  (1052 shorter events, 1234.6 us)
Async XLA Ops:
  7.2 1695.8 %all-reduce.3.cloned.1.call-start = ((), (), s32[]{:S(2)}) async-start(), calls=%async_computation | async-start | bytes 8388608 | tf_op jit(solution)/shard_map/psum | solution.py:240
  62.4 12.7 collective-permute-start
  127.3 16.8 collective-permute-start
  196.3 17.0 collective-permute-start
  269.5 13.0 collective-permute-start
  338.7 16.9 collective-permute-start
  411.8 16.9 collective-permute-start
  484.8 17.1 collective-permute-start
  554.0 21.0 %collective-permute-start = (bf16[32,2048]{1,0:T(8,128)(2,1)S(1)}, bf16[32,2048]{1,0:T(8,128)(2,1)S(1)}, u32[]{:S(2)}, u32[]{:S(2)}) collective-permute-start(bf16[32,2048]{1,0:T(8,128)(2,1)S(1)} %fusion.144), channel_id=1, source_target_pairs={{0,32},{32,64},{64,96},{96,128},{128,160},{160,192},{192,224},{1,3... | collective-permute-start | bytes 393224 | tf_op jit(solution)/shard_map/while/body/eval_jaxpr/ppermute | solution.py:21
  627.2 16.9 collective-permute-start
  696.3 16.9 collective-permute-start
  765.4 17.0 collective-permute-start
  782.4 5.1 copy-start.8
  841.2 17.4 %collective-permute-start.1 = (bf16[32,2048]{1,0:T(8,128)(2,1)S(1)}, bf16[32,2048]{1,0:T(8,128)(2,1)S(1)}, u32[]{:S(2)}, u32[]{:S(2)}) collective-permute-start(bf16[32,2048]{1,0:T(8,128)(2,1)S(1)} %fusion.157), channel_id=1, source_target_pairs={{32,0},{64,32},{96,64},{128,96},{160,128},{192,160},{224,192},{33,... | collective-permute-start | bytes 393224 | tf_op jit(solution)/shard_map/while/body/eval_jaxpr/ppermute | solution.py:21
  912.1 17.0 collective-permute-start.1
  982.5 17.0 collective-permute-start.1
  1053.0 18.2 %collective-permute-start.1 = (bf16[32,2048]{1,0:T(8,128)(2,1)S(1)}, bf16[32,2048]{1,0:T(8,128)(2,1)S(1)}, u32[]{:S(2)}, u32[]{:S(2)}) collective-permute-start(bf16[32,2048]{1,0:T(8,128)(2,1)S(1)} %fusion.157), channel_id=1, source_target_pairs={{32,0},{64,32},{96,64},{128,96},{160,128},{192,160},{224,192},{33,... | collective-permute-start | bytes 393224 | tf_op jit(solution)/shard_map/while/body/eval_jaxpr/ppermute | solution.py:21
  1134.7 17.0 collective-permute-start.1
  1215.2 16.9 collective-permute-start.1
  1295.6 16.9 collective-permute-start.1
  1376.1 16.9 collective-permute-start.1
  1446.5 17.0 collective-permute-start.1
  1516.9 16.9 collective-permute-start.1
  1587.3 16.9 collective-permute-start.1
  (37 other events, 102.0 us)
Sparse Core Ops, SparseCore 0:
  1609.8 93.1 all-reduce.2

commit v3 on v2

--- a/solution.py
+++ b/solution.py
@@ -96,18 +96,27 @@
         slots = jnp.sum(ranks * onehot, axis=1)
         return flat_ids * capacity + slots
 
+    lanes = 128
+    pieces = features // lanes
+
     def to_buffer(row_values, dest_rows):
         filled = (
-            jnp.zeros((experts_all * capacity, features), row_values.dtype)
+            jnp.zeros((experts_all * capacity, pieces, lanes), row_values.dtype)
             .at[dest_rows]
-            .set(row_values)
-        )
-        return filled.reshape(expert_devs, local_experts, capacity, features)
+            .set(row_values.reshape(-1, pieces, lanes))
+        )
+        return filled.reshape(expert_devs, local_experts * capacity * pieces, lanes)
 
     def from_buffer(buffer, dest_rows):
-        return buffer.reshape(experts_all * capacity, features)[dest_rows].reshape(
+        return buffer.reshape(experts_all * capacity, pieces, lanes)[dest_rows].reshape(
             tok_rows, top_count, features
         )
+
+    def as_rows(buffer):
+        return buffer.reshape(expert_devs, local_experts, capacity, features)
+
+    def as_pieces(buffer):
+        return buffer.reshape(expert_devs, local_experts * capacity * pieces, lanes)
 
     def repeated(normed):
         return jnp.broadcast_to(normed[:, None, :], (tok_rows, top_count, features)).reshape(
@@ -141,9 +150,9 @@
         gatev = gate_values(normed, route_rows)
         wgt = gatev / jnp.sum(gatev, axis=-1, keepdims=True)
         dest_rows = slot_rows(route_rows)
-        received = expert_exchange(to_buffer(repeated(normed), dest_rows), 3)
+        received = as_rows(expert_exchange(to_buffer(repeated(normed), dest_rows), 3))
         preact, outbuf = lax.cond(live_step, expert_forward, expert_skip, received)
-        returned = expert_exchange(outbuf, 0)
+        returned = expert_exchange(as_pieces(outbuf), 0)
         expout = from_buffer(returned, dest_rows)
         section_out = (
             as_f32 + jnp.sum(wgt[..., None] * expout.astype(jnp.float32), axis=1)
@@ -199,7 +208,7 @@
             .reshape(tok_rows * top_count, features)
         )
         dsend = to_buffer(dout, dest_rows)
-        dreceived = expert_exchange(dsend, 1)
+        dreceived = as_rows(expert_exchange(dsend, 1))
         received = lax.dynamic_index_in_dim(saved[3], fwd_index, 0, keepdims=False)
         preact = lax.dynamic_index_in_dim(saved[4], fwd_index, 0, keepdims=False)
 
@@ -213,7 +222,7 @@
             backward_skip,
             (received, dreceived, preact, acc_up, acc_down),
         )
-        dreturned = expert_exchange(dinbuf, 2)
+        dreturned = expert_exchange(as_pieces(dinbuf), 2)
         dexp = jnp.sum(from_buffer(dreturned, dest_rows).astype(jnp.float32), axis=1)
         dgate = (dwgt - jnp.sum(wgt * dwgt, axis=-1, keepdims=True)) / total
         dlogit = dgate * gatev * (1.0 - gatev)

time: 1720 us -> 1720 us (level)
  Pallas kernels: 852 us -> 647 us
  local copies, waits for them, and re-layouts: 222 us -> 399 us
  other arithmetic: 123 us -> 146 us
    pallas_call x44, Pallas kernels: 852 us -> 647 us  [expert_exchange(): pl.pallas_call(functools.partial(exchange_kernel, n), out_shape=jax.Shape...]
    scatter x11 -> x22, local copies, waits for them, and re-layouts: 16.6 us -> 144 us  [to_buffer(): filled = jnp.zeros((experts_all * capacity, pieces, lanes), row_values.dt...]
    reshape x55 -> x33, local copies, waits for them, and re-layouts: 54.7 us -> 27.8 us  [the longest x22 24.1 us: as_pieces(): return buffer.reshape(expert_devs, local_experts * capacity * pieces, lanes)]
    while x22 -> x154, local copies, waits for them, and re-layouts: 0.07 us -> 23.4 us
    gather x22, local copies, waits for them, and re-layouts: 20.6 us -> 38.7 us  [from_buffer(): buffer.reshape(experts_all * capacity, pieces, lanes)[dest_rows]]
    scatter x11 -> x0, other arithmetic: 17.3 us -> none  [to_buffer(): filled = jnp.zeros((experts_all * capacity, features), row_values.dtype)....]
where the time goes in v3:
time: 1720 us; the launch traced here: 1710 us
  Pallas kernels  647 us (38%)
  local copies, waits for them, and re-layouts  399 us (23%)
  waiting for transfers between devices  278 us (16%)
  other arithmetic  146 us (8%)
  starting transfers between devices  137 us (8%)
  matrix products  66.4 us (4%)
  loops' own time  20.7 us (1%)
    pallas_call x44, Pallas kernels, expert_exchange(): pl.pallas_call(functools.partial(exchange_kernel, n), out_shape=jax.Shape...  647 us
    ppermute x22, waiting for transfers between devices, from_behind(): return lax.ppermute(block, axis, route)  183 us
    scatter x22, local copies, waits for them, and re-layouts, to_buffer(): filled = jnp.zeros((experts_all * capacity, pieces, lanes), row_values.dt...  144 us
    ppermute x22, starting transfers between devices, from_behind(): return lax.ppermute(block, axis, route)  137 us
    psum x1, waiting for transfers between devices, local(): lax.psum((acc_up.astype(jnp.bfloat16), acc_down.astype(jnp.bfloat16)), 'dp')  95.1 us
    dynamic_update_slice x33, local copies, waits for them, and re-layouts, local(): _, saved = lax.scan(forward_step, start_act, jnp.arange(step_count))  41.5 us
    gather x22, local copies, waits for them, and re-layouts, from_buffer(): buffer.reshape(experts_all * capacity, pieces, lanes)[dest_rows]  38.7 us
  transfers between devices with their start and end apart: 23, of which 23 were waited for; matrix products, arithmetic and copies ran while one was open for 3% of the time, Pallas kernels for 0%

profile of v3, /device:TPU:62, one launch (start us, length us, event | category | flops | bytes accessed | tf_op | source)
XLA Modules:
  0.0 1708.7 jit_solution(6686647475020292882)
XLA Ops:
  7.9 716.6 %while.39 = (s32[]{:T(128)}, bf16[32,2048]{1,0:T(8,128)(2,1)}, bf16[11,32,2048]{2,1,0:T(8,128)(2,1)}, f32[11,32,4]{1,2,0:T(4,128)}, bf16[11,32,4,2048]{3,2,1,0:T...) while((s32[]{:T(128)}, bf16[32,2048]{1,0:T(8,128)(2,1)}, ...), condition=%wide.region_9.10_spmd.clone, body=%wide.region_0.9_spmd.clone.sunk | while | flops 573637120 | bytes 44745448 | solution.py:165
  18.6 16.2 eval_jaxpr.8
  36.8 15.7 eval_jaxpr.9
  96.7 15.2 eval_jaxpr.9
  160.3 14.9 eval_jaxpr.9
  228.4 14.9 eval_jaxpr.9
  292.1 15.0 eval_jaxpr.9
  428.4 14.9 eval_jaxpr.9
  511.7 15.2 collective-permute-start
  560.4 15.0 eval_jaxpr.9
  624.1 15.0 eval_jaxpr.9
  730.2 866.4 %while.40 = (s32[]{:T(128)}, bf16[32,2048]{1,0:T(8,128)(2,1)S(1)}, f32[1,2048,512]{2,1,0:T(8,128)}, f32[1,512,2048]{2,1,0:T(8,128)}, pred[]{:T(512)}, /*index=5*...) while((s32[]{:T(128)}, bf16[32,2048]{1,0:T(8,128)(2,1)S(1)}, ...), condition=%wide.region_23.24_spmd.clone.clone, body=%wide.region_10.23_spmd.clone.clone.sunk | while | flops 1154170240 | bytes 123462904 | solution.py:246
  766.0 15.0 eval_jaxpr.11
  789.6 15.5 collective-permute-done.1
  864.2 15.2 collective-permute-done.1
  938.5 15.2 collective-permute-done.1
  1012.9 18.0 %collective-permute-done.1 = bf16[32,2048]{1,0:T(8,128)(2,1)S(1)} collective-permute-done((bf16[32,2048]{1,0:T(8,128)(2,1)S(1)}, bf16[32,2048]{1,0:T(8,128)(2,1)S(1)}, u32[]{:S(2)}, u32[]{:S(2)}) %collective-permute-start.1) | collective-permute-done | bytes 131104 | tf_op jit(solution)/shard_map/while/body/eval_jaxpr/ppermute | solution.py:21
  1101.6 15.0 collective-permute-done.1
  1187.3 15.1 collective-permute-done.1
  1273.1 15.2 collective-permute-done.1
  1359.0 15.2 collective-permute-done.1
  1507.5 15.0 collective-permute-done.1
  1581.6 15.0 collective-permute-done.1
  1602.2 95.1 %all-reduce.3.cloned.1.call-done = (bf16[1,1,2048,512]{3,2,1,0:T(8,128)(2,1)}, bf16[1,1,512,2048]{3,2,1,0:T(8,128)(2,1)}) async-done(((bf16[1,1,2048,512]{3,2,1,0:T(8,128)(2,1)}, bf16[1,1,512,2048]{3,2,1,0:T(8,128)(2,1)}), (bf16[1,1,2048,512]{3,2,1,0:T(8,128)(2,1)}, bf16[1,1,512,2048]{3,2,1,0:T(8,128)(2,1)})) %all-reduce.3.cloned.1.call-update) | async-done | bytes 4194320 | tf_op jit(solution)/shard_map/psum | solution.py:249
  (1212 shorter events, 1333.0 us)
Async XLA Ops:
  7.2 1690.2 %all-reduce.3.cloned.1.call-start = ((), (), s32[]{:S(2)}) async-start(), calls=%async_computation | async-start | bytes 8388608 | tf_op jit(solution)/shard_map/psum | solution.py:249
  57.1 12.7 collective-permute-start
  116.5 16.8 collective-permute-start
  179.8 17.0 collective-permute-start
  247.9 12.6 collective-permute-start
  311.7 17.1 %collective-permute-start = (bf16[32,2048]{1,0:T(8,128)(2,1)S(1)}, bf16[32,2048]{1,0:T(8,128)(2,1)}, u32[]{:S(2)}, u32[]{:S(2)}) collective-permute-start(bf16[32,2048]{1,0:T(8,128)(2,1)S(1)} %fusion.132), channel_id=1, source_target_pairs={{0,32},{32,64},{64,96},{96,128},{128,160},{160,192},{192,224},{1,3... | collective-permute-start | bytes 393224 | tf_op jit(solution)/shard_map/while/body/eval_jaxpr/ppermute | solution.py:21
  379.8 17.1 collective-permute-start
  447.9 17.2 %collective-permute-start = (bf16[32,2048]{1,0:T(8,128)(2,1)S(1)}, bf16[32,2048]{1,0:T(8,128)(2,1)}, u32[]{:S(2)}, u32[]{:S(2)}) collective-permute-start(bf16[32,2048]{1,0:T(8,128)(2,1)S(1)} %fusion.132), channel_id=1, source_target_pairs={{0,32},{32,64},{64,96},{96,128},{128,160},{160,192},{192,224},{1,3... | collective-permute-start | bytes 393224 | tf_op jit(solution)/shard_map/while/body/eval_jaxpr/ppermute | solution.py:21
  511.7 21.7 %collective-permute-start = (bf16[32,2048]{1,0:T(8,128)(2,1)S(1)}, bf16[32,2048]{1,0:T(8,128)(2,1)}, u32[]{:S(2)}, u32[]{:S(2)}) collective-permute-start(bf16[32,2048]{1,0:T(8,128)(2,1)S(1)} %fusion.132), channel_id=1, source_target_pairs={{0,32},{32,64},{64,96},{96,128},{128,160},{160,192},{192,224},{1,3... | collective-permute-start | bytes 393224 | tf_op jit(solution)/shard_map/while/body/eval_jaxpr/ppermute | solution.py:21
  580.0 17.1 %collective-permute-start = (bf16[32,2048]{1,0:T(8,128)(2,1)S(1)}, bf16[32,2048]{1,0:T(8,128)(2,1)}, u32[]{:S(2)}, u32[]{:S(2)}) collective-permute-start(bf16[32,2048]{1,0:T(8,128)(2,1)S(1)} %fusion.132), channel_id=1, source_target_pairs={{0,32},{32,64},{64,96},{96,128},{128,160},{160,192},{192,224},{1,3... | collective-permute-start | bytes 393224 | tf_op jit(solution)/shard_map/while/body/eval_jaxpr/ppermute | solution.py:21
  643.6 17.2 %collective-permute-start = (bf16[32,2048]{1,0:T(8,128)(2,1)S(1)}, bf16[32,2048]{1,0:T(8,128)(2,1)}, u32[]{:S(2)}, u32[]{:S(2)}) collective-permute-start(bf16[32,2048]{1,0:T(8,128)(2,1)S(1)} %fusion.132), channel_id=1, source_target_pairs={{0,32},{32,64},{64,96},{96,128},{128,160},{160,192},{192,224},{1,3... | collective-permute-start | bytes 393224 | tf_op jit(solution)/shard_map/while/body/eval_jaxpr/ppermute | solution.py:21
  707.3 17.2 %collective-permute-start = (bf16[32,2048]{1,0:T(8,128)(2,1)S(1)}, bf16[32,2048]{1,0:T(8,128)(2,1)}, u32[]{:S(2)}, u32[]{:S(2)}) collective-permute-start(bf16[32,2048]{1,0:T(8,128)(2,1)S(1)} %fusion.132), channel_id=1, source_target_pairs={{0,32},{32,64},{64,96},{96,128},{128,160},{160,192},{192,224},{1,3... | collective-permute-start | bytes 393224 | tf_op jit(solution)/shard_map/while/body/eval_jaxpr/ppermute | solution.py:21
  736.2 28.6 %copy-start.3 = (bf16[1,2048,512]{2,1,0:T(8,128)(2,1)S(1)}, bf16[1,2048,512]{2,1,0:T(8,128)(2,1)}, u32[]{:S(2)}) copy-start(bf16[1,2048,512]{2,1,0:T(8,128)(2,1)} %get-tuple-element.1119) | copy-start | bytes 6291460 | tf_op jit(solution)/shard_map/while
  787.7 17.4 %collective-permute-start.1 = (bf16[32,2048]{1,0:T(8,128)(2,1)S(1)}, bf16[32,2048]{1,0:T(8,128)(2,1)S(1)}, u32[]{:S(2)}, u32[]{:S(2)}) collective-permute-start(bf16[32,2048]{1,0:T(8,128)(2,1)S(1)} %fusion.144), channel_id=1, source_target_pairs={{32,0},{64,32},{96,64},{128,96},{160,128},{192,160},{224,192},{33,... | collective-permute-start | bytes 393224 | tf_op jit(solution)/shard_map/while/body/eval_jaxpr/ppermute | solution.py:21
  862.3 17.1 %collective-permute-start.1 = (bf16[32,2048]{1,0:T(8,128)(2,1)S(1)}, bf16[32,2048]{1,0:T(8,128)(2,1)S(1)}, u32[]{:S(2)}, u32[]{:S(2)}) collective-permute-start(bf16[32,2048]{1,0:T(8,128)(2,1)S(1)} %fusion.144), channel_id=1, source_target_pairs={{32,0},{64,32},{96,64},{128,96},{160,128},{192,160},{224,192},{33,... | collective-permute-start | bytes 393224 | tf_op jit(solution)/shard_map/while/body/eval_jaxpr/ppermute | solution.py:21
  936.6 17.2 %collective-permute-start.1 = (bf16[32,2048]{1,0:T(8,128)(2,1)S(1)}, bf16[32,2048]{1,0:T(8,128)(2,1)S(1)}, u32[]{:S(2)}, u32[]{:S(2)}) collective-permute-start(bf16[32,2048]{1,0:T(8,128)(2,1)S(1)} %fusion.144), channel_id=1, source_target_pairs={{32,0},{64,32},{96,64},{128,96},{160,128},{192,160},{224,192},{33,... | collective-permute-start | bytes 393224 | tf_op jit(solution)/shard_map/while/body/eval_jaxpr/ppermute | solution.py:21
  1011.0 19.9 %collective-permute-start.1 = (bf16[32,2048]{1,0:T(8,128)(2,1)S(1)}, bf16[32,2048]{1,0:T(8,128)(2,1)S(1)}, u32[]{:S(2)}, u32[]{:S(2)}) collective-permute-start(bf16[32,2048]{1,0:T(8,128)(2,1)S(1)} %fusion.144), channel_id=1, source_target_pairs={{32,0},{64,32},{96,64},{128,96},{160,128},{192,160},{224,192},{33,... | collective-permute-start | bytes 393224 | tf_op jit(solution)/shard_map/while/body/eval_jaxpr/ppermute | solution.py:21
  1099.7 17.0 collective-permute-start.1
  1185.4 17.1 collective-permute-start.1
  1271.2 17.2 %collective-permute-start.1 = (bf16[32,2048]{1,0:T(8,128)(2,1)S(1)}, bf16[32,2048]{1,0:T(8,128)(2,1)S(1)}, u32[]{:S(2)}, u32[]{:S(2)}) collective-permute-start(bf16[32,2048]{1,0:T(8,128)(2,1)S(1)} %fusion.144), channel_id=1, source_target_pairs={{32,0},{64,32},{96,64},{128,96},{160,128},{192,160},{224,192},{33,... | collective-permute-start | bytes 393224 | tf_op jit(solution)/shard_map/while/body/eval_jaxpr/ppermute | solution.py:21
  1357.1 17.2 %collective-permute-start.1 = (bf16[32,2048]{1,0:T(8,128)(2,1)S(1)}, bf16[32,2048]{1,0:T(8,128)(2,1)S(1)}, u32[]{:S(2)}, u32[]{:S(2)}) collective-permute-start(bf16[32,2048]{1,0:T(8,128)(2,1)S(1)} %fusion.144), channel_id=1, source_target_pairs={{32,0},{64,32},{96,64},{128,96},{160,128},{192,160},{224,192},{33,... | collective-permute-start | bytes 393224 | tf_op jit(solution)/shard_map/while/body/eval_jaxpr/ppermute | solution.py:21
  1431.4 17.0 collective-permute-start.1
  1505.5 17.0 collective-permute-start.1
  1579.7 17.0 collective-permute-start.1
  (102 other events, 1085.0 us)
Sparse Core Ops, SparseCore 0:
  1602.3 94.9 all-reduce.2

commit v4 on v3

--- a/solution.py
+++ b/solution.py
@@ -99,12 +99,17 @@
     lanes = 128
     pieces = features // lanes
 
-    def to_buffer(row_values, dest_rows):
-        filled = (
-            jnp.zeros((experts_all * capacity, pieces, lanes), row_values.dtype)
-            .at[dest_rows]
-            .set(row_values.reshape(-1, pieces, lanes))
-        )
+    def slot_sources(dest_rows):
+        pair_ids = jnp.arange(dest_rows.shape[0], dtype=jnp.int32)
+        return jnp.full((experts_all * capacity,), -1, jnp.int32).at[dest_rows].set(pair_ids)
+
+    dest_all = jax.vmap(slot_rows)(route_all)
+    source_all = jax.vmap(slot_sources)(dest_all)
+
+    def to_buffer(row_values, sources, per_row):
+        pieces_of = row_values.reshape(-1, pieces, lanes)
+        picked = pieces_of[jnp.maximum(sources, 0) // per_row]
+        filled = jnp.where((sources >= 0)[:, None, None], picked, jnp.zeros_like(picked))
         return filled.reshape(expert_devs, local_experts * capacity * pieces, lanes)
 
     def from_buffer(buffer, dest_rows):
@@ -117,11 +122,6 @@
 
     def as_pieces(buffer):
         return buffer.reshape(expert_devs, local_experts * capacity * pieces, lanes)
-
-    def repeated(normed):
-        return jnp.broadcast_to(normed[:, None, :], (tok_rows, top_count, features)).reshape(
-            tok_rows * top_count, features
-        )
 
     def gate_values(normed, route_rows):
         logits = jnp.dot(normed, gate_cols, preferred_element_type=jnp.float32)
@@ -149,8 +149,9 @@
         as_f32, rscale, normed = normalize(section_in)
         gatev = gate_values(normed, route_rows)
         wgt = gatev / jnp.sum(gatev, axis=-1, keepdims=True)
-        dest_rows = slot_rows(route_rows)
-        received = as_rows(expert_exchange(to_buffer(repeated(normed), dest_rows), 3))
+        dest_rows = lax.dynamic_index_in_dim(dest_all, micro, 0, keepdims=False)
+        sources = lax.dynamic_index_in_dim(source_all, micro, 0, keepdims=False)
+        received = as_rows(expert_exchange(to_buffer(normed, sources, top_count), 3))
         preact, outbuf = lax.cond(live_step, expert_forward, expert_skip, received)
         returned = expert_exchange(as_pieces(outbuf), 0)
         expout = from_buffer(returned, dest_rows)
@@ -196,7 +197,8 @@
         last_in = lax.dynamic_index_in_dim(cotangent, micro, 0, keepdims=False)
         grad_out = jnp.where(section_pos == section_count - 1, last_in, incoming)
         route_rows = lax.dynamic_index_in_dim(route_all, micro, 0, keepdims=False)
-        dest_rows = slot_rows(route_rows)
+        dest_rows = lax.dynamic_index_in_dim(dest_all, micro, 0, keepdims=False)
+        sources = lax.dynamic_index_in_dim(source_all, micro, 0, keepdims=False)
         as_f32, rscale, normed = normalize(section_in)
         total = jnp.sum(gatev, axis=-1, keepdims=True)
         wgt = gatev / total
@@ -207,7 +209,7 @@
             .astype(jnp.bfloat16)
             .reshape(tok_rows * top_count, features)
         )
-        dsend = to_buffer(dout, dest_rows)
+        dsend = to_buffer(dout, sources, 1)
         dreceived = as_rows(expert_exchange(dsend, 1))
         received = lax.dynamic_index_in_dim(saved[3], fwd_index, 0, keepdims=False)
         preact = lax.dynamic_index_in_dim(saved[4], fwd_index, 0, keepdims=False)

time: 1720 us -> 1550 us (0.901)
  local copies, waits for them, and re-layouts: 399 us -> 236 us
  other arithmetic: 146 us -> 112 us
    scatter x22 -> x1, local copies, waits for them, and re-layouts: 144 us -> 24.7 us  [slot_sources(): jnp.full((experts_all * capacity,), -1, jnp.int32).at[dest_rows]]
    select_n x22 -> x55, other arithmetic: 0.14 us -> 27.3 us  [the longest x22 26.9 us: to_buffer(): jnp.where((sources >= 0)[:, None, None], picked, jnp.zeros_like(picked))]
    while x154 -> x11, local copies, waits for them, and re-layouts: 23.4 us -> 0.23 us
where the time goes in v4:
time: 1550 us
  Pallas kernels  646 us (42%)
  waiting for transfers between devices  295 us (19%)
  local copies, waits for them, and re-layouts  236 us (15%)
  starting transfers between devices  140 us (9%)
  other arithmetic  112 us (7%)
  matrix products  81.7 us (5%)
  loops' own time  19.7 us (1%)
    pallas_call x44, Pallas kernels, expert_exchange(): pl.pallas_call(functools.partial(exchange_kernel, n), out_shape=jax.Shape...  646 us
    ppermute x22, waiting for transfers between devices, from_behind(): return lax.ppermute(block, axis, route)  195 us
    ppermute x22, starting transfers between devices, from_behind(): return lax.ppermute(block, axis, route)  140 us
    psum x1, waiting for transfers between devices, local(): lax.psum((acc_up.astype(jnp.bfloat16), acc_down.astype(jnp.bfloat16)), 'dp')  100 us
    dynamic_update_slice x33, local copies, waits for them, and re-layouts, local(): _, saved = lax.scan(forward_step, start_act, jnp.arange(step_count))  41.6 us
    gather x22, local copies, waits for them, and re-layouts, from_buffer(): buffer.reshape(experts_all * capacity, pieces, lanes)[dest_rows]  38.7 us
  transfers between devices with their start and end apart: 23, of which 23 were waited for; matrix products, arithmetic and copies ran while one was open for 3% of the time, Pallas kernels for 0%

profile of v4, /device:TPU:62, one launch (start us, length us, event | category | flops | bytes accessed | tf_op | source)
XLA Modules:
  0.0 1545.3 jit_solution(5870525855019564651)
XLA Ops:
  9.8 24.7 %scatter_fusion = s32[4,136]{1,0:T(4,128)S(1)} fusion(s32[4,136]{1,0:T(4,128)S(1)} %broadcast_in_dim.123, s32[512]{0:T(512)S(1)} %fusion.91, s32[512]{0:T(512)S(1)} %iota_bitcast_fusion), kind=kCustom, calls=%fused_computation.5 | custom fusion | bytes 10240 | tf_op jit(solution)/shard_map/vmap()/scatter | solution.py:104
  34.6 660.3 %while.39 = (s32[]{:T(128)}, bf16[32,2048]{1,0:T(8,128)(2,1)S(1)}, bf16[11,32,2048]{2,1,0:T(8,128)(2,1)}, f32[11,32,4]{1,2,0:T(4,128)S(1)}, bf16[11,32,4,2048]{3...) while((s32[]{:T(128)}, bf16[32,2048]{1,0:T(8,128)(2,1)S(1)}, ...), condition=%wide.region_9.10_spmd, body=%wide.region_3.9_spmd.sunk | while | flops 573976576 | bytes 24260048 | solution.py:166
  40.0 16.2 %eval_jaxpr.16 = bf16[8,272,128]{2,1,0:T(8,128)(2,1)S(1)} custom-call(bf16[8,272,128]{2,1,0:T(8,128)(2,1)} %bitcast_select_fusion.8.x_ref), custom_call_target="tpu_custom_call" | custom-call | bytes 1114112 | tf_op jit(solution)/shard_map/while/body/eval_jaxpr/pallas_call | solution.py:55
  58.3 15.7 %eval_jaxpr.17 = bf16[8,272,128]{2,1,0:T(8,128)(2,1)} custom-call(bf16[8,272,128]{2,1,0:T(8,128)(2,1)} %reshape.720.x_ref), custom_call_target="tpu_custom_call" | custom-call | bytes 1114112 | tf_op jit(solution)/shard_map/while/body/eval_jaxpr/pallas_call | solution.py:55
  113.1 14.9 eval_jaxpr.17
  171.5 14.9 eval_jaxpr.17
  234.7 14.9 eval_jaxpr.17
  356.4 14.9 eval_jaxpr.17
  419.6 14.9 eval_jaxpr.17
  478.2 14.9 eval_jaxpr.17
  497.8 15.1 collective-permute-start
  541.2 14.9 eval_jaxpr.17
  699.9 728.4 %while.40 = (s32[]{:T(128)}, bf16[32,2048]{1,0:T(8,128)(2,1)S(1)}, f32[1,2048,512]{2,1,0:T(8,128)}, f32[1,512,2048]{2,1,0:T(8,128)}, pred[]{:T(512)}, /*index=5*...) while((s32[]{:T(128)}, bf16[32,2048]{1,0:T(8,128)(2,1)S(1)}, ...), condition=%wide.region_20.21_spmd.clone, body=%wide.region_10.20_spmd.clone.sunk | while | flops 1154312832 | bytes 110575424 | solution.py:248
  745.2 15.6 %collective-permute-done.1 = bf16[32,2048]{1,0:T(8,128)(2,1)S(1)} collective-permute-done((bf16[32,2048]{1,0:T(8,128)(2,1)S(1)}, bf16[32,2048]{1,0:T(8,128)(2,1)S(1)}, u32[]{:S(2)}, u32[]{:S(2)}) %collective-permute-start.1) | collective-permute-done | bytes 131104 | tf_op jit(solution)/shard_map/while/body/eval_jaxpr/ppermute | solution.py:21
  805.9 15.0 collective-permute-done.1
  866.1 15.0 collective-permute-done.1
  926.2 27.8 %collective-permute-done.1 = bf16[32,2048]{1,0:T(8,128)(2,1)S(1)} collective-permute-done((bf16[32,2048]{1,0:T(8,128)(2,1)S(1)}, bf16[32,2048]{1,0:T(8,128)(2,1)S(1)}, u32[]{:S(2)}, u32[]{:S(2)}) %collective-permute-start.1) | collective-permute-done | bytes 131104 | tf_op jit(solution)/shard_map/while/body/eval_jaxpr/ppermute | solution.py:21
  988.8 14.9 eval_jaxpr.19
  1012.4 15.0 collective-permute-done.1
  1085.8 15.0 collective-permute-done.1
  1159.2 15.0 collective-permute-done.1
  1232.7 15.0 collective-permute-done.1
  1353.2 15.0 collective-permute-done.1
  1433.9 100.0 %all-reduce.3.cloned.1.call-done = (bf16[1,1,2048,512]{3,2,1,0:T(8,128)(2,1)}, bf16[1,1,512,2048]{3,2,1,0:T(8,128)(2,1)}) async-done(((bf16[1,1,2048,512]{3,2,1,0:T(8,128)(2,1)}, bf16[1,1,512,2048]{3,2,1,0:T(8,128)(2,1)}), (bf16[1,1,2048,512]{3,2,1,0:T(8,128)(2,1)}, bf16[1,1,512,2048]{3,2,1,0:T(8,128)(2,1)})) %all-reduce.3.cloned.1.call-update) | async-done | bytes 4194320 | tf_op jit(solution)/shard_map/psum | solution.py:251
  (1015 shorter events, 1155.0 us)
Async XLA Ops:
  7.2 27.4 %copy-start.7 = (s32[1,4,32,4]{2,3,1,0:T(4,128)S(1)}, s32[1,4,32,4]{2,3,1,0:T(4,128)}, u32[]{:S(2)}) copy-start(s32[1,4,32,4]{2,3,1,0:T(4,128)} %param.19) | copy-start | bytes 6148
  7.2 1526.8 %all-reduce.3.cloned.1.call-start = ((), (), s32[]{:S(2)}) async-start(), calls=%async_computation | async-start | bytes 8388608 | tf_op jit(solution)/shard_map/psum | solution.py:251
  78.6 12.6 collective-permute-start
  132.7 17.0 %collective-permute-start = (bf16[32,2048]{1,0:T(8,128)(2,1)S(1)}, bf16[32,2048]{1,0:T(8,128)(2,1)S(1)}, u32[]{:S(2)}, u32[]{:S(2)}) collective-permute-start(bf16[32,2048]{1,0:T(8,128)(2,1)S(1)} %fusion.127), channel_id=1, source_target_pairs={{0,32},{32,64},{64,96},{96,128},{128,160},{160,192},{192,224},{1,3... | collective-permute-start | bytes 393224 | tf_op jit(solution)/shard_map/while/body/eval_jaxpr/ppermute | solution.py:21
  191.1 17.1 %collective-permute-start = (bf16[32,2048]{1,0:T(8,128)(2,1)S(1)}, bf16[32,2048]{1,0:T(8,128)(2,1)S(1)}, u32[]{:S(2)}, u32[]{:S(2)}) collective-permute-start(bf16[32,2048]{1,0:T(8,128)(2,1)S(1)} %fusion.127), channel_id=1, source_target_pairs={{0,32},{32,64},{64,96},{96,128},{128,160},{160,192},{192,224},{1,3... | collective-permute-start | bytes 393224 | tf_op jit(solution)/shard_map/while/body/eval_jaxpr/ppermute | solution.py:21
  254.3 12.4 collective-permute-start
  312.8 17.1 %collective-permute-start = (bf16[32,2048]{1,0:T(8,128)(2,1)S(1)}, bf16[32,2048]{1,0:T(8,128)(2,1)S(1)}, u32[]{:S(2)}, u32[]{:S(2)}) collective-permute-start(bf16[32,2048]{1,0:T(8,128)(2,1)S(1)} %fusion.127), channel_id=1, source_target_pairs={{0,32},{32,64},{64,96},{96,128},{128,160},{160,192},{192,224},{1,3... | collective-permute-start | bytes 393224 | tf_op jit(solution)/shard_map/while/body/eval_jaxpr/ppermute | solution.py:21
  376.0 17.2 %collective-permute-start = (bf16[32,2048]{1,0:T(8,128)(2,1)S(1)}, bf16[32,2048]{1,0:T(8,128)(2,1)S(1)}, u32[]{:S(2)}, u32[]{:S(2)}) collective-permute-start(bf16[32,2048]{1,0:T(8,128)(2,1)S(1)} %fusion.127), channel_id=1, source_target_pairs={{0,32},{32,64},{64,96},{96,128},{128,160},{160,192},{192,224},{1,3... | collective-permute-start | bytes 393224 | tf_op jit(solution)/shard_map/while/body/eval_jaxpr/ppermute | solution.py:21
  439.2 17.1 %collective-permute-start = (bf16[32,2048]{1,0:T(8,128)(2,1)S(1)}, bf16[32,2048]{1,0:T(8,128)(2,1)S(1)}, u32[]{:S(2)}, u32[]{:S(2)}) collective-permute-start(bf16[32,2048]{1,0:T(8,128)(2,1)S(1)} %fusion.127), channel_id=1, source_target_pairs={{0,32},{32,64},{64,96},{96,128},{128,160},{160,192},{192,224},{1,3... | collective-permute-start | bytes 393224 | tf_op jit(solution)/shard_map/while/body/eval_jaxpr/ppermute | solution.py:21
  497.8 21.7 %collective-permute-start = (bf16[32,2048]{1,0:T(8,128)(2,1)S(1)}, bf16[32,2048]{1,0:T(8,128)(2,1)S(1)}, u32[]{:S(2)}, u32[]{:S(2)}) collective-permute-start(bf16[32,2048]{1,0:T(8,128)(2,1)S(1)} %fusion.127), channel_id=1, source_target_pairs={{0,32},{32,64},{64,96},{96,128},{128,160},{160,192},{192,224},{1,3... | collective-permute-start | bytes 393224 | tf_op jit(solution)/shard_map/while/body/eval_jaxpr/ppermute | solution.py:21
  560.8 17.0 %collective-permute-start = (bf16[32,2048]{1,0:T(8,128)(2,1)S(1)}, bf16[32,2048]{1,0:T(8,128)(2,1)S(1)}, u32[]{:S(2)}, u32[]{:S(2)}) collective-permute-start(bf16[32,2048]{1,0:T(8,128)(2,1)S(1)} %fusion.127), channel_id=1, source_target_pairs={{0,32},{32,64},{64,96},{96,128},{128,160},{160,192},{192,224},{1,3... | collective-permute-start | bytes 393224 | tf_op jit(solution)/shard_map/while/body/eval_jaxpr/ppermute | solution.py:21
  619.2 17.1 %collective-permute-start = (bf16[32,2048]{1,0:T(8,128)(2,1)S(1)}, bf16[32,2048]{1,0:T(8,128)(2,1)S(1)}, u32[]{:S(2)}, u32[]{:S(2)}) collective-permute-start(bf16[32,2048]{1,0:T(8,128)(2,1)S(1)} %fusion.127), channel_id=1, source_target_pairs={{0,32},{32,64},{64,96},{96,128},{128,160},{160,192},{192,224},{1,3... | collective-permute-start | bytes 393224 | tf_op jit(solution)/shard_map/while/body/eval_jaxpr/ppermute | solution.py:21
  677.7 17.1 %collective-permute-start = (bf16[32,2048]{1,0:T(8,128)(2,1)S(1)}, bf16[32,2048]{1,0:T(8,128)(2,1)S(1)}, u32[]{:S(2)}, u32[]{:S(2)}) collective-permute-start(bf16[32,2048]{1,0:T(8,128)(2,1)S(1)} %fusion.127), channel_id=1, source_target_pairs={{0,32},{32,64},{64,96},{96,128},{128,160},{160,192},{192,224},{1,3... | collective-permute-start | bytes 393224 | tf_op jit(solution)/shard_map/while/body/eval_jaxpr/ppermute | solution.py:21
  743.3 17.6 %collective-permute-start.1 = (bf16[32,2048]{1,0:T(8,128)(2,1)S(1)}, bf16[32,2048]{1,0:T(8,128)(2,1)S(1)}, u32[]{:S(2)}, u32[]{:S(2)}) collective-permute-start(bf16[32,2048]{1,0:T(8,128)(2,1)S(1)} %fusion.137), channel_id=1, source_target_pairs={{32,0},{64,32},{96,64},{128,96},{160,128},{192,160},{224,192},{33,... | collective-permute-start | bytes 393224 | tf_op jit(solution)/shard_map/while/body/eval_jaxpr/ppermute | solution.py:21
  804.0 17.0 %collective-permute-start.1 = (bf16[32,2048]{1,0:T(8,128)(2,1)S(1)}, bf16[32,2048]{1,0:T(8,128)(2,1)S(1)}, u32[]{:S(2)}, u32[]{:S(2)}) collective-permute-start(bf16[32,2048]{1,0:T(8,128)(2,1)S(1)} %fusion.137), channel_id=1, source_target_pairs={{32,0},{64,32},{96,64},{128,96},{160,128},{192,160},{224,192},{33,... | collective-permute-start | bytes 393224 | tf_op jit(solution)/shard_map/while/body/eval_jaxpr/ppermute | solution.py:21
  864.1 17.0 %collective-permute-start.1 = (bf16[32,2048]{1,0:T(8,128)(2,1)S(1)}, bf16[32,2048]{1,0:T(8,128)(2,1)S(1)}, u32[]{:S(2)}, u32[]{:S(2)}) collective-permute-start(bf16[32,2048]{1,0:T(8,128)(2,1)S(1)} %fusion.137), channel_id=1, source_target_pairs={{32,0},{64,32},{96,64},{128,96},{160,128},{192,160},{224,192},{33,... | collective-permute-start | bytes 393224 | tf_op jit(solution)/shard_map/while/body/eval_jaxpr/ppermute | solution.py:21
  924.3 29.7 %collective-permute-start.1 = (bf16[32,2048]{1,0:T(8,128)(2,1)S(1)}, bf16[32,2048]{1,0:T(8,128)(2,1)S(1)}, u32[]{:S(2)}, u32[]{:S(2)}) collective-permute-start(bf16[32,2048]{1,0:T(8,128)(2,1)S(1)} %fusion.137), channel_id=1, source_target_pairs={{32,0},{64,32},{96,64},{128,96},{160,128},{192,160},{224,192},{33,... | collective-permute-start | bytes 393224 | tf_op jit(solution)/shard_map/while/body/eval_jaxpr/ppermute | solution.py:21
  1010.5 17.0 %collective-permute-start.1 = (bf16[32,2048]{1,0:T(8,128)(2,1)S(1)}, bf16[32,2048]{1,0:T(8,128)(2,1)S(1)}, u32[]{:S(2)}, u32[]{:S(2)}) collective-permute-start(bf16[32,2048]{1,0:T(8,128)(2,1)S(1)} %fusion.137), channel_id=1, source_target_pairs={{32,0},{64,32},{96,64},{128,96},{160,128},{192,160},{224,192},{33,... | collective-permute-start | bytes 393224 | tf_op jit(solution)/shard_map/while/body/eval_jaxpr/ppermute | solution.py:21
  1083.9 17.0 %collective-permute-start.1 = (bf16[32,2048]{1,0:T(8,128)(2,1)S(1)}, bf16[32,2048]{1,0:T(8,128)(2,1)S(1)}, u32[]{:S(2)}, u32[]{:S(2)}) collective-permute-start(bf16[32,2048]{1,0:T(8,128)(2,1)S(1)} %fusion.137), channel_id=1, source_target_pairs={{32,0},{64,32},{96,64},{128,96},{160,128},{192,160},{224,192},{33,... | collective-permute-start | bytes 393224 | tf_op jit(solution)/shard_map/while/body/eval_jaxpr/ppermute | solution.py:21
  1157.3 17.0 %collective-permute-start.1 = (bf16[32,2048]{1,0:T(8,128)(2,1)S(1)}, bf16[32,2048]{1,0:T(8,128)(2,1)S(1)}, u32[]{:S(2)}, u32[]{:S(2)}) collective-permute-start(bf16[32,2048]{1,0:T(8,128)(2,1)S(1)} %fusion.137), channel_id=1, source_target_pairs={{32,0},{64,32},{96,64},{128,96},{160,128},{192,160},{224,192},{33,... | collective-permute-start | bytes 393224 | tf_op jit(solution)/shard_map/while/body/eval_jaxpr/ppermute | solution.py:21
  1230.7 17.0 %collective-permute-start.1 = (bf16[32,2048]{1,0:T(8,128)(2,1)S(1)}, bf16[32,2048]{1,0:T(8,128)(2,1)S(1)}, u32[]{:S(2)}, u32[]{:S(2)}) collective-permute-start(bf16[32,2048]{1,0:T(8,128)(2,1)S(1)} %fusion.137), channel_id=1, source_target_pairs={{32,0},{64,32},{96,64},{128,96},{160,128},{192,160},{224,192},{33,... | collective-permute-start | bytes 393224 | tf_op jit(solution)/shard_map/while/body/eval_jaxpr/ppermute | solution.py:21
  1290.9 17.2 %collective-permute-start.1 = (bf16[32,2048]{1,0:T(8,128)(2,1)S(1)}, bf16[32,2048]{1,0:T(8,128)(2,1)S(1)}, u32[]{:S(2)}, u32[]{:S(2)}) collective-permute-start(bf16[32,2048]{1,0:T(8,128)(2,1)S(1)} %fusion.137), channel_id=1, source_target_pairs={{32,0},{64,32},{96,64},{128,96},{160,128},{192,160},{224,192},{33,... | collective-permute-start | bytes 393224 | tf_op jit(solution)/shard_map/while/body/eval_jaxpr/ppermute | solution.py:21
  1351.2 17.0 %collective-permute-start.1 = (bf16[32,2048]{1,0:T(8,128)(2,1)S(1)}, bf16[32,2048]{1,0:T(8,128)(2,1)S(1)}, u32[]{:S(2)}, u32[]{:S(2)}) collective-permute-start(bf16[32,2048]{1,0:T(8,128)(2,1)S(1)} %fusion.137), channel_id=1, source_target_pairs={{32,0},{64,32},{96,64},{128,96},{160,128},{192,160},{224,192},{33,... | collective-permute-start | bytes 393224 | tf_op jit(solution)/shard_map/while/body/eval_jaxpr/ppermute | solution.py:21
  1411.4 17.0 %collective-permute-start.1 = (bf16[32,2048]{1,0:T(8,128)(2,1)S(1)}, bf16[32,2048]{1,0:T(8,128)(2,1)S(1)}, u32[]{:S(2)}, u32[]{:S(2)}) collective-permute-start(bf16[32,2048]{1,0:T(8,128)(2,1)S(1)} %fusion.137), channel_id=1, source_target_pairs={{32,0},{64,32},{96,64},{128,96},{160,128},{192,160},{224,192},{33,... | collective-permute-start | bytes 393224 | tf_op jit(solution)/shard_map/while/body/eval_jaxpr/ppermute | solution.py:21
  (19 other events, 102.8 us)
Sparse Core Ops, SparseCore 0:
  1434.0 99.8 all-reduce.2

commit v5 on v4

--- a/solution.py
+++ b/solution.py
@@ -101,7 +101,9 @@
 
     def slot_sources(dest_rows):
         pair_ids = jnp.arange(dest_rows.shape[0], dtype=jnp.int32)
-        return jnp.full((experts_all * capacity,), -1, jnp.int32).at[dest_rows].set(pair_ids)
+        slot_ids = jnp.arange(experts_all * capacity, dtype=jnp.int32)
+        hits = dest_rows[:, None] == slot_ids[None, :]
+        return jnp.max(jnp.where(hits, pair_ids[:, None], -1), axis=0)
 
     dest_all = jax.vmap(slot_rows)(route_all)
     source_all = jax.vmap(slot_sources)(dest_all)
@@ -165,28 +167,26 @@
     start_act = jnp.zeros((tok_rows, features), jnp.bfloat16)
     _, saved = lax.scan(forward_step, start_act, jnp.arange(step_count))
 
-    def expert_backward(received, dreceived, preact):
-        hidden = jax.nn.gelu(preact).astype(jnp.bfloat16)
-        down_inc = jnp.einsum(
-            "sech,secd->ehd", hidden, dreceived, preferred_element_type=jnp.float32
-        )
+    def expert_backward(dreceived, preact):
         dhidden = jnp.einsum(
             "secd,ehd->sech", dreceived, w_down, preferred_element_type=jnp.float32
         )
         _, pullback = jax.vjp(jax.nn.gelu, preact)
         dpre = pullback(dhidden)[0].astype(jnp.bfloat16)
-        up_inc = jnp.einsum("secd,sech->edh", received, dpre, preferred_element_type=jnp.float32)
         dinbuf = jnp.einsum(
             "sech,edh->secd", dpre, w_up, preferred_element_type=jnp.float32
         ).astype(jnp.bfloat16)
-        return (up_inc, down_inc, dinbuf)
+        return (dinbuf, dpre, dreceived)
 
     def backward_skip(operands):
-        received, acc_up, acc_down = operands[0], operands[3], operands[4]
-        return (acc_up, acc_down, jnp.zeros_like(received))
-
-    def backward_step(carry, step_index):
-        incoming, acc_up, acc_down = carry
+        dreceived, preact = operands
+        return (
+            jnp.zeros_like(dreceived),
+            jnp.zeros(preact.shape, jnp.bfloat16),
+            jnp.zeros_like(dreceived),
+        )
+
+    def backward_step(incoming, step_index):
         micro_raw = step_index - (section_count - 1 - section_pos)
         live_step = (micro_raw >= 0) & (micro_raw < micro_count)
         micro = jnp.clip(micro_raw, 0, micro_count - 1)
@@ -199,7 +199,7 @@
         route_rows = lax.dynamic_index_in_dim(route_all, micro, 0, keepdims=False)
         dest_rows = lax.dynamic_index_in_dim(dest_all, micro, 0, keepdims=False)
         sources = lax.dynamic_index_in_dim(source_all, micro, 0, keepdims=False)
-        as_f32, rscale, normed = normalize(section_in)
+        as_f32, rscale, _ = normalize(section_in)
         total = jnp.sum(gatev, axis=-1, keepdims=True)
         wgt = gatev / total
         grad_f32 = grad_out.astype(jnp.float32)
@@ -211,19 +211,12 @@
         )
         dsend = to_buffer(dout, sources, 1)
         dreceived = as_rows(expert_exchange(dsend, 1))
-        received = lax.dynamic_index_in_dim(saved[3], fwd_index, 0, keepdims=False)
         preact = lax.dynamic_index_in_dim(saved[4], fwd_index, 0, keepdims=False)
 
         def backward_live(operands):
-            up_inc, down_inc, dinbuf = expert_backward(operands[0], operands[1], operands[2])
-            return (operands[3] + up_inc, operands[4] + down_inc, dinbuf)
-
-        new_up, new_down, dinbuf = lax.cond(
-            live_step,
-            backward_live,
-            backward_skip,
-            (received, dreceived, preact, acc_up, acc_down),
-        )
+            return expert_backward(operands[0], operands[1])
+
+        dinbuf, dpre, dkept = lax.cond(live_step, backward_live, backward_skip, (dreceived, preact))
         dreturned = expert_exchange(as_pieces(dinbuf), 2)
         dexp = jnp.sum(from_buffer(dreturned, dest_rows).astype(jnp.float32), axis=1)
         dgate = (dwgt - jnp.sum(wgt * dwgt, axis=-1, keepdims=True)) / total
@@ -238,16 +231,21 @@
             - as_f32 * rscale**3 * jnp.mean(dnorm * as_f32, axis=-1, keepdims=True)
         ).astype(jnp.bfloat16)
         passed = from_behind(grad_in, "section", -1)
-        return ((passed, new_up, new_down), None)
-
-    start_carry = (
-        jnp.zeros((tok_rows, features), jnp.bfloat16),
-        jnp.zeros(w_up.shape, jnp.float32),
-        jnp.zeros(w_down.shape, jnp.float32),
-    )
-    final_carry, _ = lax.scan(backward_step, start_carry, jnp.arange(step_count))
-    acc_up = final_carry[1]
-    acc_down = final_carry[2]
+        return (passed, (dpre, dkept))
+
+    start_grad = jnp.zeros((tok_rows, features), jnp.bfloat16)
+    _, (dpre_all, dreceived_all) = lax.scan(backward_step, start_grad, jnp.arange(step_count))
+    back_steps = jnp.arange(step_count)
+    fwd_of_back = jnp.clip(back_steps - (section_count - 1 - section_pos), 0, micro_count - 1)
+    fwd_of_back = fwd_of_back + section_pos
+    received_all = jnp.take(saved[3], fwd_of_back, axis=0)
+    hidden_all = jax.nn.gelu(jnp.take(saved[4], fwd_of_back, axis=0)).astype(jnp.bfloat16)
+    acc_up = jnp.einsum(
+        "bsecd,bsech->edh", received_all, dpre_all, preferred_element_type=jnp.float32
+    )
+    acc_down = jnp.einsum(
+        "bsech,bsecd->ehd", hidden_all, dreceived_all, preferred_element_type=jnp.float32
+    )
     sum_up, sum_down = lax.psum(
         (acc_up.astype(jnp.bfloat16), acc_down.astype(jnp.bfloat16)), "dp"
     )

time: 1550 us -> 1520 us (0.981)
  waiting for transfers between devices: 295 us -> 255 us
  local copies, waits for them, and re-layouts: 236 us -> 255 us
    ppermute x22, waiting for transfers between devices: 195 us -> 162 us  [from_behind(): return lax.ppermute(block, axis, route)]
    scatter x1 -> x0, local copies, waits for them, and re-layouts: 24.7 us -> none  [slot_sources(): jnp.full((experts_all * capacity,), -1, jnp.int32).at[dest_rows]]
    dynamic_update_slice x0 -> x11, local copies, waits for them, and re-layouts: none -> 17.7 us  [local(): lax.scan(backward_step, start_grad, jnp.arange(step_count))]
    dynamic_update_slice x33 -> x44, local copies, waits for them, and re-layouts: 41.6 us -> 52.3 us  [local(): _, saved = lax.scan(forward_step, start_act, jnp.arange(step_count))]
  transfers between devices with their start and end apart: 23 -> 23, of which waited for: 23 -> 23; matrix products, arithmetic and copies ran while one was open for 3% -> 5% of each run, Pallas kernels for 0% -> 0%
where the time goes in v5:
time: 1520 us; the launch traced here: 1510 us
  Pallas kernels  646 us (42%)
  local copies, waits for them, and re-layouts  255 us (17%)
  waiting for transfers between devices  255 us (17%)
  starting transfers between devices  132 us (9%)
  other arithmetic  106 us (7%)
  matrix products  78.9 us (5%)
  loops' own time  19.4 us (1%)
    pallas_call x44, Pallas kernels, expert_exchange(): pl.pallas_call(functools.partial(exchange_kernel, n), out_shape=jax.Shape...  646 us
    ppermute x22, waiting for transfers between devices, from_behind(): return lax.ppermute(block, axis, route)  162 us
    ppermute x22, starting transfers between devices, from_behind(): return lax.ppermute(block, axis, route)  132 us
    psum x1, waiting for transfers between devices, local(): lax.psum((acc_up.astype(jnp.bfloat16), acc_down.astype(jnp.bfloat16)), 'dp')  93.2 us
    dynamic_update_slice x44, local copies, waits for them, and re-layouts, local(): _, saved = lax.scan(forward_step, start_act, jnp.arange(step_count))  52.3 us
    gather x22, local copies, waits for them, and re-layouts, from_buffer(): buffer.reshape(experts_all * capacity, pieces, lanes)[dest_rows]  38.7 us
  transfers between devices with their start and end apart: 23, of which 23 were waited for; matrix products, arithmetic and copies ran while one was open for 5% of the time, Pallas kernels for 0%

profile of v5, /device:TPU:62, one launch (start us, length us, event | category | flops | bytes accessed | tf_op | source)
XLA Modules:
  0.0 1506.9 jit_solution(7722996465665083293)
XLA Ops:
  13.6 660.1 %while.39 = (s32[]{:T(128)}, bf16[32,2048]{1,0:T(8,128)(2,1)S(1)}, bf16[11,32,2048]{2,1,0:T(8,128)(2,1)}, f32[11,32,4]{1,2,0:T(4,128)S(1)}, bf16[11,32,4,2048]{3...) while((s32[]{:T(128)}, bf16[32,2048]{1,0:T(8,128)(2,1)S(1)}, ...), condition=%wide.region_9.10_spmd, body=%wide.region_3.9_spmd.sunk | while | flops 573976576 | bytes 24260048 | solution.py:168
  19.0 16.2 %eval_jaxpr.16 = bf16[8,272,128]{2,1,0:T(8,128)(2,1)S(1)} custom-call(bf16[8,272,128]{2,1,0:T(8,128)(2,1)} %bitcast_select_fusion.8.x_ref), custom_call_target="tpu_custom_call" | custom-call | bytes 1114112 | tf_op jit(solution)/shard_map/while/body/eval_jaxpr/pallas_call | solution.py:55
  37.3 15.7 %eval_jaxpr.17 = bf16[8,272,128]{2,1,0:T(8,128)(2,1)} custom-call(bf16[8,272,128]{2,1,0:T(8,128)(2,1)} %reshape.736.x_ref), custom_call_target="tpu_custom_call" | custom-call | bytes 1114112 | tf_op jit(solution)/shard_map/while/body/eval_jaxpr/pallas_call | solution.py:55
  92.1 14.9 eval_jaxpr.17
  150.4 14.9 eval_jaxpr.17
  213.7 14.9 eval_jaxpr.17
  272.1 14.9 eval_jaxpr.17
  335.3 14.9 eval_jaxpr.17
  457.1 14.9 eval_jaxpr.17
  476.7 15.1 %collective-permute-start = (bf16[32,2048]{1,0:T(8,128)(2,1)S(1)}, bf16[32,2048]{1,0:T(8,128)(2,1)S(1)}, u32[]{:S(2)}, u32[]{:S(2)}) collective-permute-start(bf16[32,2048]{1,0:T(8,128)(2,1)S(1)} %fusion.137), channel_id=1, source_target_pairs={{0,32},{32,64},{64,96},{96,128},{128,160},{160,192},{192,224},{1,3... | collective-permute-start | bytes 393224 | tf_op jit(solution)/shard_map/while/body/eval_jaxpr/ppermute | solution.py:21
  520.1 14.9 eval_jaxpr.17
  578.5 14.9 eval_jaxpr.17
  636.9 14.9 eval_jaxpr.17
  691.9 693.0 %while.40 = (s32[]{:T(128)}, bf16[32,2048]{1,0:T(8,128)(2,1)S(1)}, bf16[11,8,1,17,512]{4,3,1,2,0:T(8,128)(2,1)}, bf16[11,8,1,17,2048]{4,3,1,2,0:T(8,128)(2,1)}, ...) while((s32[]{:T(128)}, bf16[32,2048]{1,0:T(8,128)(2,1)S(1)}, ...), condition=%wide.region_20.21_spmd.clone, body=%wide.region_10.20_spmd.clone.sunk | while | flops 581163648 | bytes 27663032 | solution.py:237
  714.4 14.9 eval_jaxpr.19
  775.7 14.9 eval_jaxpr.19
  836.6 14.9 eval_jaxpr.19
  897.4 14.9 eval_jaxpr.19
  1030.5 14.9 eval_jaxpr.19
  1097.0 14.9 eval_jaxpr.19
  1163.4 14.9 eval_jaxpr.19
  1224.2 14.9 eval_jaxpr.19
  1285.2 14.9 eval_jaxpr.19
  1402.3 93.2 %all-reduce.3.cloned.1.call-done = (bf16[1,1,2048,512]{3,2,1,0:T(8,128)(2,1)}, bf16[1,1,512,2048]{3,2,1,0:T(8,128)(2,1)}) async-done(((bf16[1,1,2048,512]{3,2,1,0:T(8,128)(2,1)}, bf16[1,1,512,2048]{3,2,1,0:T(8,128)(2,1)}), (bf16[1,1,2048,512]{3,2,1,0:T(8,128)(2,1)}, bf16[1,1,512,2048]{3,2,1,0:T(8,128)(2,1)})) %all-reduce.3.cloned.1.call-update) | async-done | bytes 4194320 | tf_op jit(solution)/shard_map/psum | solution.py:249
  (1016 shorter events, 1125.4 us)
Async XLA Ops:
  7.2 1488.4 %all-reduce.3.cloned.1.call-start = ((), (), s32[]{:S(2)}) async-start(), calls=%async_computation | async-start | bytes 8388608 | tf_op jit(solution)/shard_map/psum | solution.py:249
  57.6 12.7 collective-permute-start
  111.7 17.0 %collective-permute-start = (bf16[32,2048]{1,0:T(8,128)(2,1)S(1)}, bf16[32,2048]{1,0:T(8,128)(2,1)S(1)}, u32[]{:S(2)}, u32[]{:S(2)}) collective-permute-start(bf16[32,2048]{1,0:T(8,128)(2,1)S(1)} %fusion.137), channel_id=1, source_target_pairs={{0,32},{32,64},{64,96},{96,128},{128,160},{160,192},{192,224},{1,3... | collective-permute-start | bytes 393224 | tf_op jit(solution)/shard_map/while/body/eval_jaxpr/ppermute | solution.py:21
  170.0 17.1 %collective-permute-start = (bf16[32,2048]{1,0:T(8,128)(2,1)S(1)}, bf16[32,2048]{1,0:T(8,128)(2,1)S(1)}, u32[]{:S(2)}, u32[]{:S(2)}) collective-permute-start(bf16[32,2048]{1,0:T(8,128)(2,1)S(1)} %fusion.137), channel_id=1, source_target_pairs={{0,32},{32,64},{64,96},{96,128},{128,160},{160,192},{192,224},{1,3... | collective-permute-start | bytes 393224 | tf_op jit(solution)/shard_map/while/body/eval_jaxpr/ppermute | solution.py:21
  233.3 12.4 collective-permute-start
  291.7 17.1 %collective-permute-start = (bf16[32,2048]{1,0:T(8,128)(2,1)S(1)}, bf16[32,2048]{1,0:T(8,128)(2,1)S(1)}, u32[]{:S(2)}, u32[]{:S(2)}) collective-permute-start(bf16[32,2048]{1,0:T(8,128)(2,1)S(1)} %fusion.137), channel_id=1, source_target_pairs={{0,32},{32,64},{64,96},{96,128},{128,160},{160,192},{192,224},{1,3... | collective-permute-start | bytes 393224 | tf_op jit(solution)/shard_map/while/body/eval_jaxpr/ppermute | solution.py:21
  354.9 17.2 %collective-permute-start = (bf16[32,2048]{1,0:T(8,128)(2,1)S(1)}, bf16[32,2048]{1,0:T(8,128)(2,1)S(1)}, u32[]{:S(2)}, u32[]{:S(2)}) collective-permute-start(bf16[32,2048]{1,0:T(8,128)(2,1)S(1)} %fusion.137), channel_id=1, source_target_pairs={{0,32},{32,64},{64,96},{96,128},{128,160},{160,192},{192,224},{1,3... | collective-permute-start | bytes 393224 | tf_op jit(solution)/shard_map/while/body/eval_jaxpr/ppermute | solution.py:21
  418.2 17.1 %collective-permute-start = (bf16[32,2048]{1,0:T(8,128)(2,1)S(1)}, bf16[32,2048]{1,0:T(8,128)(2,1)S(1)}, u32[]{:S(2)}, u32[]{:S(2)}) collective-permute-start(bf16[32,2048]{1,0:T(8,128)(2,1)S(1)} %fusion.137), channel_id=1, source_target_pairs={{0,32},{32,64},{64,96},{96,128},{128,160},{160,192},{192,224},{1,3... | collective-permute-start | bytes 393224 | tf_op jit(solution)/shard_map/while/body/eval_jaxpr/ppermute | solution.py:21
  476.7 21.7 %collective-permute-start = (bf16[32,2048]{1,0:T(8,128)(2,1)S(1)}, bf16[32,2048]{1,0:T(8,128)(2,1)S(1)}, u32[]{:S(2)}, u32[]{:S(2)}) collective-permute-start(bf16[32,2048]{1,0:T(8,128)(2,1)S(1)} %fusion.137), channel_id=1, source_target_pairs={{0,32},{32,64},{64,96},{96,128},{128,160},{160,192},{192,224},{1,3... | collective-permute-start | bytes 393224 | tf_op jit(solution)/shard_map/while/body/eval_jaxpr/ppermute | solution.py:21
  539.7 17.0 %collective-permute-start = (bf16[32,2048]{1,0:T(8,128)(2,1)S(1)}, bf16[32,2048]{1,0:T(8,128)(2,1)S(1)}, u32[]{:S(2)}, u32[]{:S(2)}) collective-permute-start(bf16[32,2048]{1,0:T(8,128)(2,1)S(1)} %fusion.137), channel_id=1, source_target_pairs={{0,32},{32,64},{64,96},{96,128},{128,160},{160,192},{192,224},{1,3... | collective-permute-start | bytes 393224 | tf_op jit(solution)/shard_map/while/body/eval_jaxpr/ppermute | solution.py:21
  598.1 17.1 %collective-permute-start = (bf16[32,2048]{1,0:T(8,128)(2,1)S(1)}, bf16[32,2048]{1,0:T(8,128)(2,1)S(1)}, u32[]{:S(2)}, u32[]{:S(2)}) collective-permute-start(bf16[32,2048]{1,0:T(8,128)(2,1)S(1)} %fusion.137), channel_id=1, source_target_pairs={{0,32},{32,64},{64,96},{96,128},{128,160},{160,192},{192,224},{1,3... | collective-permute-start | bytes 393224 | tf_op jit(solution)/shard_map/while/body/eval_jaxpr/ppermute | solution.py:21
  656.5 17.1 %collective-permute-start = (bf16[32,2048]{1,0:T(8,128)(2,1)S(1)}, bf16[32,2048]{1,0:T(8,128)(2,1)S(1)}, u32[]{:S(2)}, u32[]{:S(2)}) collective-permute-start(bf16[32,2048]{1,0:T(8,128)(2,1)S(1)} %fusion.137), channel_id=1, source_target_pairs={{0,32},{32,64},{64,96},{96,128},{128,160},{160,192},{192,224},{1,3... | collective-permute-start | bytes 393224 | tf_op jit(solution)/shard_map/while/body/eval_jaxpr/ppermute | solution.py:21
  736.0 17.4 %collective-permute-start.1 = (bf16[32,2048]{1,0:T(8,128)(2,1)S(1)}, bf16[32,2048]{1,0:T(8,128)(2,1)S(1)}, u32[]{:S(2)}, u32[]{:S(2)}) collective-permute-start(bf16[32,2048]{1,0:T(8,128)(2,1)S(1)} %fusion.148), channel_id=1, source_target_pairs={{32,0},{64,32},{96,64},{128,96},{160,128},{192,160},{224,192},{33,... | collective-permute-start | bytes 393224 | tf_op jit(solution)/shard_map/while/body/eval_jaxpr/ppermute | solution.py:21
  797.3 17.0 %collective-permute-start.1 = (bf16[32,2048]{1,0:T(8,128)(2,1)S(1)}, bf16[32,2048]{1,0:T(8,128)(2,1)S(1)}, u32[]{:S(2)}, u32[]{:S(2)}) collective-permute-start(bf16[32,2048]{1,0:T(8,128)(2,1)S(1)} %fusion.148), channel_id=1, source_target_pairs={{32,0},{64,32},{96,64},{128,96},{160,128},{192,160},{224,192},{33,... | collective-permute-start | bytes 393224 | tf_op jit(solution)/shard_map/while/body/eval_jaxpr/ppermute | solution.py:21
  858.2 17.0 %collective-permute-start.1 = (bf16[32,2048]{1,0:T(8,128)(2,1)S(1)}, bf16[32,2048]{1,0:T(8,128)(2,1)S(1)}, u32[]{:S(2)}, u32[]{:S(2)}) collective-permute-start(bf16[32,2048]{1,0:T(8,128)(2,1)S(1)} %fusion.148), channel_id=1, source_target_pairs={{32,0},{64,32},{96,64},{128,96},{160,128},{192,160},{224,192},{33,... | collective-permute-start | bytes 393224 | tf_op jit(solution)/shard_map/while/body/eval_jaxpr/ppermute | solution.py:21
  919.1 17.0 %collective-permute-start.1 = (bf16[32,2048]{1,0:T(8,128)(2,1)S(1)}, bf16[32,2048]{1,0:T(8,128)(2,1)S(1)}, u32[]{:S(2)}, u32[]{:S(2)}) collective-permute-start(bf16[32,2048]{1,0:T(8,128)(2,1)S(1)} %fusion.148), channel_id=1, source_target_pairs={{32,0},{64,32},{96,64},{128,96},{160,128},{192,160},{224,192},{33,... | collective-permute-start | bytes 393224 | tf_op jit(solution)/shard_map/while/body/eval_jaxpr/ppermute | solution.py:21
  985.4 17.2 %collective-permute-start.1 = (bf16[32,2048]{1,0:T(8,128)(2,1)S(1)}, bf16[32,2048]{1,0:T(8,128)(2,1)S(1)}, u32[]{:S(2)}, u32[]{:S(2)}) collective-permute-start(bf16[32,2048]{1,0:T(8,128)(2,1)S(1)} %fusion.148), channel_id=1, source_target_pairs={{32,0},{64,32},{96,64},{128,96},{160,128},{192,160},{224,192},{33,... | collective-permute-start | bytes 393224 | tf_op jit(solution)/shard_map/while/body/eval_jaxpr/ppermute | solution.py:21
  1052.1 17.1 %collective-permute-start.1 = (bf16[32,2048]{1,0:T(8,128)(2,1)S(1)}, bf16[32,2048]{1,0:T(8,128)(2,1)S(1)}, u32[]{:S(2)}, u32[]{:S(2)}) collective-permute-start(bf16[32,2048]{1,0:T(8,128)(2,1)S(1)} %fusion.148), channel_id=1, source_target_pairs={{32,0},{64,32},{96,64},{128,96},{160,128},{192,160},{224,192},{33,... | collective-permute-start | bytes 393224 | tf_op jit(solution)/shard_map/while/body/eval_jaxpr/ppermute | solution.py:21
  1118.6 17.0 %collective-permute-start.1 = (bf16[32,2048]{1,0:T(8,128)(2,1)S(1)}, bf16[32,2048]{1,0:T(8,128)(2,1)S(1)}, u32[]{:S(2)}, u32[]{:S(2)}) collective-permute-start(bf16[32,2048]{1,0:T(8,128)(2,1)S(1)} %fusion.148), channel_id=1, source_target_pairs={{32,0},{64,32},{96,64},{128,96},{160,128},{192,160},{224,192},{33,... | collective-permute-start | bytes 393224 | tf_op jit(solution)/shard_map/while/body/eval_jaxpr/ppermute | solution.py:21
  1185.0 17.0 %collective-permute-start.1 = (bf16[32,2048]{1,0:T(8,128)(2,1)S(1)}, bf16[32,2048]{1,0:T(8,128)(2,1)S(1)}, u32[]{:S(2)}, u32[]{:S(2)}) collective-permute-start(bf16[32,2048]{1,0:T(8,128)(2,1)S(1)} %fusion.148), channel_id=1, source_target_pairs={{32,0},{64,32},{96,64},{128,96},{160,128},{192,160},{224,192},{33,... | collective-permute-start | bytes 393224 | tf_op jit(solution)/shard_map/while/body/eval_jaxpr/ppermute | solution.py:21
  1245.9 17.1 %collective-permute-start.1 = (bf16[32,2048]{1,0:T(8,128)(2,1)S(1)}, bf16[32,2048]{1,0:T(8,128)(2,1)S(1)}, u32[]{:S(2)}, u32[]{:S(2)}) collective-permute-start(bf16[32,2048]{1,0:T(8,128)(2,1)S(1)} %fusion.148), channel_id=1, source_target_pairs={{32,0},{64,32},{96,64},{128,96},{160,128},{192,160},{224,192},{33,... | collective-permute-start | bytes 393224 | tf_op jit(solution)/shard_map/while/body/eval_jaxpr/ppermute | solution.py:21
  1306.9 17.1 %collective-permute-start.1 = (bf16[32,2048]{1,0:T(8,128)(2,1)S(1)}, bf16[32,2048]{1,0:T(8,128)(2,1)S(1)}, u32[]{:S(2)}, u32[]{:S(2)}) collective-permute-start(bf16[32,2048]{1,0:T(8,128)(2,1)S(1)} %fusion.148), channel_id=1, source_target_pairs={{32,0},{64,32},{96,64},{128,96},{160,128},{192,160},{224,192},{33,... | collective-permute-start | bytes 393224 | tf_op jit(solution)/shard_map/while/body/eval_jaxpr/ppermute | solution.py:21
  1367.9 17.0 %collective-permute-start.1 = (bf16[32,2048]{1,0:T(8,128)(2,1)S(1)}, bf16[32,2048]{1,0:T(8,128)(2,1)S(1)}, u32[]{:S(2)}, u32[]{:S(2)}) collective-permute-start(bf16[32,2048]{1,0:T(8,128)(2,1)S(1)} %fusion.148), channel_id=1, source_target_pairs={{32,0},{64,32},{96,64},{128,96},{160,128},{192,160},{224,192},{33,... | collective-permute-start | bytes 393224 | tf_op jit(solution)/shard_map/while/body/eval_jaxpr/ppermute | solution.py:21
  1384.9 10.9 copy-start.4
  (4 other events, 23.0 us)
Sparse Core Ops, SparseCore 0:
  1402.4 93.0 all-reduce.2

commit v6 on v5

--- a/solution.py
+++ b/solution.py
@@ -235,20 +235,20 @@
 
     start_grad = jnp.zeros((tok_rows, features), jnp.bfloat16)
     _, (dpre_all, dreceived_all) = lax.scan(backward_step, start_grad, jnp.arange(step_count))
-    back_steps = jnp.arange(step_count)
-    fwd_of_back = jnp.clip(back_steps - (section_count - 1 - section_pos), 0, micro_count - 1)
-    fwd_of_back = fwd_of_back + section_pos
-    received_all = jnp.take(saved[3], fwd_of_back, axis=0)
-    hidden_all = jax.nn.gelu(jnp.take(saved[4], fwd_of_back, axis=0)).astype(jnp.bfloat16)
+    first_back = section_count - 1 - section_pos
+    dpre_live = lax.dynamic_slice_in_dim(dpre_all, first_back, micro_count, axis=0)
+    dreceived_live = lax.dynamic_slice_in_dim(dreceived_all, first_back, micro_count, axis=0)
+    received_live = lax.dynamic_slice_in_dim(saved[3], section_pos, micro_count, axis=0)
+    preact_live = lax.dynamic_slice_in_dim(saved[4], section_pos, micro_count, axis=0)
+    hidden_live = jax.nn.gelu(preact_live).astype(jnp.bfloat16)
     acc_up = jnp.einsum(
-        "bsecd,bsech->edh", received_all, dpre_all, preferred_element_type=jnp.float32
+        "bsecd,bsech->edh", received_live, dpre_live, preferred_element_type=jnp.float32
     )
+    sum_up = lax.psum(acc_up.astype(jnp.bfloat16), "dp")
     acc_down = jnp.einsum(
-        "bsech,bsecd->ehd", hidden_all, dreceived_all, preferred_element_type=jnp.float32
+        "bsech,bsecd->ehd", hidden_live, dreceived_live, preferred_element_type=jnp.float32
     )
-    sum_up, sum_down = lax.psum(
-        (acc_up.astype(jnp.bfloat16), acc_down.astype(jnp.bfloat16)), "dp"
-    )
+    sum_down = lax.psum(acc_down.astype(jnp.bfloat16), "dp")
     up_out = sum_up.astype(jnp.bfloat16)
     down_out = sum_down.astype(jnp.bfloat16)
     return (up_out[None], down_out[None])

time: 1520 us -> 1500 us (0.987)
  no operation moved by 1% of the time
where the time goes in v6:
time: 1500 us; the launch traced here: 1490 us
  Pallas kernels  646 us (43%)
  waiting for transfers between devices  255 us (17%)
  local copies, waits for them, and re-layouts  241 us (16%)
  starting transfers between devices  132 us (9%)
  other arithmetic  106 us (7%)
  matrix products  72.5 us (5%)
  loops' own time  19.4 us (1%)
    pallas_call x44, Pallas kernels, expert_exchange(): pl.pallas_call(functools.partial(exchange_kernel, n), out_shape=jax.Shape...  646 us
    ppermute x22, waiting for transfers between devices, from_behind(): return lax.ppermute(block, axis, route)  162 us
    ppermute x22, starting transfers between devices, from_behind(): return lax.ppermute(block, axis, route)  132 us
    psum x1, waiting for transfers between devices, local(): sum_up = lax.psum(acc_up.astype(jnp.bfloat16), 'dp')  93.1 us
    dynamic_update_slice x44, local copies, waits for them, and re-layouts, local(): _, saved = lax.scan(forward_step, start_act, jnp.arange(step_count))  52.2 us
    gather x22, local copies, waits for them, and re-layouts, from_buffer(): buffer.reshape(experts_all * capacity, pieces, lanes)[dest_rows]  38.7 us
  transfers between devices with their start and end apart: 23, of which 23 were waited for; matrix products, arithmetic and copies ran while one was open for 5% of the time, Pallas kernels for 0%

profile of v6, /device:TPU:62, one launch (start us, length us, event | category | flops | bytes accessed | tf_op | source)
XLA Modules:
  0.0 1487.4 jit_solution(4150944755578851513)
XLA Ops:
  13.5 660.4 %while.39 = (s32[]{:T(128)}, bf16[32,2048]{1,0:T(8,128)(2,1)S(1)}, bf16[11,32,2048]{2,1,0:T(8,128)(2,1)}, f32[11,32,4]{1,2,0:T(4,128)S(1)}, bf16[11,32,4,2048]{3...) while((s32[]{:T(128)}, bf16[32,2048]{1,0:T(8,128)(2,1)S(1)}, ...), condition=%wide.region_9.10_spmd, body=%wide.region_3.9_spmd.sunk | while | flops 573976576 | bytes 24260048 | solution.py:168
  19.0 16.2 %eval_jaxpr.16 = bf16[8,272,128]{2,1,0:T(8,128)(2,1)S(1)} custom-call(bf16[8,272,128]{2,1,0:T(8,128)(2,1)} %bitcast_select_fusion.8.x_ref), custom_call_target="tpu_custom_call" | custom-call | bytes 1114112 | tf_op jit(solution)/shard_map/while/body/eval_jaxpr/pallas_call | solution.py:55
  37.2 15.7 %eval_jaxpr.17 = bf16[8,272,128]{2,1,0:T(8,128)(2,1)} custom-call(bf16[8,272,128]{2,1,0:T(8,128)(2,1)} %reshape.677.x_ref), custom_call_target="tpu_custom_call" | custom-call | bytes 1114112 | tf_op jit(solution)/shard_map/while/body/eval_jaxpr/pallas_call | solution.py:55
  92.1 14.9 %eval_jaxpr.17 = bf16[8,272,128]{2,1,0:T(8,128)(2,1)} custom-call(bf16[8,272,128]{2,1,0:T(8,128)(2,1)} %reshape.677.x_ref), custom_call_target="tpu_custom_call" | custom-call | bytes 1114112 | tf_op jit(solution)/shard_map/while/body/eval_jaxpr/pallas_call | solution.py:55
  150.5 14.9 %eval_jaxpr.17 = bf16[8,272,128]{2,1,0:T(8,128)(2,1)} custom-call(bf16[8,272,128]{2,1,0:T(8,128)(2,1)} %reshape.677.x_ref), custom_call_target="tpu_custom_call" | custom-call | bytes 1114112 | tf_op jit(solution)/shard_map/while/body/eval_jaxpr/pallas_call | solution.py:55
  213.7 14.9 %eval_jaxpr.17 = bf16[8,272,128]{2,1,0:T(8,128)(2,1)} custom-call(bf16[8,272,128]{2,1,0:T(8,128)(2,1)} %reshape.677.x_ref), custom_call_target="tpu_custom_call" | custom-call | bytes 1114112 | tf_op jit(solution)/shard_map/while/body/eval_jaxpr/pallas_call | solution.py:55
  272.2 14.9 %eval_jaxpr.17 = bf16[8,272,128]{2,1,0:T(8,128)(2,1)} custom-call(bf16[8,272,128]{2,1,0:T(8,128)(2,1)} %reshape.677.x_ref), custom_call_target="tpu_custom_call" | custom-call | bytes 1114112 | tf_op jit(solution)/shard_map/while/body/eval_jaxpr/pallas_call | solution.py:55
  335.4 14.9 %eval_jaxpr.17 = bf16[8,272,128]{2,1,0:T(8,128)(2,1)} custom-call(bf16[8,272,128]{2,1,0:T(8,128)(2,1)} %reshape.677.x_ref), custom_call_target="tpu_custom_call" | custom-call | bytes 1114112 | tf_op jit(solution)/shard_map/while/body/eval_jaxpr/pallas_call | solution.py:55
  398.7 14.9 %eval_jaxpr.17 = bf16[8,272,128]{2,1,0:T(8,128)(2,1)} custom-call(bf16[8,272,128]{2,1,0:T(8,128)(2,1)} %reshape.677.x_ref), custom_call_target="tpu_custom_call" | custom-call | bytes 1114112 | tf_op jit(solution)/shard_map/while/body/eval_jaxpr/pallas_call | solution.py:55
  457.2 14.9 %eval_jaxpr.17 = bf16[8,272,128]{2,1,0:T(8,128)(2,1)} custom-call(bf16[8,272,128]{2,1,0:T(8,128)(2,1)} %reshape.677.x_ref), custom_call_target="tpu_custom_call" | custom-call | bytes 1114112 | tf_op jit(solution)/shard_map/while/body/eval_jaxpr/pallas_call | solution.py:55
  476.8 15.1 %collective-permute-start = (bf16[32,2048]{1,0:T(8,128)(2,1)S(1)}, bf16[32,2048]{1,0:T(8,128)(2,1)S(1)}, u32[]{:S(2)}, u32[]{:S(2)}) collective-permute-start(bf16[32,2048]{1,0:T(8,128)(2,1)S(1)} %fusion.129), channel_id=1, source_target_pairs={{0,32},{32,64},{64,96},{96,128},{128,160},{160,192},{192,224},{1,3... | collective-permute-start | bytes 393224 | tf_op jit(solution)/shard_map/while/body/eval_jaxpr/ppermute | solution.py:21
  520.3 14.9 %eval_jaxpr.17 = bf16[8,272,128]{2,1,0:T(8,128)(2,1)} custom-call(bf16[8,272,128]{2,1,0:T(8,128)(2,1)} %reshape.677.x_ref), custom_call_target="tpu_custom_call" | custom-call | bytes 1114112 | tf_op jit(solution)/shard_map/while/body/eval_jaxpr/pallas_call | solution.py:55
  578.7 14.9 %eval_jaxpr.17 = bf16[8,272,128]{2,1,0:T(8,128)(2,1)} custom-call(bf16[8,272,128]{2,1,0:T(8,128)(2,1)} %reshape.677.x_ref), custom_call_target="tpu_custom_call" | custom-call | bytes 1114112 | tf_op jit(solution)/shard_map/while/body/eval_jaxpr/pallas_call | solution.py:55
  637.2 14.9 %eval_jaxpr.17 = bf16[8,272,128]{2,1,0:T(8,128)(2,1)} custom-call(bf16[8,272,128]{2,1,0:T(8,128)(2,1)} %reshape.677.x_ref), custom_call_target="tpu_custom_call" | custom-call | bytes 1114112 | tf_op jit(solution)/shard_map/while/body/eval_jaxpr/pallas_call | solution.py:55
  678.3 693.7 %while.40 = (s32[]{:T(128)}, bf16[32,2048]{1,0:T(8,128)(2,1)S(1)}, bf16[11,8,1,17,512]{4,3,1,2,0:T(8,128)(2,1)}, bf16[11,8,1,17,2048]{4,3,1,2,0:T(8,128)(2,1)}, ...) while((s32[]{:T(128)}, bf16[32,2048]{1,0:T(8,128)(2,1)S(1)}, ...), condition=%wide.region_20.21_spmd.clone, body=%wide.region_10.20_spmd.clone.sunk | while | flops 581163648 | bytes 27663032 | solution.py:237
  700.8 14.9 %eval_jaxpr.19 = bf16[8,272,128]{2,1,0:T(8,128)(2,1)} custom-call(bf16[8,272,128]{2,1,0:T(8,128)(2,1)} %reshape.685.x_ref), custom_call_target="tpu_custom_call" | custom-call | bytes 1114112 | tf_op jit(solution)/shard_map/while/body/eval_jaxpr/pallas_call | solution.py:55
  762.4 14.9 %eval_jaxpr.19 = bf16[8,272,128]{2,1,0:T(8,128)(2,1)} custom-call(bf16[8,272,128]{2,1,0:T(8,128)(2,1)} %reshape.685.x_ref), custom_call_target="tpu_custom_call" | custom-call | bytes 1114112 | tf_op jit(solution)/shard_map/while/body/eval_jaxpr/pallas_call | solution.py:55
  823.3 14.9 %eval_jaxpr.19 = bf16[8,272,128]{2,1,0:T(8,128)(2,1)} custom-call(bf16[8,272,128]{2,1,0:T(8,128)(2,1)} %reshape.685.x_ref), custom_call_target="tpu_custom_call" | custom-call | bytes 1114112 | tf_op jit(solution)/shard_map/while/body/eval_jaxpr/pallas_call | solution.py:55
  884.3 14.9 %eval_jaxpr.19 = bf16[8,272,128]{2,1,0:T(8,128)(2,1)} custom-call(bf16[8,272,128]{2,1,0:T(8,128)(2,1)} %reshape.685.x_ref), custom_call_target="tpu_custom_call" | custom-call | bytes 1114112 | tf_op jit(solution)/shard_map/while/body/eval_jaxpr/pallas_call | solution.py:55
  950.7 14.9 %eval_jaxpr.19 = bf16[8,272,128]{2,1,0:T(8,128)(2,1)} custom-call(bf16[8,272,128]{2,1,0:T(8,128)(2,1)} %reshape.685.x_ref), custom_call_target="tpu_custom_call" | custom-call | bytes 1114112 | tf_op jit(solution)/shard_map/while/body/eval_jaxpr/pallas_call | solution.py:55
  1017.4 14.9 %eval_jaxpr.19 = bf16[8,272,128]{2,1,0:T(8,128)(2,1)} custom-call(bf16[8,272,128]{2,1,0:T(8,128)(2,1)} %reshape.685.x_ref), custom_call_target="tpu_custom_call" | custom-call | bytes 1114112 | tf_op jit(solution)/shard_map/while/body/eval_jaxpr/pallas_call | solution.py:55
  1083.9 14.9 %eval_jaxpr.19 = bf16[8,272,128]{2,1,0:T(8,128)(2,1)} custom-call(bf16[8,272,128]{2,1,0:T(8,128)(2,1)} %reshape.685.x_ref), custom_call_target="tpu_custom_call" | custom-call | bytes 1114112 | tf_op jit(solution)/shard_map/while/body/eval_jaxpr/pallas_call | solution.py:55
  1211.3 14.9 %eval_jaxpr.19 = bf16[8,272,128]{2,1,0:T(8,128)(2,1)} custom-call(bf16[8,272,128]{2,1,0:T(8,128)(2,1)} %reshape.685.x_ref), custom_call_target="tpu_custom_call" | custom-call | bytes 1114112 | tf_op jit(solution)/shard_map/while/body/eval_jaxpr/pallas_call | solution.py:55
  1382.9 93.1 %all-reduce.3.cloned.1.call-done = (bf16[1,1,2048,512]{3,2,1,0:T(8,128)(2,1)}, bf16[1,1,512,2048]{3,2,1,0:T(8,128)(2,1)}) async-done(((bf16[1,1,2048,512]{3,2,1,0:T(8,128)(2,1)}, bf16[1,1,512,2048]{3,2,1,0:T(8,128)(2,1)}), (bf16[1,1,2048,512]{3,2,1,0:T(8,128)(2,1)}, bf16[1,1,512,2048]{3,2,1,0:T(8,128)(2,1)})) %all-reduce.3.cloned.1.call-update) | async-done | bytes 4194320 | tf_op jit(solution)/shard_map/psum | solution.py:247
  (1007 shorter events, 1106.2 us)
Async XLA Ops:
  7.2 1468.9 %all-reduce.3.cloned.1.call-start = ((), (), s32[]{:S(2)}) async-start(), calls=%async_computation | async-start | bytes 8388608 | tf_op jit(solution)/shard_map/psum | solution.py:247
  9.1 4.4 copy-start.1
  57.6 12.7 collective-permute-start
  111.7 17.0 %collective-permute-start = (bf16[32,2048]{1,0:T(8,128)(2,1)S(1)}, bf16[32,2048]{1,0:T(8,128)(2,1)S(1)}, u32[]{:S(2)}, u32[]{:S(2)}) collective-permute-start(bf16[32,2048]{1,0:T(8,128)(2,1)S(1)} %fusion.129), channel_id=1, source_target_pairs={{0,32},{32,64},{64,96},{96,128},{128,160},{160,192},{192,224},{1,3... | collective-permute-start | bytes 393224 | tf_op jit(solution)/shard_map/while/body/eval_jaxpr/ppermute | solution.py:21
  170.1 17.1 %collective-permute-start = (bf16[32,2048]{1,0:T(8,128)(2,1)S(1)}, bf16[32,2048]{1,0:T(8,128)(2,1)S(1)}, u32[]{:S(2)}, u32[]{:S(2)}) collective-permute-start(bf16[32,2048]{1,0:T(8,128)(2,1)S(1)} %fusion.129), channel_id=1, source_target_pairs={{0,32},{32,64},{64,96},{96,128},{128,160},{160,192},{192,224},{1,3... | collective-permute-start | bytes 393224 | tf_op jit(solution)/shard_map/while/body/eval_jaxpr/ppermute | solution.py:21
  233.3 12.4 collective-permute-start
  291.8 17.1 %collective-permute-start = (bf16[32,2048]{1,0:T(8,128)(2,1)S(1)}, bf16[32,2048]{1,0:T(8,128)(2,1)S(1)}, u32[]{:S(2)}, u32[]{:S(2)}) collective-permute-start(bf16[32,2048]{1,0:T(8,128)(2,1)S(1)} %fusion.129), channel_id=1, source_target_pairs={{0,32},{32,64},{64,96},{96,128},{128,160},{160,192},{192,224},{1,3... | collective-permute-start | bytes 393224 | tf_op jit(solution)/shard_map/while/body/eval_jaxpr/ppermute | solution.py:21
  355.0 17.2 %collective-permute-start = (bf16[32,2048]{1,0:T(8,128)(2,1)S(1)}, bf16[32,2048]{1,0:T(8,128)(2,1)S(1)}, u32[]{:S(2)}, u32[]{:S(2)}) collective-permute-start(bf16[32,2048]{1,0:T(8,128)(2,1)S(1)} %fusion.129), channel_id=1, source_target_pairs={{0,32},{32,64},{64,96},{96,128},{128,160},{160,192},{192,224},{1,3... | collective-permute-start | bytes 393224 | tf_op jit(solution)/shard_map/while/body/eval_jaxpr/ppermute | solution.py:21
  418.3 17.1 %collective-permute-start = (bf16[32,2048]{1,0:T(8,128)(2,1)S(1)}, bf16[32,2048]{1,0:T(8,128)(2,1)S(1)}, u32[]{:S(2)}, u32[]{:S(2)}) collective-permute-start(bf16[32,2048]{1,0:T(8,128)(2,1)S(1)} %fusion.129), channel_id=1, source_target_pairs={{0,32},{32,64},{64,96},{96,128},{128,160},{160,192},{192,224},{1,3... | collective-permute-start | bytes 393224 | tf_op jit(solution)/shard_map/while/body/eval_jaxpr/ppermute | solution.py:21
  476.8 21.6 %collective-permute-start = (bf16[32,2048]{1,0:T(8,128)(2,1)S(1)}, bf16[32,2048]{1,0:T(8,128)(2,1)S(1)}, u32[]{:S(2)}, u32[]{:S(2)}) collective-permute-start(bf16[32,2048]{1,0:T(8,128)(2,1)S(1)} %fusion.129), channel_id=1, source_target_pairs={{0,32},{32,64},{64,96},{96,128},{128,160},{160,192},{192,224},{1,3... | collective-permute-start | bytes 393224 | tf_op jit(solution)/shard_map/while/body/eval_jaxpr/ppermute | solution.py:21
  539.9 17.0 %collective-permute-start = (bf16[32,2048]{1,0:T(8,128)(2,1)S(1)}, bf16[32,2048]{1,0:T(8,128)(2,1)S(1)}, u32[]{:S(2)}, u32[]{:S(2)}) collective-permute-start(bf16[32,2048]{1,0:T(8,128)(2,1)S(1)} %fusion.129), channel_id=1, source_target_pairs={{0,32},{32,64},{64,96},{96,128},{128,160},{160,192},{192,224},{1,3... | collective-permute-start | bytes 393224 | tf_op jit(solution)/shard_map/while/body/eval_jaxpr/ppermute | solution.py:21
  598.3 17.1 %collective-permute-start = (bf16[32,2048]{1,0:T(8,128)(2,1)S(1)}, bf16[32,2048]{1,0:T(8,128)(2,1)S(1)}, u32[]{:S(2)}, u32[]{:S(2)}) collective-permute-start(bf16[32,2048]{1,0:T(8,128)(2,1)S(1)} %fusion.129), channel_id=1, source_target_pairs={{0,32},{32,64},{64,96},{96,128},{128,160},{160,192},{192,224},{1,3... | collective-permute-start | bytes 393224 | tf_op jit(solution)/shard_map/while/body/eval_jaxpr/ppermute | solution.py:21
  656.8 17.1 %collective-permute-start = (bf16[32,2048]{1,0:T(8,128)(2,1)S(1)}, bf16[32,2048]{1,0:T(8,128)(2,1)S(1)}, u32[]{:S(2)}, u32[]{:S(2)}) collective-permute-start(bf16[32,2048]{1,0:T(8,128)(2,1)S(1)} %fusion.129), channel_id=1, source_target_pairs={{0,32},{32,64},{64,96},{96,128},{128,160},{160,192},{192,224},{1,3... | collective-permute-start | bytes 393224 | tf_op jit(solution)/shard_map/while/body/eval_jaxpr/ppermute | solution.py:21
  722.5 17.6 %collective-permute-start.1 = (bf16[32,2048]{1,0:T(8,128)(2,1)S(1)}, bf16[32,2048]{1,0:T(8,128)(2,1)S(1)}, u32[]{:S(2)}, u32[]{:S(2)}) collective-permute-start(bf16[32,2048]{1,0:T(8,128)(2,1)S(1)} %fusion.140), channel_id=1, source_target_pairs={{32,0},{64,32},{96,64},{128,96},{160,128},{192,160},{224,192},{33,... | collective-permute-start | bytes 393224 | tf_op jit(solution)/shard_map/while/body/eval_jaxpr/ppermute | solution.py:21
  784.1 17.0 %collective-permute-start.1 = (bf16[32,2048]{1,0:T(8,128)(2,1)S(1)}, bf16[32,2048]{1,0:T(8,128)(2,1)S(1)}, u32[]{:S(2)}, u32[]{:S(2)}) collective-permute-start(bf16[32,2048]{1,0:T(8,128)(2,1)S(1)} %fusion.140), channel_id=1, source_target_pairs={{32,0},{64,32},{96,64},{128,96},{160,128},{192,160},{224,192},{33,... | collective-permute-start | bytes 393224 | tf_op jit(solution)/shard_map/while/body/eval_jaxpr/ppermute | solution.py:21
  845.0 17.0 %collective-permute-start.1 = (bf16[32,2048]{1,0:T(8,128)(2,1)S(1)}, bf16[32,2048]{1,0:T(8,128)(2,1)S(1)}, u32[]{:S(2)}, u32[]{:S(2)}) collective-permute-start(bf16[32,2048]{1,0:T(8,128)(2,1)S(1)} %fusion.140), channel_id=1, source_target_pairs={{32,0},{64,32},{96,64},{128,96},{160,128},{192,160},{224,192},{33,... | collective-permute-start | bytes 393224 | tf_op jit(solution)/shard_map/while/body/eval_jaxpr/ppermute | solution.py:21
  905.9 17.0 %collective-permute-start.1 = (bf16[32,2048]{1,0:T(8,128)(2,1)S(1)}, bf16[32,2048]{1,0:T(8,128)(2,1)S(1)}, u32[]{:S(2)}, u32[]{:S(2)}) collective-permute-start(bf16[32,2048]{1,0:T(8,128)(2,1)S(1)} %fusion.140), channel_id=1, source_target_pairs={{32,0},{64,32},{96,64},{128,96},{160,128},{192,160},{224,192},{33,... | collective-permute-start | bytes 393224 | tf_op jit(solution)/shard_map/while/body/eval_jaxpr/ppermute | solution.py:21
  972.4 17.2 %collective-permute-start.1 = (bf16[32,2048]{1,0:T(8,128)(2,1)S(1)}, bf16[32,2048]{1,0:T(8,128)(2,1)S(1)}, u32[]{:S(2)}, u32[]{:S(2)}) collective-permute-start(bf16[32,2048]{1,0:T(8,128)(2,1)S(1)} %fusion.140), channel_id=1, source_target_pairs={{32,0},{64,32},{96,64},{128,96},{160,128},{192,160},{224,192},{33,... | collective-permute-start | bytes 393224 | tf_op jit(solution)/shard_map/while/body/eval_jaxpr/ppermute | solution.py:21
  1039.0 17.1 %collective-permute-start.1 = (bf16[32,2048]{1,0:T(8,128)(2,1)S(1)}, bf16[32,2048]{1,0:T(8,128)(2,1)S(1)}, u32[]{:S(2)}, u32[]{:S(2)}) collective-permute-start(bf16[32,2048]{1,0:T(8,128)(2,1)S(1)} %fusion.140), channel_id=1, source_target_pairs={{32,0},{64,32},{96,64},{128,96},{160,128},{192,160},{224,192},{33,... | collective-permute-start | bytes 393224 | tf_op jit(solution)/shard_map/while/body/eval_jaxpr/ppermute | solution.py:21
  1105.6 17.0 %collective-permute-start.1 = (bf16[32,2048]{1,0:T(8,128)(2,1)S(1)}, bf16[32,2048]{1,0:T(8,128)(2,1)S(1)}, u32[]{:S(2)}, u32[]{:S(2)}) collective-permute-start(bf16[32,2048]{1,0:T(8,128)(2,1)S(1)} %fusion.140), channel_id=1, source_target_pairs={{32,0},{64,32},{96,64},{128,96},{160,128},{192,160},{224,192},{33,... | collective-permute-start | bytes 393224 | tf_op jit(solution)/shard_map/while/body/eval_jaxpr/ppermute | solution.py:21
  1172.0 17.0 %collective-permute-start.1 = (bf16[32,2048]{1,0:T(8,128)(2,1)S(1)}, bf16[32,2048]{1,0:T(8,128)(2,1)S(1)}, u32[]{:S(2)}, u32[]{:S(2)}) collective-permute-start(bf16[32,2048]{1,0:T(8,128)(2,1)S(1)} %fusion.140), channel_id=1, source_target_pairs={{32,0},{64,32},{96,64},{128,96},{160,128},{192,160},{224,192},{33,... | collective-permute-start | bytes 393224 | tf_op jit(solution)/shard_map/while/body/eval_jaxpr/ppermute | solution.py:21
  1233.0 17.1 %collective-permute-start.1 = (bf16[32,2048]{1,0:T(8,128)(2,1)S(1)}, bf16[32,2048]{1,0:T(8,128)(2,1)S(1)}, u32[]{:S(2)}, u32[]{:S(2)}) collective-permute-start(bf16[32,2048]{1,0:T(8,128)(2,1)S(1)} %fusion.140), channel_id=1, source_target_pairs={{32,0},{64,32},{96,64},{128,96},{160,128},{192,160},{224,192},{33,... | collective-permute-start | bytes 393224 | tf_op jit(solution)/shard_map/while/body/eval_jaxpr/ppermute | solution.py:21
  1294.0 17.1 %collective-permute-start.1 = (bf16[32,2048]{1,0:T(8,128)(2,1)S(1)}, bf16[32,2048]{1,0:T(8,128)(2,1)S(1)}, u32[]{:S(2)}, u32[]{:S(2)}) collective-permute-start(bf16[32,2048]{1,0:T(8,128)(2,1)S(1)} %fusion.140), channel_id=1, source_target_pairs={{32,0},{64,32},{96,64},{128,96},{160,128},{192,160},{224,192},{33,... | collective-permute-start | bytes 393224 | tf_op jit(solution)/shard_map/while/body/eval_jaxpr/ppermute | solution.py:21
  1355.1 17.0 %collective-permute-start.1 = (bf16[32,2048]{1,0:T(8,128)(2,1)S(1)}, bf16[32,2048]{1,0:T(8,128)(2,1)S(1)}, u32[]{:S(2)}, u32[]{:S(2)}) collective-permute-start(bf16[32,2048]{1,0:T(8,128)(2,1)S(1)} %fusion.140), channel_id=1, source_target_pairs={{32,0},{64,32},{96,64},{128,96},{160,128},{192,160},{224,192},{33,... | collective-permute-start | bytes 393224 | tf_op jit(solution)/shard_map/while/body/eval_jaxpr/ppermute | solution.py:21
  (2 other events, 7.6 us)
Sparse Core Ops, SparseCore 0:
  1383.0 92.9 all-reduce.2

commit v7 on v6

--- a/solution.py
+++ b/solution.py
@@ -65,6 +65,30 @@
         compiler_params=pltpu.CompilerParams(collective_id=site, has_side_effects=True),
         cost_estimate=pl.CostEstimate(flops=0, bytes_accessed=2 * nbytes, transcendentals=0),
     )(block)
+
+
+def ring_sum(flat, axis):
+    count = lax.axis_size(axis)
+    me = lax.axis_index(axis)
+    halves = flat.reshape(2, count, -1, 128)
+    results = []
+    for half, way in ((0, 1), (1, -1)):
+        own = halves[half]
+        route = [(i, (i + way) % count) for i in range(count)]
+        send = lax.dynamic_index_in_dim(own, me, 0, keepdims=False).astype(jnp.bfloat16)
+        for step in range(count - 1):
+            got = lax.ppermute(send, axis, route)
+            chunk = lax.rem(me - way * (1 + step) + 2 * count, count)
+            part = lax.dynamic_index_in_dim(own, chunk, 0, keepdims=False)
+            send = (got.astype(jnp.float32) + part).astype(jnp.bfloat16)
+        out = jnp.zeros(own.shape, jnp.bfloat16)
+        out = lax.dynamic_update_index_in_dim(out, send, lax.rem(me + way + count, count), 0)
+        for step in range(count - 1):
+            send = lax.ppermute(send, axis, route)
+            chunk = lax.rem(me - way * step + 2 * count, count)
+            out = lax.dynamic_update_index_in_dim(out, send, chunk, 0)
+        results.append(out.reshape(-1))
+    return jnp.concatenate(results)
 
 
 def normalize(section_in):
@@ -244,11 +268,12 @@
     acc_up = jnp.einsum(
         "bsecd,bsech->edh", received_live, dpre_live, preferred_element_type=jnp.float32
     )
-    sum_up = lax.psum(acc_up.astype(jnp.bfloat16), "dp")
     acc_down = jnp.einsum(
         "bsech,bsecd->ehd", hidden_live, dreceived_live, preferred_element_type=jnp.float32
     )
-    sum_down = lax.psum(acc_down.astype(jnp.bfloat16), "dp")
+    summed = ring_sum(jnp.concatenate([acc_up.reshape(-1), acc_down.reshape(-1)]), "dp")
+    sum_up = summed[: acc_up.size].reshape(acc_up.shape)
+    sum_down = summed[acc_up.size :].reshape(acc_down.shape)
     up_out = sum_up.astype(jnp.bfloat16)
     down_out = sum_down.astype(jnp.bfloat16)
     return (up_out[None], down_out[None])

time: 1500 us -> 1490 us (level)
  waiting for transfers between devices: 255 us -> 206 us
  starting transfers between devices: 132 us -> 155 us
  local copies, waits for them, and re-layouts: 241 us -> 261 us
    psum x1 -> x0, waiting for transfers between devices: 93.1 us -> none  [local(): sum_up = lax.psum(acc_up.astype(jnp.bfloat16), 'dp')]
    ppermute x0 -> x12, waiting for transfers between devices: none -> 43.7 us  [the longest x6 25.2 us: ring_sum(): got = lax.ppermute(send, axis, route)]
    ppermute x0 -> x12, starting transfers between devices: none -> 22.4 us  [the longest x6 11.2 us: ring_sum(): send = lax.ppermute(send, axis, route)]
  transfers between devices with their start and end apart: 23 -> 34, of which waited for: 23 -> 28; matrix products, arithmetic and copies ran while one was open for 5% -> 7% of each run, Pallas kernels for 0% -> 0%
where the time goes in v7:
time: 1490 us; the launch traced here: 1480 us
  Pallas kernels  646 us (43%)
  local copies, waits for them, and re-layouts  261 us (18%)
  waiting for transfers between devices  206 us (14%)
  starting transfers between devices  155 us (10%)
  other arithmetic  116 us (8%)
  matrix products  73.7 us (5%)
  loops' own time  19.4 us (1%)
    pallas_call x44, Pallas kernels, expert_exchange(): pl.pallas_call(functools.partial(exchange_kernel, n), out_shape=jax.Shape...  646 us
    ppermute x22, waiting for transfers between devices, from_behind(): return lax.ppermute(block, axis, route)  162 us
    ppermute x22, starting transfers between devices, from_behind(): return lax.ppermute(block, axis, route)  132 us
    dynamic_update_slice x44, local copies, waits for them, and re-layouts, local(): _, saved = lax.scan(forward_step, start_act, jnp.arange(step_count))  52.2 us
    gather x22, local copies, waits for them, and re-layouts, from_buffer(): buffer.reshape(experts_all * capacity, pieces, lanes)[dest_rows]  38.7 us
  transfers between devices with their start and end apart: 34, of which 28 were waited for; matrix products, arithmetic and copies ran while one was open for 7% of the time, Pallas kernels for 0%

profile of v7, /device:TPU:62, one launch (start us, length us, event | category | flops | bytes accessed | tf_op | source)
XLA Modules:
  0.0 1477.7 jit_solution(4600838990355104625)
XLA Ops:
  7.0 660.2 %while.39 = (s32[]{:T(128)}, bf16[32,2048]{1,0:T(8,128)(2,1)S(1)}, bf16[11,32,2048]{2,1,0:T(8,128)(2,1)}, f32[11,32,4]{1,2,0:T(4,128)S(1)}, bf16[11,32,4,2048]{3...) while((s32[]{:T(128)}, bf16[32,2048]{1,0:T(8,128)(2,1)S(1)}, ...), condition=%wide.region_9.10_spmd, body=%wide.region_3.9_spmd.sunk | while | flops 573976576 | bytes 24260048 | solution.py:192
  12.4 16.2 %eval_jaxpr.16 = bf16[8,272,128]{2,1,0:T(8,128)(2,1)S(1)} custom-call(bf16[8,272,128]{2,1,0:T(8,128)(2,1)} %bitcast_select_fusion.8.x_ref), custom_call_target="tpu_custom_call" | custom-call | bytes 1114112 | tf_op jit(solution)/shard_map/while/body/eval_jaxpr/pallas_call | solution.py:55
  30.7 15.7 %eval_jaxpr.17 = bf16[8,272,128]{2,1,0:T(8,128)(2,1)} custom-call(bf16[8,272,128]{2,1,0:T(8,128)(2,1)} %reshape.686.x_ref), custom_call_target="tpu_custom_call" | custom-call | bytes 1114112 | tf_op jit(solution)/shard_map/while/body/eval_jaxpr/pallas_call | solution.py:55
  85.5 14.9 %eval_jaxpr.17 = bf16[8,272,128]{2,1,0:T(8,128)(2,1)} custom-call(bf16[8,272,128]{2,1,0:T(8,128)(2,1)} %reshape.686.x_ref), custom_call_target="tpu_custom_call" | custom-call | bytes 1114112 | tf_op jit(solution)/shard_map/while/body/eval_jaxpr/pallas_call | solution.py:55
  143.9 14.9 %eval_jaxpr.17 = bf16[8,272,128]{2,1,0:T(8,128)(2,1)} custom-call(bf16[8,272,128]{2,1,0:T(8,128)(2,1)} %reshape.686.x_ref), custom_call_target="tpu_custom_call" | custom-call | bytes 1114112 | tf_op jit(solution)/shard_map/while/body/eval_jaxpr/pallas_call | solution.py:55
  207.1 14.9 %eval_jaxpr.17 = bf16[8,272,128]{2,1,0:T(8,128)(2,1)} custom-call(bf16[8,272,128]{2,1,0:T(8,128)(2,1)} %reshape.686.x_ref), custom_call_target="tpu_custom_call" | custom-call | bytes 1114112 | tf_op jit(solution)/shard_map/while/body/eval_jaxpr/pallas_call | solution.py:55
  265.6 14.9 %eval_jaxpr.17 = bf16[8,272,128]{2,1,0:T(8,128)(2,1)} custom-call(bf16[8,272,128]{2,1,0:T(8,128)(2,1)} %reshape.686.x_ref), custom_call_target="tpu_custom_call" | custom-call | bytes 1114112 | tf_op jit(solution)/shard_map/while/body/eval_jaxpr/pallas_call | solution.py:55
  328.7 14.9 %eval_jaxpr.17 = bf16[8,272,128]{2,1,0:T(8,128)(2,1)} custom-call(bf16[8,272,128]{2,1,0:T(8,128)(2,1)} %reshape.686.x_ref), custom_call_target="tpu_custom_call" | custom-call | bytes 1114112 | tf_op jit(solution)/shard_map/while/body/eval_jaxpr/pallas_call | solution.py:55
  392.0 14.9 %eval_jaxpr.17 = bf16[8,272,128]{2,1,0:T(8,128)(2,1)} custom-call(bf16[8,272,128]{2,1,0:T(8,128)(2,1)} %reshape.686.x_ref), custom_call_target="tpu_custom_call" | custom-call | bytes 1114112 | tf_op jit(solution)/shard_map/while/body/eval_jaxpr/pallas_call | solution.py:55
  450.5 14.9 %eval_jaxpr.17 = bf16[8,272,128]{2,1,0:T(8,128)(2,1)} custom-call(bf16[8,272,128]{2,1,0:T(8,128)(2,1)} %reshape.686.x_ref), custom_call_target="tpu_custom_call" | custom-call | bytes 1114112 | tf_op jit(solution)/shard_map/while/body/eval_jaxpr/pallas_call | solution.py:55
  470.1 15.1 %collective-permute-start = (bf16[32,2048]{1,0:T(8,128)(2,1)S(1)}, bf16[32,2048]{1,0:T(8,128)(2,1)S(1)}, u32[]{:S(2)}, u32[]{:S(2)}) collective-permute-start(bf16[32,2048]{1,0:T(8,128)(2,1)S(1)} %fusion.133), channel_id=1, source_target_pairs={{0,32},{32,64},{64,96},{96,128},{128,160},{160,192},{192,224},{1,3... | collective-permute-start | bytes 393224 | tf_op jit(solution)/shard_map/while/body/eval_jaxpr/ppermute | solution.py:21
  513.6 14.9 %eval_jaxpr.17 = bf16[8,272,128]{2,1,0:T(8,128)(2,1)} custom-call(bf16[8,272,128]{2,1,0:T(8,128)(2,1)} %reshape.686.x_ref), custom_call_target="tpu_custom_call" | custom-call | bytes 1114112 | tf_op jit(solution)/shard_map/while/body/eval_jaxpr/pallas_call | solution.py:55
  572.0 14.9 %eval_jaxpr.17 = bf16[8,272,128]{2,1,0:T(8,128)(2,1)} custom-call(bf16[8,272,128]{2,1,0:T(8,128)(2,1)} %reshape.686.x_ref), custom_call_target="tpu_custom_call" | custom-call | bytes 1114112 | tf_op jit(solution)/shard_map/while/body/eval_jaxpr/pallas_call | solution.py:55
  630.5 14.9 %eval_jaxpr.17 = bf16[8,272,128]{2,1,0:T(8,128)(2,1)} custom-call(bf16[8,272,128]{2,1,0:T(8,128)(2,1)} %reshape.686.x_ref), custom_call_target="tpu_custom_call" | custom-call | bytes 1114112 | tf_op jit(solution)/shard_map/while/body/eval_jaxpr/pallas_call | solution.py:55
  671.6 693.3 %while.40 = (s32[]{:T(128)}, bf16[32,2048]{1,0:T(8,128)(2,1)S(1)}, bf16[11,8,1,17,512]{4,3,1,2,0:T(8,128)(2,1)}, bf16[11,8,1,17,2048]{4,3,1,2,0:T(8,128)(2,1)}, ...) while((s32[]{:T(128)}, bf16[32,2048]{1,0:T(8,128)(2,1)S(1)}, ...), condition=%wide.region_20.21_spmd.clone, body=%wide.region_10.20_spmd.clone.sunk | while | flops 581163648 | bytes 27663032 | solution.py:261
  694.1 14.9 %eval_jaxpr.19 = bf16[8,272,128]{2,1,0:T(8,128)(2,1)} custom-call(bf16[8,272,128]{2,1,0:T(8,128)(2,1)} %reshape.694.x_ref), custom_call_target="tpu_custom_call" | custom-call | bytes 1114112 | tf_op jit(solution)/shard_map/while/body/eval_jaxpr/pallas_call | solution.py:55
  755.6 14.9 %eval_jaxpr.19 = bf16[8,272,128]{2,1,0:T(8,128)(2,1)} custom-call(bf16[8,272,128]{2,1,0:T(8,128)(2,1)} %reshape.694.x_ref), custom_call_target="tpu_custom_call" | custom-call | bytes 1114112 | tf_op jit(solution)/shard_map/while/body/eval_jaxpr/pallas_call | solution.py:55
  816.5 14.9 %eval_jaxpr.19 = bf16[8,272,128]{2,1,0:T(8,128)(2,1)} custom-call(bf16[8,272,128]{2,1,0:T(8,128)(2,1)} %reshape.694.x_ref), custom_call_target="tpu_custom_call" | custom-call | bytes 1114112 | tf_op jit(solution)/shard_map/while/body/eval_jaxpr/pallas_call | solution.py:55
  877.4 14.9 %eval_jaxpr.19 = bf16[8,272,128]{2,1,0:T(8,128)(2,1)} custom-call(bf16[8,272,128]{2,1,0:T(8,128)(2,1)} %reshape.694.x_ref), custom_call_target="tpu_custom_call" | custom-call | bytes 1114112 | tf_op jit(solution)/shard_map/while/body/eval_jaxpr/pallas_call | solution.py:55
  943.8 14.9 %eval_jaxpr.19 = bf16[8,272,128]{2,1,0:T(8,128)(2,1)} custom-call(bf16[8,272,128]{2,1,0:T(8,128)(2,1)} %reshape.694.x_ref), custom_call_target="tpu_custom_call" | custom-call | bytes 1114112 | tf_op jit(solution)/shard_map/while/body/eval_jaxpr/pallas_call | solution.py:55
  1010.4 14.9 %eval_jaxpr.19 = bf16[8,272,128]{2,1,0:T(8,128)(2,1)} custom-call(bf16[8,272,128]{2,1,0:T(8,128)(2,1)} %reshape.694.x_ref), custom_call_target="tpu_custom_call" | custom-call | bytes 1114112 | tf_op jit(solution)/shard_map/while/body/eval_jaxpr/pallas_call | solution.py:55
  1143.4 14.9 %eval_jaxpr.19 = bf16[8,272,128]{2,1,0:T(8,128)(2,1)} custom-call(bf16[8,272,128]{2,1,0:T(8,128)(2,1)} %reshape.694.x_ref), custom_call_target="tpu_custom_call" | custom-call | bytes 1114112 | tf_op jit(solution)/shard_map/while/body/eval_jaxpr/pallas_call | solution.py:55
  1204.3 14.9 %eval_jaxpr.19 = bf16[8,272,128]{2,1,0:T(8,128)(2,1)} custom-call(bf16[8,272,128]{2,1,0:T(8,128)(2,1)} %reshape.694.x_ref), custom_call_target="tpu_custom_call" | custom-call | bytes 1114112 | tf_op jit(solution)/shard_map/while/body/eval_jaxpr/pallas_call | solution.py:55
  1265.3 14.9 %eval_jaxpr.19 = bf16[8,272,128]{2,1,0:T(8,128)(2,1)} custom-call(bf16[8,272,128]{2,1,0:T(8,128)(2,1)} %reshape.694.x_ref), custom_call_target="tpu_custom_call" | custom-call | bytes 1114112 | tf_op jit(solution)/shard_map/while/body/eval_jaxpr/pallas_call | solution.py:55
  (1044 shorter events, 1188.0 us)
Async XLA Ops:
  105.1 17.0 %collective-permute-start = (bf16[32,2048]{1,0:T(8,128)(2,1)S(1)}, bf16[32,2048]{1,0:T(8,128)(2,1)S(1)}, u32[]{:S(2)}, u32[]{:S(2)}) collective-permute-start(bf16[32,2048]{1,0:T(8,128)(2,1)S(1)} %fusion.133), channel_id=1, source_target_pairs={{0,32},{32,64},{64,96},{96,128},{128,160},{160,192},{192,224},{1,3... | collective-permute-start | bytes 393224 | tf_op jit(solution)/shard_map/while/body/eval_jaxpr/ppermute | solution.py:21
  163.5 17.1 %collective-permute-start = (bf16[32,2048]{1,0:T(8,128)(2,1)S(1)}, bf16[32,2048]{1,0:T(8,128)(2,1)S(1)}, u32[]{:S(2)}, u32[]{:S(2)}) collective-permute-start(bf16[32,2048]{1,0:T(8,128)(2,1)S(1)} %fusion.133), channel_id=1, source_target_pairs={{0,32},{32,64},{64,96},{96,128},{128,160},{160,192},{192,224},{1,3... | collective-permute-start | bytes 393224 | tf_op jit(solution)/shard_map/while/body/eval_jaxpr/ppermute | solution.py:21
  285.2 17.1 %collective-permute-start = (bf16[32,2048]{1,0:T(8,128)(2,1)S(1)}, bf16[32,2048]{1,0:T(8,128)(2,1)S(1)}, u32[]{:S(2)}, u32[]{:S(2)}) collective-permute-start(bf16[32,2048]{1,0:T(8,128)(2,1)S(1)} %fusion.133), channel_id=1, source_target_pairs={{0,32},{32,64},{64,96},{96,128},{128,160},{160,192},{192,224},{1,3... | collective-permute-start | bytes 393224 | tf_op jit(solution)/shard_map/while/body/eval_jaxpr/ppermute | solution.py:21
  348.3 17.2 %collective-permute-start = (bf16[32,2048]{1,0:T(8,128)(2,1)S(1)}, bf16[32,2048]{1,0:T(8,128)(2,1)S(1)}, u32[]{:S(2)}, u32[]{:S(2)}) collective-permute-start(bf16[32,2048]{1,0:T(8,128)(2,1)S(1)} %fusion.133), channel_id=1, source_target_pairs={{0,32},{32,64},{64,96},{96,128},{128,160},{160,192},{192,224},{1,3... | collective-permute-start | bytes 393224 | tf_op jit(solution)/shard_map/while/body/eval_jaxpr/ppermute | solution.py:21
  411.6 17.1 %collective-permute-start = (bf16[32,2048]{1,0:T(8,128)(2,1)S(1)}, bf16[32,2048]{1,0:T(8,128)(2,1)S(1)}, u32[]{:S(2)}, u32[]{:S(2)}) collective-permute-start(bf16[32,2048]{1,0:T(8,128)(2,1)S(1)} %fusion.133), channel_id=1, source_target_pairs={{0,32},{32,64},{64,96},{96,128},{128,160},{160,192},{192,224},{1,3... | collective-permute-start | bytes 393224 | tf_op jit(solution)/shard_map/while/body/eval_jaxpr/ppermute | solution.py:21
  470.1 21.7 %collective-permute-start = (bf16[32,2048]{1,0:T(8,128)(2,1)S(1)}, bf16[32,2048]{1,0:T(8,128)(2,1)S(1)}, u32[]{:S(2)}, u32[]{:S(2)}) collective-permute-start(bf16[32,2048]{1,0:T(8,128)(2,1)S(1)} %fusion.133), channel_id=1, source_target_pairs={{0,32},{32,64},{64,96},{96,128},{128,160},{160,192},{192,224},{1,3... | collective-permute-start | bytes 393224 | tf_op jit(solution)/shard_map/while/body/eval_jaxpr/ppermute | solution.py:21
  533.2 17.0 %collective-permute-start = (bf16[32,2048]{1,0:T(8,128)(2,1)S(1)}, bf16[32,2048]{1,0:T(8,128)(2,1)S(1)}, u32[]{:S(2)}, u32[]{:S(2)}) collective-permute-start(bf16[32,2048]{1,0:T(8,128)(2,1)S(1)} %fusion.133), channel_id=1, source_target_pairs={{0,32},{32,64},{64,96},{96,128},{128,160},{160,192},{192,224},{1,3... | collective-permute-start | bytes 393224 | tf_op jit(solution)/shard_map/while/body/eval_jaxpr/ppermute | solution.py:21
  591.6 17.1 %collective-permute-start = (bf16[32,2048]{1,0:T(8,128)(2,1)S(1)}, bf16[32,2048]{1,0:T(8,128)(2,1)S(1)}, u32[]{:S(2)}, u32[]{:S(2)}) collective-permute-start(bf16[32,2048]{1,0:T(8,128)(2,1)S(1)} %fusion.133), channel_id=1, source_target_pairs={{0,32},{32,64},{64,96},{96,128},{128,160},{160,192},{192,224},{1,3... | collective-permute-start | bytes 393224 | tf_op jit(solution)/shard_map/while/body/eval_jaxpr/ppermute | solution.py:21
  650.1 17.1 %collective-permute-start = (bf16[32,2048]{1,0:T(8,128)(2,1)S(1)}, bf16[32,2048]{1,0:T(8,128)(2,1)S(1)}, u32[]{:S(2)}, u32[]{:S(2)}) collective-permute-start(bf16[32,2048]{1,0:T(8,128)(2,1)S(1)} %fusion.133), channel_id=1, source_target_pairs={{0,32},{32,64},{64,96},{96,128},{128,160},{160,192},{192,224},{1,3... | collective-permute-start | bytes 393224 | tf_op jit(solution)/shard_map/while/body/eval_jaxpr/ppermute | solution.py:21
  715.7 17.6 %collective-permute-start.1 = (bf16[32,2048]{1,0:T(8,128)(2,1)S(1)}, bf16[32,2048]{1,0:T(8,128)(2,1)S(1)}, u32[]{:S(2)}, u32[]{:S(2)}) collective-permute-start(bf16[32,2048]{1,0:T(8,128)(2,1)S(1)} %fusion.144), channel_id=1, source_target_pairs={{32,0},{64,32},{96,64},{128,96},{160,128},{192,160},{224,192},{33,... | collective-permute-start | bytes 393224 | tf_op jit(solution)/shard_map/while/body/eval_jaxpr/ppermute | solution.py:21
  777.2 17.0 %collective-permute-start.1 = (bf16[32,2048]{1,0:T(8,128)(2,1)S(1)}, bf16[32,2048]{1,0:T(8,128)(2,1)S(1)}, u32[]{:S(2)}, u32[]{:S(2)}) collective-permute-start(bf16[32,2048]{1,0:T(8,128)(2,1)S(1)} %fusion.144), channel_id=1, source_target_pairs={{32,0},{64,32},{96,64},{128,96},{160,128},{192,160},{224,192},{33,... | collective-permute-start | bytes 393224 | tf_op jit(solution)/shard_map/while/body/eval_jaxpr/ppermute | solution.py:21
  838.1 17.0 %collective-permute-start.1 = (bf16[32,2048]{1,0:T(8,128)(2,1)S(1)}, bf16[32,2048]{1,0:T(8,128)(2,1)S(1)}, u32[]{:S(2)}, u32[]{:S(2)}) collective-permute-start(bf16[32,2048]{1,0:T(8,128)(2,1)S(1)} %fusion.144), channel_id=1, source_target_pairs={{32,0},{64,32},{96,64},{128,96},{160,128},{192,160},{224,192},{33,... | collective-permute-start | bytes 393224 | tf_op jit(solution)/shard_map/while/body/eval_jaxpr/ppermute | solution.py:21
  899.0 17.0 %collective-permute-start.1 = (bf16[32,2048]{1,0:T(8,128)(2,1)S(1)}, bf16[32,2048]{1,0:T(8,128)(2,1)S(1)}, u32[]{:S(2)}, u32[]{:S(2)}) collective-permute-start(bf16[32,2048]{1,0:T(8,128)(2,1)S(1)} %fusion.144), channel_id=1, source_target_pairs={{32,0},{64,32},{96,64},{128,96},{160,128},{192,160},{224,192},{33,... | collective-permute-start | bytes 393224 | tf_op jit(solution)/shard_map/while/body/eval_jaxpr/ppermute | solution.py:21
  965.4 17.2 %collective-permute-start.1 = (bf16[32,2048]{1,0:T(8,128)(2,1)S(1)}, bf16[32,2048]{1,0:T(8,128)(2,1)S(1)}, u32[]{:S(2)}, u32[]{:S(2)}) collective-permute-start(bf16[32,2048]{1,0:T(8,128)(2,1)S(1)} %fusion.144), channel_id=1, source_target_pairs={{32,0},{64,32},{96,64},{128,96},{160,128},{192,160},{224,192},{33,... | collective-permute-start | bytes 393224 | tf_op jit(solution)/shard_map/while/body/eval_jaxpr/ppermute | solution.py:21
  1032.1 17.1 %collective-permute-start.1 = (bf16[32,2048]{1,0:T(8,128)(2,1)S(1)}, bf16[32,2048]{1,0:T(8,128)(2,1)S(1)}, u32[]{:S(2)}, u32[]{:S(2)}) collective-permute-start(bf16[32,2048]{1,0:T(8,128)(2,1)S(1)} %fusion.144), channel_id=1, source_target_pairs={{32,0},{64,32},{96,64},{128,96},{160,128},{192,160},{224,192},{33,... | collective-permute-start | bytes 393224 | tf_op jit(solution)/shard_map/while/body/eval_jaxpr/ppermute | solution.py:21
  1098.6 17.0 %collective-permute-start.1 = (bf16[32,2048]{1,0:T(8,128)(2,1)S(1)}, bf16[32,2048]{1,0:T(8,128)(2,1)S(1)}, u32[]{:S(2)}, u32[]{:S(2)}) collective-permute-start(bf16[32,2048]{1,0:T(8,128)(2,1)S(1)} %fusion.144), channel_id=1, source_target_pairs={{32,0},{64,32},{96,64},{128,96},{160,128},{192,160},{224,192},{33,... | collective-permute-start | bytes 393224 | tf_op jit(solution)/shard_map/while/body/eval_jaxpr/ppermute | solution.py:21
  1165.0 17.0 %collective-permute-start.1 = (bf16[32,2048]{1,0:T(8,128)(2,1)S(1)}, bf16[32,2048]{1,0:T(8,128)(2,1)S(1)}, u32[]{:S(2)}, u32[]{:S(2)}) collective-permute-start(bf16[32,2048]{1,0:T(8,128)(2,1)S(1)} %fusion.144), channel_id=1, source_target_pairs={{32,0},{64,32},{96,64},{128,96},{160,128},{192,160},{224,192},{33,... | collective-permute-start | bytes 393224 | tf_op jit(solution)/shard_map/while/body/eval_jaxpr/ppermute | solution.py:21
  1225.9 17.1 %collective-permute-start.1 = (bf16[32,2048]{1,0:T(8,128)(2,1)S(1)}, bf16[32,2048]{1,0:T(8,128)(2,1)S(1)}, u32[]{:S(2)}, u32[]{:S(2)}) collective-permute-start(bf16[32,2048]{1,0:T(8,128)(2,1)S(1)} %fusion.144), channel_id=1, source_target_pairs={{32,0},{64,32},{96,64},{128,96},{160,128},{192,160},{224,192},{33,... | collective-permute-start | bytes 393224 | tf_op jit(solution)/shard_map/while/body/eval_jaxpr/ppermute | solution.py:21
  1286.9 17.1 %collective-permute-start.1 = (bf16[32,2048]{1,0:T(8,128)(2,1)S(1)}, bf16[32,2048]{1,0:T(8,128)(2,1)S(1)}, u32[]{:S(2)}, u32[]{:S(2)}) collective-permute-start(bf16[32,2048]{1,0:T(8,128)(2,1)S(1)} %fusion.144), channel_id=1, source_target_pairs={{32,0},{64,32},{96,64},{128,96},{160,128},{192,160},{224,192},{33,... | collective-permute-start | bytes 393224 | tf_op jit(solution)/shard_map/while/body/eval_jaxpr/ppermute | solution.py:21
  1347.9 17.0 %collective-permute-start.1 = (bf16[32,2048]{1,0:T(8,128)(2,1)S(1)}, bf16[32,2048]{1,0:T(8,128)(2,1)S(1)}, u32[]{:S(2)}, u32[]{:S(2)}) collective-permute-start(bf16[32,2048]{1,0:T(8,128)(2,1)S(1)} %fusion.144), channel_id=1, source_target_pairs={{32,0},{64,32},{96,64},{128,96},{160,128},{192,160},{224,192},{33,... | collective-permute-start | bytes 393224 | tf_op jit(solution)/shard_map/while/body/eval_jaxpr/ppermute | solution.py:21
  1377.3 15.4 %collective-permute-start.8 = (bf16[2048,128]{1,0:T(8,128)(2,1)S(1)}, bf16[2048,128]{1,0:T(8,128)(2,1)S(1)}, u32[]{:S(2)}, u32[]{:S(2)}) collective-permute-start(bf16[2048,128]{1,0:T(8,128)(2,1)S(1)} %fusion.91), channel_id=1, source_target_pairs={{0,24},{8,0},{16,8},{24,16},{1,25},{9,1},{17,9},{25,17},{2,26},{10... | collective-permute-start | bytes 1572872 | tf_op jit(solution)/shard_map/ppermute | solution.py:80
  1394.1 14.8 %collective-permute-start.9 = (bf16[2048,128]{1,0:T(8,128)(2,1)S(1)}, bf16[2048,128]{1,0:T(8,128)(2,1)S(1)}, u32[]{:S(2)}, u32[]{:S(2)}) collective-permute-start(bf16[2048,128]{1,0:T(8,128)(2,1)S(1)} %fusion.79), channel_id=1, source_target_pairs={{0,24},{8,0},{16,8},{24,16},{1,25},{9,1},{17,9},{25,17},{2,26},{10... | collective-permute-start | bytes 1572872 | tf_op jit(solution)/shard_map/ppermute | solution.py:80
  1410.3 13.9 collective-permute-start.10
  1426.7 14.6 collective-permute-start.11
  (12 other events, 135.6 us)

commit v8 on v7

--- a/solution.py
+++ b/solution.py
@@ -70,7 +70,7 @@
 def ring_sum(flat, axis):
     count = lax.axis_size(axis)
     me = lax.axis_index(axis)
-    halves = flat.reshape(2, count, -1, 128)
+    halves = flat.reshape(2, count, -1, flat.shape[-1])
     results = []
     for half, way in ((0, 1), (1, -1)):
         own = halves[half]
@@ -87,8 +87,8 @@
             send = lax.ppermute(send, axis, route)
             chunk = lax.rem(me - way * step + 2 * count, count)
             out = lax.dynamic_update_index_in_dim(out, send, chunk, 0)
-        results.append(out.reshape(-1))
-    return jnp.concatenate(results)
+        results.append(out)
+    return jnp.stack(results).reshape(flat.shape)
 
 
 def normalize(section_in):
@@ -265,15 +265,14 @@
     received_live = lax.dynamic_slice_in_dim(saved[3], section_pos, micro_count, axis=0)
     preact_live = lax.dynamic_slice_in_dim(saved[4], section_pos, micro_count, axis=0)
     hidden_live = jax.nn.gelu(preact_live).astype(jnp.bfloat16)
-    acc_up = jnp.einsum(
-        "bsecd,bsech->edh", received_live, dpre_live, preferred_element_type=jnp.float32
+    rows_both = jnp.stack([received_live, dreceived_live])
+    cols_both = jnp.stack([dpre_live, hidden_live])
+    grads = jnp.einsum(
+        "kbsecd,kbsech->kedh", rows_both, cols_both, preferred_element_type=jnp.float32
     )
-    acc_down = jnp.einsum(
-        "bsech,bsecd->ehd", hidden_live, dreceived_live, preferred_element_type=jnp.float32
-    )
-    summed = ring_sum(jnp.concatenate([acc_up.reshape(-1), acc_down.reshape(-1)]), "dp")
-    sum_up = summed[: acc_up.size].reshape(acc_up.shape)
-    sum_down = summed[acc_up.size :].reshape(acc_down.shape)
+    summed = ring_sum(grads.reshape(2, features, w_up.shape[2]), "dp")
+    sum_up = summed[0].reshape(w_up.shape)
+    sum_down = summed[1].T.reshape(w_down.shape)
     up_out = sum_up.astype(jnp.bfloat16)
     down_out = sum_down.astype(jnp.bfloat16)
     return (up_out[None], down_out[None])

time: 1490 us -> 1630 us (1.094)
  local copies, waits for them, and re-layouts: 261 us -> 403 us
    dynamic_update_slice x6 -> x7, local copies, waits for them, and re-layouts: 3.82 us -> 104 us  [ring_sum(): out = lax.dynamic_update_index_in_dim(out, send, chunk, 0)]
    dynamic_update_slice x0 -> x2, local copies, waits for them, and re-layouts: none -> 28 us  [ring_sum(): lax.dynamic_update_index_in_dim(out, send, lax.rem(me + way + count, coun...]
    another operation x30 -> x38, local copies, waits for them, and re-layouts: 20.5 us -> 37.6 us  [the longest x10 21 us: ring_sum(): return jnp.stack(results).reshape(flat.shape)]
  transfers between devices with their start and end apart: 34 -> 34, of which waited for: 28 -> 29; matrix products, arithmetic and copies ran while one was open for 7% -> 13% of each run, Pallas kernels for 0% -> 0%
where the time goes in v8:
time: 1630 us; the launch traced here: 1610 us
  Pallas kernels  646 us (40%)
  local copies, waits for them, and re-layouts  403 us (25%)
  waiting for transfers between devices  208 us (13%)
  starting transfers between devices  153 us (9%)
  other arithmetic  116 us (7%)
  matrix products  65.8 us (4%)
  loops' own time  19.9 us (1%)
    pallas_call x44, Pallas kernels, expert_exchange(): pl.pallas_call(functools.partial(exchange_kernel, n), out_shape=jax.Shape...  646 us
    ppermute x22, waiting for transfers between devices, from_behind(): return lax.ppermute(block, axis, route)  162 us
    ppermute x22, starting transfers between devices, from_behind(): return lax.ppermute(block, axis, route)  132 us
    dynamic_update_slice x7, local copies, waits for them, and re-layouts, ring_sum(): out = lax.dynamic_update_index_in_dim(out, send, chunk, 0)  104 us
    dynamic_update_slice x44, local copies, waits for them, and re-layouts, local(): _, saved = lax.scan(forward_step, start_act, jnp.arange(step_count))  52.2 us
    gather x22, local copies, waits for them, and re-layouts, from_buffer(): buffer.reshape(experts_all * capacity, pieces, lanes)[dest_rows]  38.7 us
  transfers between devices with their start and end apart: 34, of which 29 were waited for; matrix products, arithmetic and copies ran while one was open for 13% of the time, Pallas kernels for 0%

profile of v8, /device:TPU:62, one launch (start us, length us, event | category | flops | bytes accessed | tf_op | source)
XLA Modules:
  0.0 1612.4 jit_solution(7401044503084151046)
XLA Ops:
  7.0 659.9 %while.39 = (s32[]{:T(128)}, bf16[32,2048]{1,0:T(8,128)(2,1)S(1)}, bf16[11,32,2048]{2,1,0:T(8,128)(2,1)}, f32[11,32,4]{1,2,0:T(4,128)S(1)}, bf16[11,32,4,2048]{3...) while((s32[]{:T(128)}, bf16[32,2048]{1,0:T(8,128)(2,1)S(1)}, ...), condition=%wide.region_9.10_spmd, body=%wide.region_3.9_spmd.sunk | while | flops 573976576 | bytes 24260048 | solution.py:192
  12.4 16.2 %eval_jaxpr.16 = bf16[8,272,128]{2,1,0:T(8,128)(2,1)S(1)} custom-call(bf16[8,272,128]{2,1,0:T(8,128)(2,1)} %bitcast_select_fusion.8.x_ref), custom_call_target="tpu_custom_call" | custom-call | bytes 1114112 | tf_op jit(solution)/shard_map/while/body/eval_jaxpr/pallas_call | solution.py:55
  30.6 15.7 eval_jaxpr.17
  143.8 14.9 eval_jaxpr.17
  207.0 14.9 eval_jaxpr.17
  265.4 14.9 eval_jaxpr.17
  450.3 14.9 eval_jaxpr.17
  470.0 15.1 collective-permute-start
  513.4 14.9 eval_jaxpr.17
  571.7 14.9 eval_jaxpr.17
  630.2 14.9 eval_jaxpr.17
  671.3 693.8 %while.40 = (s32[]{:T(128)}, bf16[32,2048]{1,0:T(8,128)(2,1)S(1)}, bf16[11,8,1,17,512]{4,3,1,2,0:T(8,128)(2,1)}, bf16[11,8,1,17,2048]{4,3,1,2,0:T(8,128)(2,1)}, ...) while((s32[]{:T(128)}, bf16[32,2048]{1,0:T(8,128)(2,1)S(1)}, ...), condition=%wide.region_20.21_spmd.clone, body=%wide.region_10.20_spmd.clone.sunk | while | flops 581163648 | bytes 27663032 | solution.py:261
  694.1 14.9 eval_jaxpr.19
  755.6 14.9 eval_jaxpr.19
  816.5 14.9 eval_jaxpr.19
  943.8 14.9 eval_jaxpr.19
  1010.5 14.9 eval_jaxpr.19
  1077.0 14.9 eval_jaxpr.19
  1460.9 19.2 %dynamic_update_slice.81 = bf16[1,4,512,512]{2,1,3,0:T(4,128)(2,1)} dynamic-update-slice(bf16[1,4,512,512]{2,1,3,0:T(4,128)(2,1)} %stack.39.clone, bf16[1,1,512,512]{2,1,3,0:T(2,128)(2,1)S(1)} %copy.108, s32[]{:T(128)} %constant.399.clone.1, s32[]{:T(128)S(6)} %select_n.241, s32[]{:T(128)} %constant.399.clone.1, s32[]{:T(128)} %constant.399.clone.1) | dynamic-update-slice | bytes 1048580 | tf_op jit(solution)/shard_map/jit(dynamic_update_index_in_dim)/dynamic_update_slice | solution.py:85
  1495.4 16.6 %dynamic_update_slice.86 = bf16[1,4,512,512]{2,1,3,0:T(4,128)(2,1)S(1)} dynamic-update-slice(bf16[1,4,512,512]{2,1,3,0:T(4,128)(2,1)S(1)} %dynamic_update_slice.85, bf16[1,1,512,512]{2,1,3,0:T(2,128)(2,1)} %copy.114, s32[]{:T(128)} %constant.399.clone.1, s32[]{:T(128)S(6)} %select_n.242, s32[]{:T(128)} %constant.399.clone.1, s32[]{:T(128)} %constant.399.clone.1) | dynamic-update-slice | bytes 1048580 | tf_op jit(solution)/shard_map/jit(dynamic_update_index_in_dim)/dynamic_update_slice | solution.py:89
  1512.1 19.2 %dynamic_update_slice.82 = bf16[1,4,512,512]{2,1,3,0:T(4,128)(2,1)} dynamic-update-slice(bf16[1,4,512,512]{2,1,3,0:T(4,128)(2,1)} %dynamic_update_slice.81, bf16[1,1,512,512]{2,1,3,0:T(2,128)(2,1)S(1)} %copy.109, s32[]{:T(128)} %constant.399.clone.1, s32[]{:T(128)S(6)} %select_n.242, s32[]{:T(128)} %constant.399.clone.1, s32[]{:T(128)} %constant.399.clone.1) | dynamic-update-slice | bytes 1048580 | tf_op jit(solution)/shard_map/jit(dynamic_update_index_in_dim)/dynamic_update_slice | solution.py:89
  1537.2 16.6 %dynamic_update_slice.87 = bf16[1,4,512,512]{2,1,3,0:T(4,128)(2,1)S(1)} dynamic-update-slice(bf16[1,4,512,512]{2,1,3,0:T(4,128)(2,1)S(1)} %dynamic_update_slice.86, bf16[1,1,512,512]{2,1,3,0:T(2,128)(2,1)} %copy.115, s32[]{:T(128)} %constant.399.clone.1, s32[]{:T(128)S(6)} %select_n.243, s32[]{:T(128)} %constant.399.clone.1, s32[]{:T(128)} %constant.399.clone.1) | dynamic-update-slice | bytes 1048580 | tf_op jit(solution)/shard_map/jit(dynamic_update_index_in_dim)/dynamic_update_slice | solution.py:89
  1553.9 19.2 %dynamic_update_slice.83 = bf16[1,4,512,512]{2,1,3,0:T(4,128)(2,1)} dynamic-update-slice(bf16[1,4,512,512]{2,1,3,0:T(4,128)(2,1)} %dynamic_update_slice.82, bf16[1,1,512,512]{2,1,3,0:T(2,128)(2,1)S(1)} %copy.110, s32[]{:T(128)} %constant.399.clone.1, s32[]{:T(128)S(6)} %select_n.239, s32[]{:T(128)} %constant.399.clone.1, s32[]{:T(128)} %constant.399.clone.1) | dynamic-update-slice | bytes 1048580 | tf_op jit(solution)/shard_map/jit(dynamic_update_index_in_dim)/dynamic_update_slice | solution.py:89
  1588.7 19.2 %dynamic_update_slice.84 = bf16[1,4,512,512]{2,1,3,0:T(4,128)(2,1)} dynamic-update-slice(bf16[1,4,512,512]{2,1,3,0:T(4,128)(2,1)} %dynamic_update_slice.83, bf16[1,1,512,512]{2,1,3,0:T(2,128)(2,1)S(1)} %copy.111, s32[]{:T(128)} %constant.399.clone.1, s32[]{:T(128)S(6)} %select_n.240, s32[]{:T(128)} %constant.399.clone.1, s32[]{:T(128)} %constant.399.clone.1) | dynamic-update-slice | bytes 1048580 | tf_op jit(solution)/shard_map/jit(dynamic_update_index_in_dim)/dynamic_update_slice | solution.py:89
  (1059 shorter events, 1301.0 us)
Async XLA Ops:
  105.0 17.0 %collective-permute-start = (bf16[32,2048]{1,0:T(8,128)(2,1)S(1)}, bf16[32,2048]{1,0:T(8,128)(2,1)S(1)}, u32[]{:S(2)}, u32[]{:S(2)}) collective-permute-start(bf16[32,2048]{1,0:T(8,128)(2,1)S(1)} %fusion.123), channel_id=1, source_target_pairs={{0,32},{32,64},{64,96},{96,128},{128,160},{160,192},{192,224},{1,3... | collective-permute-start | bytes 393224 | tf_op jit(solution)/shard_map/while/body/eval_jaxpr/ppermute | solution.py:21
  163.4 17.1 %collective-permute-start = (bf16[32,2048]{1,0:T(8,128)(2,1)S(1)}, bf16[32,2048]{1,0:T(8,128)(2,1)S(1)}, u32[]{:S(2)}, u32[]{:S(2)}) collective-permute-start(bf16[32,2048]{1,0:T(8,128)(2,1)S(1)} %fusion.123), channel_id=1, source_target_pairs={{0,32},{32,64},{64,96},{96,128},{128,160},{160,192},{192,224},{1,3... | collective-permute-start | bytes 393224 | tf_op jit(solution)/shard_map/while/body/eval_jaxpr/ppermute | solution.py:21
  285.0 17.1 %collective-permute-start = (bf16[32,2048]{1,0:T(8,128)(2,1)S(1)}, bf16[32,2048]{1,0:T(8,128)(2,1)S(1)}, u32[]{:S(2)}, u32[]{:S(2)}) collective-permute-start(bf16[32,2048]{1,0:T(8,128)(2,1)S(1)} %fusion.123), channel_id=1, source_target_pairs={{0,32},{32,64},{64,96},{96,128},{128,160},{160,192},{192,224},{1,3... | collective-permute-start | bytes 393224 | tf_op jit(solution)/shard_map/while/body/eval_jaxpr/ppermute | solution.py:21
  348.2 17.2 %collective-permute-start = (bf16[32,2048]{1,0:T(8,128)(2,1)S(1)}, bf16[32,2048]{1,0:T(8,128)(2,1)S(1)}, u32[]{:S(2)}, u32[]{:S(2)}) collective-permute-start(bf16[32,2048]{1,0:T(8,128)(2,1)S(1)} %fusion.123), channel_id=1, source_target_pairs={{0,32},{32,64},{64,96},{96,128},{128,160},{160,192},{192,224},{1,3... | collective-permute-start | bytes 393224 | tf_op jit(solution)/shard_map/while/body/eval_jaxpr/ppermute | solution.py:21
  411.4 17.1 %collective-permute-start = (bf16[32,2048]{1,0:T(8,128)(2,1)S(1)}, bf16[32,2048]{1,0:T(8,128)(2,1)S(1)}, u32[]{:S(2)}, u32[]{:S(2)}) collective-permute-start(bf16[32,2048]{1,0:T(8,128)(2,1)S(1)} %fusion.123), channel_id=1, source_target_pairs={{0,32},{32,64},{64,96},{96,128},{128,160},{160,192},{192,224},{1,3... | collective-permute-start | bytes 393224 | tf_op jit(solution)/shard_map/while/body/eval_jaxpr/ppermute | solution.py:21
  470.0 21.7 %collective-permute-start = (bf16[32,2048]{1,0:T(8,128)(2,1)S(1)}, bf16[32,2048]{1,0:T(8,128)(2,1)S(1)}, u32[]{:S(2)}, u32[]{:S(2)}) collective-permute-start(bf16[32,2048]{1,0:T(8,128)(2,1)S(1)} %fusion.123), channel_id=1, source_target_pairs={{0,32},{32,64},{64,96},{96,128},{128,160},{160,192},{192,224},{1,3... | collective-permute-start | bytes 393224 | tf_op jit(solution)/shard_map/while/body/eval_jaxpr/ppermute | solution.py:21
  533.0 17.0 %collective-permute-start = (bf16[32,2048]{1,0:T(8,128)(2,1)S(1)}, bf16[32,2048]{1,0:T(8,128)(2,1)S(1)}, u32[]{:S(2)}, u32[]{:S(2)}) collective-permute-start(bf16[32,2048]{1,0:T(8,128)(2,1)S(1)} %fusion.123), channel_id=1, source_target_pairs={{0,32},{32,64},{64,96},{96,128},{128,160},{160,192},{192,224},{1,3... | collective-permute-start | bytes 393224 | tf_op jit(solution)/shard_map/while/body/eval_jaxpr/ppermute | solution.py:21
  591.3 17.1 %collective-permute-start = (bf16[32,2048]{1,0:T(8,128)(2,1)S(1)}, bf16[32,2048]{1,0:T(8,128)(2,1)S(1)}, u32[]{:S(2)}, u32[]{:S(2)}) collective-permute-start(bf16[32,2048]{1,0:T(8,128)(2,1)S(1)} %fusion.123), channel_id=1, source_target_pairs={{0,32},{32,64},{64,96},{96,128},{128,160},{160,192},{192,224},{1,3... | collective-permute-start | bytes 393224 | tf_op jit(solution)/shard_map/while/body/eval_jaxpr/ppermute | solution.py:21
  649.8 17.1 %collective-permute-start = (bf16[32,2048]{1,0:T(8,128)(2,1)S(1)}, bf16[32,2048]{1,0:T(8,128)(2,1)S(1)}, u32[]{:S(2)}, u32[]{:S(2)}) collective-permute-start(bf16[32,2048]{1,0:T(8,128)(2,1)S(1)} %fusion.123), channel_id=1, source_target_pairs={{0,32},{32,64},{64,96},{96,128},{128,160},{160,192},{192,224},{1,3... | collective-permute-start | bytes 393224 | tf_op jit(solution)/shard_map/while/body/eval_jaxpr/ppermute | solution.py:21
  715.7 17.6 %collective-permute-start.1 = (bf16[32,2048]{1,0:T(8,128)(2,1)S(1)}, bf16[32,2048]{1,0:T(8,128)(2,1)S(1)}, u32[]{:S(2)}, u32[]{:S(2)}) collective-permute-start(bf16[32,2048]{1,0:T(8,128)(2,1)S(1)} %fusion.134), channel_id=1, source_target_pairs={{32,0},{64,32},{96,64},{128,96},{160,128},{192,160},{224,192},{33,... | collective-permute-start | bytes 393224 | tf_op jit(solution)/shard_map/while/body/eval_jaxpr/ppermute | solution.py:21
  777.3 17.0 %collective-permute-start.1 = (bf16[32,2048]{1,0:T(8,128)(2,1)S(1)}, bf16[32,2048]{1,0:T(8,128)(2,1)S(1)}, u32[]{:S(2)}, u32[]{:S(2)}) collective-permute-start(bf16[32,2048]{1,0:T(8,128)(2,1)S(1)} %fusion.134), channel_id=1, source_target_pairs={{32,0},{64,32},{96,64},{128,96},{160,128},{192,160},{224,192},{33,... | collective-permute-start | bytes 393224 | tf_op jit(solution)/shard_map/while/body/eval_jaxpr/ppermute | solution.py:21
  838.1 17.0 %collective-permute-start.1 = (bf16[32,2048]{1,0:T(8,128)(2,1)S(1)}, bf16[32,2048]{1,0:T(8,128)(2,1)S(1)}, u32[]{:S(2)}, u32[]{:S(2)}) collective-permute-start(bf16[32,2048]{1,0:T(8,128)(2,1)S(1)} %fusion.134), channel_id=1, source_target_pairs={{32,0},{64,32},{96,64},{128,96},{160,128},{192,160},{224,192},{33,... | collective-permute-start | bytes 393224 | tf_op jit(solution)/shard_map/while/body/eval_jaxpr/ppermute | solution.py:21
  899.0 17.0 %collective-permute-start.1 = (bf16[32,2048]{1,0:T(8,128)(2,1)S(1)}, bf16[32,2048]{1,0:T(8,128)(2,1)S(1)}, u32[]{:S(2)}, u32[]{:S(2)}) collective-permute-start(bf16[32,2048]{1,0:T(8,128)(2,1)S(1)} %fusion.134), channel_id=1, source_target_pairs={{32,0},{64,32},{96,64},{128,96},{160,128},{192,160},{224,192},{33,... | collective-permute-start | bytes 393224 | tf_op jit(solution)/shard_map/while/body/eval_jaxpr/ppermute | solution.py:21
  965.4 17.2 %collective-permute-start.1 = (bf16[32,2048]{1,0:T(8,128)(2,1)S(1)}, bf16[32,2048]{1,0:T(8,128)(2,1)S(1)}, u32[]{:S(2)}, u32[]{:S(2)}) collective-permute-start(bf16[32,2048]{1,0:T(8,128)(2,1)S(1)} %fusion.134), channel_id=1, source_target_pairs={{32,0},{64,32},{96,64},{128,96},{160,128},{192,160},{224,192},{33,... | collective-permute-start | bytes 393224 | tf_op jit(solution)/shard_map/while/body/eval_jaxpr/ppermute | solution.py:21
  1032.1 17.1 %collective-permute-start.1 = (bf16[32,2048]{1,0:T(8,128)(2,1)S(1)}, bf16[32,2048]{1,0:T(8,128)(2,1)S(1)}, u32[]{:S(2)}, u32[]{:S(2)}) collective-permute-start(bf16[32,2048]{1,0:T(8,128)(2,1)S(1)} %fusion.134), channel_id=1, source_target_pairs={{32,0},{64,32},{96,64},{128,96},{160,128},{192,160},{224,192},{33,... | collective-permute-start | bytes 393224 | tf_op jit(solution)/shard_map/while/body/eval_jaxpr/ppermute | solution.py:21
  1098.6 17.0 %collective-permute-start.1 = (bf16[32,2048]{1,0:T(8,128)(2,1)S(1)}, bf16[32,2048]{1,0:T(8,128)(2,1)S(1)}, u32[]{:S(2)}, u32[]{:S(2)}) collective-permute-start(bf16[32,2048]{1,0:T(8,128)(2,1)S(1)} %fusion.134), channel_id=1, source_target_pairs={{32,0},{64,32},{96,64},{128,96},{160,128},{192,160},{224,192},{33,... | collective-permute-start | bytes 393224 | tf_op jit(solution)/shard_map/while/body/eval_jaxpr/ppermute | solution.py:21
  1165.0 17.0 %collective-permute-start.1 = (bf16[32,2048]{1,0:T(8,128)(2,1)S(1)}, bf16[32,2048]{1,0:T(8,128)(2,1)S(1)}, u32[]{:S(2)}, u32[]{:S(2)}) collective-permute-start(bf16[32,2048]{1,0:T(8,128)(2,1)S(1)} %fusion.134), channel_id=1, source_target_pairs={{32,0},{64,32},{96,64},{128,96},{160,128},{192,160},{224,192},{33,... | collective-permute-start | bytes 393224 | tf_op jit(solution)/shard_map/while/body/eval_jaxpr/ppermute | solution.py:21
  1225.9 17.1 %collective-permute-start.1 = (bf16[32,2048]{1,0:T(8,128)(2,1)S(1)}, bf16[32,2048]{1,0:T(8,128)(2,1)S(1)}, u32[]{:S(2)}, u32[]{:S(2)}) collective-permute-start(bf16[32,2048]{1,0:T(8,128)(2,1)S(1)} %fusion.134), channel_id=1, source_target_pairs={{32,0},{64,32},{96,64},{128,96},{160,128},{192,160},{224,192},{33,... | collective-permute-start | bytes 393224 | tf_op jit(solution)/shard_map/while/body/eval_jaxpr/ppermute | solution.py:21
  1286.9 17.1 %collective-permute-start.1 = (bf16[32,2048]{1,0:T(8,128)(2,1)S(1)}, bf16[32,2048]{1,0:T(8,128)(2,1)S(1)}, u32[]{:S(2)}, u32[]{:S(2)}) collective-permute-start(bf16[32,2048]{1,0:T(8,128)(2,1)S(1)} %fusion.134), channel_id=1, source_target_pairs={{32,0},{64,32},{96,64},{128,96},{160,128},{192,160},{224,192},{33,... | collective-permute-start | bytes 393224 | tf_op jit(solution)/shard_map/while/body/eval_jaxpr/ppermute | solution.py:21
  1348.0 17.0 %collective-permute-start.1 = (bf16[32,2048]{1,0:T(8,128)(2,1)S(1)}, bf16[32,2048]{1,0:T(8,128)(2,1)S(1)}, u32[]{:S(2)}, u32[]{:S(2)}) collective-permute-start(bf16[32,2048]{1,0:T(8,128)(2,1)S(1)} %fusion.134), channel_id=1, source_target_pairs={{32,0},{64,32},{96,64},{128,96},{160,128},{192,160},{224,192},{33,... | collective-permute-start | bytes 393224 | tf_op jit(solution)/shard_map/while/body/eval_jaxpr/ppermute | solution.py:21
  1381.4 15.1 collective-permute-start.8
  1383.6 14.4 collective-permute-start.2
  1452.8 120.3 %collective-permute-start.13 = (bf16[512,512]{1,0:T(8,128)(2,1)}, bf16[512,512]{1,0:T(8,128)(2,1)}, u32[]{:S(2)}, u32[]{:S(2)}) collective-permute-start(bf16[512,512]{1,0:T(8,128)(2,1)} %collective-permute-done.12), channel_id=1, source_target_pairs={{0,24},{8,0},{16,8},{24,16},{1,25},{9,1},{17,9},{25,17},{2,26},{10... | collective-permute-start | bytes 1572872 | tf_op jit(solution)/shard_map/ppermute | solution.py:87
  1453.8 132.4 %collective-permute-start.7 = (bf16[512,512]{1,0:T(8,128)(2,1)}, bf16[512,512]{1,0:T(8,128)(2,1)}, u32[]{:S(2)}, u32[]{:S(2)}) collective-permute-start(bf16[512,512]{1,0:T(8,128)(2,1)} %collective-permute-done.6), channel_id=1, source_target_pairs={{0,8},{8,16},{16,24},{24,0},{1,9},{9,17},{17,25},{25,1},{2,10},{10... | collective-permute-start | bytes 1572872 | tf_op jit(solution)/shard_map/ppermute | solution.py:87
  (14 other events, 165.6 us)

commit v9 on v8

--- a/solution.py
+++ b/solution.py
@@ -81,13 +81,18 @@
             chunk = lax.rem(me - way * (1 + step) + 2 * count, count)
             part = lax.dynamic_index_in_dim(own, chunk, 0, keepdims=False)
             send = (got.astype(jnp.float32) + part).astype(jnp.bfloat16)
-        out = jnp.zeros(own.shape, jnp.bfloat16)
-        out = lax.dynamic_update_index_in_dim(out, send, lax.rem(me + way + count, count), 0)
+        arrived = [send]
         for step in range(count - 1):
             send = lax.ppermute(send, axis, route)
-            chunk = lax.rem(me - way * step + 2 * count, count)
-            out = lax.dynamic_update_index_in_dim(out, send, chunk, 0)
-        results.append(out)
+            arrived.append(send)
+        if way == 1:
+            ordered = jnp.stack(arrived[1:][::-1] + [arrived[0]])
+            first = lax.rem(count - 2 - me + 2 * count, count)
+        else:
+            ordered = jnp.stack(arrived)
+            first = lax.rem(1 - me + 2 * count, count)
+        doubled = jnp.concatenate([ordered, ordered])
+        results.append(lax.dynamic_slice_in_dim(doubled, first, count, axis=0))
     return jnp.stack(results).reshape(flat.shape)
 
 

time: 1630 us -> 1480 us (0.908)
  local copies, waits for them, and re-layouts: 403 us -> 264 us
    dynamic_update_slice x9 -> x0, local copies, waits for them, and re-layouts: 132 us -> none  [the longest x7 104 us: ring_sum(): out = lax.dynamic_update_index_in_dim(out, send, chunk, 0)]
    another operation x36 -> x26, local copies, waits for them, and re-layouts: 33 us -> 12 us  [the longest x10 21 us: ring_sum(): return jnp.stack(results).reshape(flat.shape)]
  transfers between devices with their start and end apart: 34 -> 34, of which waited for: 29 -> 29; matrix products, arithmetic and copies ran while one was open for 13% -> 7% of each run, Pallas kernels for 0% -> 0%
where the time goes in v9:
time: 1480 us
  Pallas kernels  646 us (44%)
  local copies, waits for them, and re-layouts  264 us (18%)
  waiting for transfers between devices  212 us (14%)
  starting transfers between devices  153 us (10%)
  other arithmetic  117 us (8%)
  matrix products  65.8 us (4%)
  loops' own time  19.4 us (1%)
    pallas_call x44, Pallas kernels, expert_exchange(): pl.pallas_call(functools.partial(exchange_kernel, n), out_shape=jax.Shape...  646 us
    ppermute x22, waiting for transfers between devices, from_behind(): return lax.ppermute(block, axis, route)  162 us
    ppermute x22, starting transfers between devices, from_behind(): return lax.ppermute(block, axis, route)  132 us
    dynamic_update_slice x44, local copies, waits for them, and re-layouts, local(): _, saved = lax.scan(forward_step, start_act, jnp.arange(step_count))  52.2 us
    gather x22, local copies, waits for them, and re-layouts, from_buffer(): buffer.reshape(experts_all * capacity, pieces, lanes)[dest_rows]  38.6 us
  transfers between devices with their start and end apart: 34, of which 29 were waited for; matrix products, arithmetic and copies ran while one was open for 7% of the time, Pallas kernels for 0%

profile of v9, /device:TPU:62, one launch (start us, length us, event | category | flops | bytes accessed | tf_op | source)
XLA Modules:
  0.0 1477.9 jit_solution(14283727324085533142)
XLA Ops:
  7.0 659.9 %while.39 = (s32[]{:T(128)}, bf16[32,2048]{1,0:T(8,128)(2,1)S(1)}, bf16[11,32,2048]{2,1,0:T(8,128)(2,1)}, f32[11,32,4]{1,2,0:T(4,128)S(1)}, bf16[11,32,4,2048]{3...) while((s32[]{:T(128)}, bf16[32,2048]{1,0:T(8,128)(2,1)S(1)}, ...), condition=%wide.region_9.10_spmd, body=%wide.region_3.9_spmd.sunk | while | flops 573976576 | bytes 24260048 | solution.py:197
  12.4 16.2 %eval_jaxpr.16 = bf16[8,272,128]{2,1,0:T(8,128)(2,1)S(1)} custom-call(bf16[8,272,128]{2,1,0:T(8,128)(2,1)} %bitcast_select_fusion.8.x_ref), custom_call_target="tpu_custom_call" | custom-call | bytes 1114112 | tf_op jit(solution)/shard_map/while/body/eval_jaxpr/pallas_call | solution.py:55
  30.6 15.7 %eval_jaxpr.17 = bf16[8,272,128]{2,1,0:T(8,128)(2,1)} custom-call(bf16[8,272,128]{2,1,0:T(8,128)(2,1)} %reshape.677.x_ref), custom_call_target="tpu_custom_call" | custom-call | bytes 1114112 | tf_op jit(solution)/shard_map/while/body/eval_jaxpr/pallas_call | solution.py:55
  85.4 14.9 %eval_jaxpr.17 = bf16[8,272,128]{2,1,0:T(8,128)(2,1)} custom-call(bf16[8,272,128]{2,1,0:T(8,128)(2,1)} %reshape.677.x_ref), custom_call_target="tpu_custom_call" | custom-call | bytes 1114112 | tf_op jit(solution)/shard_map/while/body/eval_jaxpr/pallas_call | solution.py:55
  143.8 14.9 %eval_jaxpr.17 = bf16[8,272,128]{2,1,0:T(8,128)(2,1)} custom-call(bf16[8,272,128]{2,1,0:T(8,128)(2,1)} %reshape.677.x_ref), custom_call_target="tpu_custom_call" | custom-call | bytes 1114112 | tf_op jit(solution)/shard_map/while/body/eval_jaxpr/pallas_call | solution.py:55
  207.0 14.9 %eval_jaxpr.17 = bf16[8,272,128]{2,1,0:T(8,128)(2,1)} custom-call(bf16[8,272,128]{2,1,0:T(8,128)(2,1)} %reshape.677.x_ref), custom_call_target="tpu_custom_call" | custom-call | bytes 1114112 | tf_op jit(solution)/shard_map/while/body/eval_jaxpr/pallas_call | solution.py:55
  265.4 14.9 %eval_jaxpr.17 = bf16[8,272,128]{2,1,0:T(8,128)(2,1)} custom-call(bf16[8,272,128]{2,1,0:T(8,128)(2,1)} %reshape.677.x_ref), custom_call_target="tpu_custom_call" | custom-call | bytes 1114112 | tf_op jit(solution)/shard_map/while/body/eval_jaxpr/pallas_call | solution.py:55
  391.8 14.9 %eval_jaxpr.17 = bf16[8,272,128]{2,1,0:T(8,128)(2,1)} custom-call(bf16[8,272,128]{2,1,0:T(8,128)(2,1)} %reshape.677.x_ref), custom_call_target="tpu_custom_call" | custom-call | bytes 1114112 | tf_op jit(solution)/shard_map/while/body/eval_jaxpr/pallas_call | solution.py:55
  450.3 14.9 %eval_jaxpr.17 = bf16[8,272,128]{2,1,0:T(8,128)(2,1)} custom-call(bf16[8,272,128]{2,1,0:T(8,128)(2,1)} %reshape.677.x_ref), custom_call_target="tpu_custom_call" | custom-call | bytes 1114112 | tf_op jit(solution)/shard_map/while/body/eval_jaxpr/pallas_call | solution.py:55
  469.9 15.1 %collective-permute-start = (bf16[32,2048]{1,0:T(8,128)(2,1)S(1)}, bf16[32,2048]{1,0:T(8,128)(2,1)S(1)}, u32[]{:S(2)}, u32[]{:S(2)}) collective-permute-start(bf16[32,2048]{1,0:T(8,128)(2,1)S(1)} %fusion.124), channel_id=1, source_target_pairs={{0,32},{32,64},{64,96},{96,128},{128,160},{160,192},{192,224},{1,3... | collective-permute-start | bytes 393224 | tf_op jit(solution)/shard_map/while/body/eval_jaxpr/ppermute | solution.py:21
  513.4 14.9 %eval_jaxpr.17 = bf16[8,272,128]{2,1,0:T(8,128)(2,1)} custom-call(bf16[8,272,128]{2,1,0:T(8,128)(2,1)} %reshape.677.x_ref), custom_call_target="tpu_custom_call" | custom-call | bytes 1114112 | tf_op jit(solution)/shard_map/while/body/eval_jaxpr/pallas_call | solution.py:55
  571.7 14.9 %eval_jaxpr.17 = bf16[8,272,128]{2,1,0:T(8,128)(2,1)} custom-call(bf16[8,272,128]{2,1,0:T(8,128)(2,1)} %reshape.677.x_ref), custom_call_target="tpu_custom_call" | custom-call | bytes 1114112 | tf_op jit(solution)/shard_map/while/body/eval_jaxpr/pallas_call | solution.py:55
  630.2 14.9 %eval_jaxpr.17 = bf16[8,272,128]{2,1,0:T(8,128)(2,1)} custom-call(bf16[8,272,128]{2,1,0:T(8,128)(2,1)} %reshape.677.x_ref), custom_call_target="tpu_custom_call" | custom-call | bytes 1114112 | tf_op jit(solution)/shard_map/while/body/eval_jaxpr/pallas_call | solution.py:55
  671.3 693.3 %while.40 = (s32[]{:T(128)}, bf16[32,2048]{1,0:T(8,128)(2,1)S(1)}, bf16[11,8,1,17,512]{4,3,1,2,0:T(8,128)(2,1)}, bf16[11,8,1,17,2048]{4,3,1,2,0:T(8,128)(2,1)}, ...) while((s32[]{:T(128)}, bf16[32,2048]{1,0:T(8,128)(2,1)S(1)}, ...), condition=%wide.region_20.21_spmd.clone, body=%wide.region_10.20_spmd.clone.sunk | while | flops 581163648 | bytes 27663032 | solution.py:266
  693.8 14.9 %eval_jaxpr.19 = bf16[8,272,128]{2,1,0:T(8,128)(2,1)} custom-call(bf16[8,272,128]{2,1,0:T(8,128)(2,1)} %reshape.685.x_ref), custom_call_target="tpu_custom_call" | custom-call | bytes 1114112 | tf_op jit(solution)/shard_map/while/body/eval_jaxpr/pallas_call | solution.py:55
  755.3 14.9 %eval_jaxpr.19 = bf16[8,272,128]{2,1,0:T(8,128)(2,1)} custom-call(bf16[8,272,128]{2,1,0:T(8,128)(2,1)} %reshape.685.x_ref), custom_call_target="tpu_custom_call" | custom-call | bytes 1114112 | tf_op jit(solution)/shard_map/while/body/eval_jaxpr/pallas_call | solution.py:55
  816.2 14.9 %eval_jaxpr.19 = bf16[8,272,128]{2,1,0:T(8,128)(2,1)} custom-call(bf16[8,272,128]{2,1,0:T(8,128)(2,1)} %reshape.685.x_ref), custom_call_target="tpu_custom_call" | custom-call | bytes 1114112 | tf_op jit(solution)/shard_map/while/body/eval_jaxpr/pallas_call | solution.py:55
  877.1 14.9 %eval_jaxpr.19 = bf16[8,272,128]{2,1,0:T(8,128)(2,1)} custom-call(bf16[8,272,128]{2,1,0:T(8,128)(2,1)} %reshape.685.x_ref), custom_call_target="tpu_custom_call" | custom-call | bytes 1114112 | tf_op jit(solution)/shard_map/while/body/eval_jaxpr/pallas_call | solution.py:55
  943.5 14.9 %eval_jaxpr.19 = bf16[8,272,128]{2,1,0:T(8,128)(2,1)} custom-call(bf16[8,272,128]{2,1,0:T(8,128)(2,1)} %reshape.685.x_ref), custom_call_target="tpu_custom_call" | custom-call | bytes 1114112 | tf_op jit(solution)/shard_map/while/body/eval_jaxpr/pallas_call | solution.py:55
  1010.2 14.9 %eval_jaxpr.19 = bf16[8,272,128]{2,1,0:T(8,128)(2,1)} custom-call(bf16[8,272,128]{2,1,0:T(8,128)(2,1)} %reshape.685.x_ref), custom_call_target="tpu_custom_call" | custom-call | bytes 1114112 | tf_op jit(solution)/shard_map/while/body/eval_jaxpr/pallas_call | solution.py:55
  1076.7 14.9 %eval_jaxpr.19 = bf16[8,272,128]{2,1,0:T(8,128)(2,1)} custom-call(bf16[8,272,128]{2,1,0:T(8,128)(2,1)} %reshape.685.x_ref), custom_call_target="tpu_custom_call" | custom-call | bytes 1114112 | tf_op jit(solution)/shard_map/while/body/eval_jaxpr/pallas_call | solution.py:55
  1204.0 14.9 %eval_jaxpr.19 = bf16[8,272,128]{2,1,0:T(8,128)(2,1)} custom-call(bf16[8,272,128]{2,1,0:T(8,128)(2,1)} %reshape.685.x_ref), custom_call_target="tpu_custom_call" | custom-call | bytes 1114112 | tf_op jit(solution)/shard_map/while/body/eval_jaxpr/pallas_call | solution.py:55
  1265.0 14.9 %eval_jaxpr.19 = bf16[8,272,128]{2,1,0:T(8,128)(2,1)} custom-call(bf16[8,272,128]{2,1,0:T(8,128)(2,1)} %reshape.685.x_ref), custom_call_target="tpu_custom_call" | custom-call | bytes 1114112 | tf_op jit(solution)/shard_map/while/body/eval_jaxpr/pallas_call | solution.py:55
  1326.0 14.9 %eval_jaxpr.19 = bf16[8,272,128]{2,1,0:T(8,128)(2,1)} custom-call(bf16[8,272,128]{2,1,0:T(8,128)(2,1)} %reshape.685.x_ref), custom_call_target="tpu_custom_call" | custom-call | bytes 1114112 | tf_op jit(solution)/shard_map/while/body/eval_jaxpr/pallas_call | solution.py:55
  (1053 shorter events, 1188.0 us)
Async XLA Ops:
  105.0 17.0 %collective-permute-start = (bf16[32,2048]{1,0:T(8,128)(2,1)S(1)}, bf16[32,2048]{1,0:T(8,128)(2,1)S(1)}, u32[]{:S(2)}, u32[]{:S(2)}) collective-permute-start(bf16[32,2048]{1,0:T(8,128)(2,1)S(1)} %fusion.124), channel_id=1, source_target_pairs={{0,32},{32,64},{64,96},{96,128},{128,160},{160,192},{192,224},{1,3... | collective-permute-start | bytes 393224 | tf_op jit(solution)/shard_map/while/body/eval_jaxpr/ppermute | solution.py:21
  163.4 17.1 %collective-permute-start = (bf16[32,2048]{1,0:T(8,128)(2,1)S(1)}, bf16[32,2048]{1,0:T(8,128)(2,1)S(1)}, u32[]{:S(2)}, u32[]{:S(2)}) collective-permute-start(bf16[32,2048]{1,0:T(8,128)(2,1)S(1)} %fusion.124), channel_id=1, source_target_pairs={{0,32},{32,64},{64,96},{96,128},{128,160},{160,192},{192,224},{1,3... | collective-permute-start | bytes 393224 | tf_op jit(solution)/shard_map/while/body/eval_jaxpr/ppermute | solution.py:21
  285.0 17.1 %collective-permute-start = (bf16[32,2048]{1,0:T(8,128)(2,1)S(1)}, bf16[32,2048]{1,0:T(8,128)(2,1)S(1)}, u32[]{:S(2)}, u32[]{:S(2)}) collective-permute-start(bf16[32,2048]{1,0:T(8,128)(2,1)S(1)} %fusion.124), channel_id=1, source_target_pairs={{0,32},{32,64},{64,96},{96,128},{128,160},{160,192},{192,224},{1,3... | collective-permute-start | bytes 393224 | tf_op jit(solution)/shard_map/while/body/eval_jaxpr/ppermute | solution.py:21
  348.2 17.2 %collective-permute-start = (bf16[32,2048]{1,0:T(8,128)(2,1)S(1)}, bf16[32,2048]{1,0:T(8,128)(2,1)S(1)}, u32[]{:S(2)}, u32[]{:S(2)}) collective-permute-start(bf16[32,2048]{1,0:T(8,128)(2,1)S(1)} %fusion.124), channel_id=1, source_target_pairs={{0,32},{32,64},{64,96},{96,128},{128,160},{160,192},{192,224},{1,3... | collective-permute-start | bytes 393224 | tf_op jit(solution)/shard_map/while/body/eval_jaxpr/ppermute | solution.py:21
  411.4 17.1 %collective-permute-start = (bf16[32,2048]{1,0:T(8,128)(2,1)S(1)}, bf16[32,2048]{1,0:T(8,128)(2,1)S(1)}, u32[]{:S(2)}, u32[]{:S(2)}) collective-permute-start(bf16[32,2048]{1,0:T(8,128)(2,1)S(1)} %fusion.124), channel_id=1, source_target_pairs={{0,32},{32,64},{64,96},{96,128},{128,160},{160,192},{192,224},{1,3... | collective-permute-start | bytes 393224 | tf_op jit(solution)/shard_map/while/body/eval_jaxpr/ppermute | solution.py:21
  469.9 21.7 %collective-permute-start = (bf16[32,2048]{1,0:T(8,128)(2,1)S(1)}, bf16[32,2048]{1,0:T(8,128)(2,1)S(1)}, u32[]{:S(2)}, u32[]{:S(2)}) collective-permute-start(bf16[32,2048]{1,0:T(8,128)(2,1)S(1)} %fusion.124), channel_id=1, source_target_pairs={{0,32},{32,64},{64,96},{96,128},{128,160},{160,192},{192,224},{1,3... | collective-permute-start | bytes 393224 | tf_op jit(solution)/shard_map/while/body/eval_jaxpr/ppermute | solution.py:21
  533.0 17.0 %collective-permute-start = (bf16[32,2048]{1,0:T(8,128)(2,1)S(1)}, bf16[32,2048]{1,0:T(8,128)(2,1)S(1)}, u32[]{:S(2)}, u32[]{:S(2)}) collective-permute-start(bf16[32,2048]{1,0:T(8,128)(2,1)S(1)} %fusion.124), channel_id=1, source_target_pairs={{0,32},{32,64},{64,96},{96,128},{128,160},{160,192},{192,224},{1,3... | collective-permute-start | bytes 393224 | tf_op jit(solution)/shard_map/while/body/eval_jaxpr/ppermute | solution.py:21
  591.3 17.1 %collective-permute-start = (bf16[32,2048]{1,0:T(8,128)(2,1)S(1)}, bf16[32,2048]{1,0:T(8,128)(2,1)S(1)}, u32[]{:S(2)}, u32[]{:S(2)}) collective-permute-start(bf16[32,2048]{1,0:T(8,128)(2,1)S(1)} %fusion.124), channel_id=1, source_target_pairs={{0,32},{32,64},{64,96},{96,128},{128,160},{160,192},{192,224},{1,3... | collective-permute-start | bytes 393224 | tf_op jit(solution)/shard_map/while/body/eval_jaxpr/ppermute | solution.py:21
  649.8 17.1 %collective-permute-start = (bf16[32,2048]{1,0:T(8,128)(2,1)S(1)}, bf16[32,2048]{1,0:T(8,128)(2,1)S(1)}, u32[]{:S(2)}, u32[]{:S(2)}) collective-permute-start(bf16[32,2048]{1,0:T(8,128)(2,1)S(1)} %fusion.124), channel_id=1, source_target_pairs={{0,32},{32,64},{64,96},{96,128},{128,160},{160,192},{192,224},{1,3... | collective-permute-start | bytes 393224 | tf_op jit(solution)/shard_map/while/body/eval_jaxpr/ppermute | solution.py:21
  715.4 17.6 %collective-permute-start.1 = (bf16[32,2048]{1,0:T(8,128)(2,1)S(1)}, bf16[32,2048]{1,0:T(8,128)(2,1)S(1)}, u32[]{:S(2)}, u32[]{:S(2)}) collective-permute-start(bf16[32,2048]{1,0:T(8,128)(2,1)S(1)} %fusion.135), channel_id=1, source_target_pairs={{32,0},{64,32},{96,64},{128,96},{160,128},{192,160},{224,192},{33,... | collective-permute-start | bytes 393224 | tf_op jit(solution)/shard_map/while/body/eval_jaxpr/ppermute | solution.py:21
  777.0 17.0 %collective-permute-start.1 = (bf16[32,2048]{1,0:T(8,128)(2,1)S(1)}, bf16[32,2048]{1,0:T(8,128)(2,1)S(1)}, u32[]{:S(2)}, u32[]{:S(2)}) collective-permute-start(bf16[32,2048]{1,0:T(8,128)(2,1)S(1)} %fusion.135), channel_id=1, source_target_pairs={{32,0},{64,32},{96,64},{128,96},{160,128},{192,160},{224,192},{33,... | collective-permute-start | bytes 393224 | tf_op jit(solution)/shard_map/while/body/eval_jaxpr/ppermute | solution.py:21
  837.8 17.0 %collective-permute-start.1 = (bf16[32,2048]{1,0:T(8,128)(2,1)S(1)}, bf16[32,2048]{1,0:T(8,128)(2,1)S(1)}, u32[]{:S(2)}, u32[]{:S(2)}) collective-permute-start(bf16[32,2048]{1,0:T(8,128)(2,1)S(1)} %fusion.135), channel_id=1, source_target_pairs={{32,0},{64,32},{96,64},{128,96},{160,128},{192,160},{224,192},{33,... | collective-permute-start | bytes 393224 | tf_op jit(solution)/shard_map/while/body/eval_jaxpr/ppermute | solution.py:21
  898.7 17.0 %collective-permute-start.1 = (bf16[32,2048]{1,0:T(8,128)(2,1)S(1)}, bf16[32,2048]{1,0:T(8,128)(2,1)S(1)}, u32[]{:S(2)}, u32[]{:S(2)}) collective-permute-start(bf16[32,2048]{1,0:T(8,128)(2,1)S(1)} %fusion.135), channel_id=1, source_target_pairs={{32,0},{64,32},{96,64},{128,96},{160,128},{192,160},{224,192},{33,... | collective-permute-start | bytes 393224 | tf_op jit(solution)/shard_map/while/body/eval_jaxpr/ppermute | solution.py:21
  965.1 17.2 %collective-permute-start.1 = (bf16[32,2048]{1,0:T(8,128)(2,1)S(1)}, bf16[32,2048]{1,0:T(8,128)(2,1)S(1)}, u32[]{:S(2)}, u32[]{:S(2)}) collective-permute-start(bf16[32,2048]{1,0:T(8,128)(2,1)S(1)} %fusion.135), channel_id=1, source_target_pairs={{32,0},{64,32},{96,64},{128,96},{160,128},{192,160},{224,192},{33,... | collective-permute-start | bytes 393224 | tf_op jit(solution)/shard_map/while/body/eval_jaxpr/ppermute | solution.py:21
  1031.8 17.1 %collective-permute-start.1 = (bf16[32,2048]{1,0:T(8,128)(2,1)S(1)}, bf16[32,2048]{1,0:T(8,128)(2,1)S(1)}, u32[]{:S(2)}, u32[]{:S(2)}) collective-permute-start(bf16[32,2048]{1,0:T(8,128)(2,1)S(1)} %fusion.135), channel_id=1, source_target_pairs={{32,0},{64,32},{96,64},{128,96},{160,128},{192,160},{224,192},{33,... | collective-permute-start | bytes 393224 | tf_op jit(solution)/shard_map/while/body/eval_jaxpr/ppermute | solution.py:21
  1098.3 17.0 %collective-permute-start.1 = (bf16[32,2048]{1,0:T(8,128)(2,1)S(1)}, bf16[32,2048]{1,0:T(8,128)(2,1)S(1)}, u32[]{:S(2)}, u32[]{:S(2)}) collective-permute-start(bf16[32,2048]{1,0:T(8,128)(2,1)S(1)} %fusion.135), channel_id=1, source_target_pairs={{32,0},{64,32},{96,64},{128,96},{160,128},{192,160},{224,192},{33,... | collective-permute-start | bytes 393224 | tf_op jit(solution)/shard_map/while/body/eval_jaxpr/ppermute | solution.py:21
  1164.7 17.0 %collective-permute-start.1 = (bf16[32,2048]{1,0:T(8,128)(2,1)S(1)}, bf16[32,2048]{1,0:T(8,128)(2,1)S(1)}, u32[]{:S(2)}, u32[]{:S(2)}) collective-permute-start(bf16[32,2048]{1,0:T(8,128)(2,1)S(1)} %fusion.135), channel_id=1, source_target_pairs={{32,0},{64,32},{96,64},{128,96},{160,128},{192,160},{224,192},{33,... | collective-permute-start | bytes 393224 | tf_op jit(solution)/shard_map/while/body/eval_jaxpr/ppermute | solution.py:21
  1225.6 17.1 %collective-permute-start.1 = (bf16[32,2048]{1,0:T(8,128)(2,1)S(1)}, bf16[32,2048]{1,0:T(8,128)(2,1)S(1)}, u32[]{:S(2)}, u32[]{:S(2)}) collective-permute-start(bf16[32,2048]{1,0:T(8,128)(2,1)S(1)} %fusion.135), channel_id=1, source_target_pairs={{32,0},{64,32},{96,64},{128,96},{160,128},{192,160},{224,192},{33,... | collective-permute-start | bytes 393224 | tf_op jit(solution)/shard_map/while/body/eval_jaxpr/ppermute | solution.py:21
  1286.6 17.1 %collective-permute-start.1 = (bf16[32,2048]{1,0:T(8,128)(2,1)S(1)}, bf16[32,2048]{1,0:T(8,128)(2,1)S(1)}, u32[]{:S(2)}, u32[]{:S(2)}) collective-permute-start(bf16[32,2048]{1,0:T(8,128)(2,1)S(1)} %fusion.135), channel_id=1, source_target_pairs={{32,0},{64,32},{96,64},{128,96},{160,128},{192,160},{224,192},{33,... | collective-permute-start | bytes 393224 | tf_op jit(solution)/shard_map/while/body/eval_jaxpr/ppermute | solution.py:21
  1347.7 17.0 %collective-permute-start.1 = (bf16[32,2048]{1,0:T(8,128)(2,1)S(1)}, bf16[32,2048]{1,0:T(8,128)(2,1)S(1)}, u32[]{:S(2)}, u32[]{:S(2)}) collective-permute-start(bf16[32,2048]{1,0:T(8,128)(2,1)S(1)} %fusion.135), channel_id=1, source_target_pairs={{32,0},{64,32},{96,64},{128,96},{160,128},{192,160},{224,192},{33,... | collective-permute-start | bytes 393224 | tf_op jit(solution)/shard_map/while/body/eval_jaxpr/ppermute | solution.py:21
  1381.0 15.1 %collective-permute-start.8 = (bf16[512,512]{1,0:T(8,128)(2,1)S(1)}, bf16[512,512]{1,0:T(8,128)(2,1)S(1)}, u32[]{:S(2)}, u32[]{:S(2)}) collective-permute-start(bf16[512,512]{1,0:T(8,128)(2,1)S(1)} %fusion.87), channel_id=1, source_target_pairs={{0,24},{8,0},{16,8},{24,16},{1,25},{9,1},{17,9},{25,17},{2,26},{10... | collective-permute-start | bytes 1572872 | tf_op jit(solution)/shard_map/ppermute | solution.py:80
  1383.3 14.4 collective-permute-start.2
  1397.5 14.3 collective-permute-start.9
  1453.9 18.0 %collective-permute-start.7 = (bf16[512,512]{1,0:T(8,128)(2,1)}, bf16[512,512]{1,0:T(8,128)(2,1)}, u32[]{:S(2)}, u32[]{:S(2)}) collective-permute-start(bf16[512,512]{1,0:T(8,128)(2,1)} %collective-permute-done.6), channel_id=1, source_target_pairs={{0,8},{8,16},{16,24},{24,0},{1,9},{9,17},{17,25},{25,1},{2,10},{10... | collective-permute-start | bytes 1572872 | tf_op jit(solution)/shard_map/ppermute | solution.py:86
  (12 other events, 134.4 us)

commit v10 on v9

--- a/solution.py
+++ b/solution.py
@@ -205,15 +205,11 @@
         dinbuf = jnp.einsum(
             "sech,edh->secd", dpre, w_up, preferred_element_type=jnp.float32
         ).astype(jnp.bfloat16)
-        return (dinbuf, dpre, dreceived)
+        return (dinbuf, dpre)
 
     def backward_skip(operands):
         dreceived, preact = operands
-        return (
-            jnp.zeros_like(dreceived),
-            jnp.zeros(preact.shape, jnp.bfloat16),
-            jnp.zeros_like(dreceived),
-        )
+        return (jnp.zeros_like(dreceived), jnp.zeros(preact.shape, jnp.bfloat16))
 
     def backward_step(incoming, step_index):
         micro_raw = step_index - (section_count - 1 - section_pos)
@@ -245,7 +241,7 @@
         def backward_live(operands):
             return expert_backward(operands[0], operands[1])
 
-        dinbuf, dpre, dkept = lax.cond(live_step, backward_live, backward_skip, (dreceived, preact))
+        dinbuf, dpre = lax.cond(live_step, backward_live, backward_skip, (dreceived, preact))
         dreturned = expert_exchange(as_pieces(dinbuf), 2)
         dexp = jnp.sum(from_buffer(dreturned, dest_rows).astype(jnp.float32), axis=1)
         dgate = (dwgt - jnp.sum(wgt * dwgt, axis=-1, keepdims=True)) / total
@@ -260,7 +256,7 @@
             - as_f32 * rscale**3 * jnp.mean(dnorm * as_f32, axis=-1, keepdims=True)
         ).astype(jnp.bfloat16)
         passed = from_behind(grad_in, "section", -1)
-        return (passed, (dpre, dkept))
+        return (passed, (dpre, dreceived))
 
     start_grad = jnp.zeros((tok_rows, features), jnp.bfloat16)
     _, (dpre_all, dreceived_all) = lax.scan(backward_step, start_grad, jnp.arange(step_count))

time: 1480 us -> 1480 us (level)
  no operation moved by 1% of the time
where the time goes in v10:
time: 1480 us
  Pallas kernels  646 us (44%)
  local copies, waits for them, and re-layouts  265 us (18%)
  waiting for transfers between devices  209 us (14%)
  starting transfers between devices  153 us (10%)
  other arithmetic  117 us (8%)
  matrix products  65.8 us (4%)
  loops' own time  19.4 us (1%)
    pallas_call x44, Pallas kernels, expert_exchange(): pl.pallas_call(functools.partial(exchange_kernel, n), out_shape=jax.Shape...  646 us
    ppermute x22, waiting for transfers between devices, from_behind(): return lax.ppermute(block, axis, route)  159 us
    ppermute x22, starting transfers between devices, from_behind(): return lax.ppermute(block, axis, route)  132 us
    dynamic_update_slice x44, local copies, waits for them, and re-layouts, local(): _, saved = lax.scan(forward_step, start_act, jnp.arange(step_count))  52.2 us
    gather x22, local copies, waits for them, and re-layouts, from_buffer(): buffer.reshape(experts_all * capacity, pieces, lanes)[dest_rows]  38.6 us
  transfers between devices with their start and end apart: 34, of which 29 were waited for; matrix products, arithmetic and copies ran while one was open for 7% of the time, Pallas kernels for 0%

profile of v10, /device:TPU:62, one launch (start us, length us, event | category | flops | bytes accessed | tf_op | source)
XLA Modules:
  0.0 1476.2 jit_solution(8853098148482230523)
XLA Ops:
  7.0 659.9 %while.39 = (s32[]{:T(128)}, bf16[32,2048]{1,0:T(8,128)(2,1)S(1)}, bf16[11,32,2048]{2,1,0:T(8,128)(2,1)}, f32[11,32,4]{1,2,0:T(4,128)S(1)}, bf16[11,32,4,2048]{3...) while((s32[]{:T(128)}, bf16[32,2048]{1,0:T(8,128)(2,1)S(1)}, ...), condition=%wide.region_9.10_spmd, body=%wide.region_3.9_spmd.sunk | while | flops 573976576 | bytes 24260048 | solution.py:197
  12.4 16.2 %eval_jaxpr.16 = bf16[8,272,128]{2,1,0:T(8,128)(2,1)S(1)} custom-call(bf16[8,272,128]{2,1,0:T(8,128)(2,1)} %bitcast_select_fusion.8.x_ref), custom_call_target="tpu_custom_call" | custom-call | bytes 1114112 | tf_op jit(solution)/shard_map/while/body/eval_jaxpr/pallas_call | solution.py:55
  30.6 15.7 %eval_jaxpr.17 = bf16[8,272,128]{2,1,0:T(8,128)(2,1)} custom-call(bf16[8,272,128]{2,1,0:T(8,128)(2,1)} %reshape.677.x_ref), custom_call_target="tpu_custom_call" | custom-call | bytes 1114112 | tf_op jit(solution)/shard_map/while/body/eval_jaxpr/pallas_call | solution.py:55
  85.4 14.9 %eval_jaxpr.17 = bf16[8,272,128]{2,1,0:T(8,128)(2,1)} custom-call(bf16[8,272,128]{2,1,0:T(8,128)(2,1)} %reshape.677.x_ref), custom_call_target="tpu_custom_call" | custom-call | bytes 1114112 | tf_op jit(solution)/shard_map/while/body/eval_jaxpr/pallas_call | solution.py:55
  143.8 14.9 %eval_jaxpr.17 = bf16[8,272,128]{2,1,0:T(8,128)(2,1)} custom-call(bf16[8,272,128]{2,1,0:T(8,128)(2,1)} %reshape.677.x_ref), custom_call_target="tpu_custom_call" | custom-call | bytes 1114112 | tf_op jit(solution)/shard_map/while/body/eval_jaxpr/pallas_call | solution.py:55
  207.0 14.9 %eval_jaxpr.17 = bf16[8,272,128]{2,1,0:T(8,128)(2,1)} custom-call(bf16[8,272,128]{2,1,0:T(8,128)(2,1)} %reshape.677.x_ref), custom_call_target="tpu_custom_call" | custom-call | bytes 1114112 | tf_op jit(solution)/shard_map/while/body/eval_jaxpr/pallas_call | solution.py:55
  265.4 14.9 %eval_jaxpr.17 = bf16[8,272,128]{2,1,0:T(8,128)(2,1)} custom-call(bf16[8,272,128]{2,1,0:T(8,128)(2,1)} %reshape.677.x_ref), custom_call_target="tpu_custom_call" | custom-call | bytes 1114112 | tf_op jit(solution)/shard_map/while/body/eval_jaxpr/pallas_call | solution.py:55
  328.6 14.9 %eval_jaxpr.17 = bf16[8,272,128]{2,1,0:T(8,128)(2,1)} custom-call(bf16[8,272,128]{2,1,0:T(8,128)(2,1)} %reshape.677.x_ref), custom_call_target="tpu_custom_call" | custom-call | bytes 1114112 | tf_op jit(solution)/shard_map/while/body/eval_jaxpr/pallas_call | solution.py:55
  391.8 14.9 %eval_jaxpr.17 = bf16[8,272,128]{2,1,0:T(8,128)(2,1)} custom-call(bf16[8,272,128]{2,1,0:T(8,128)(2,1)} %reshape.677.x_ref), custom_call_target="tpu_custom_call" | custom-call | bytes 1114112 | tf_op jit(solution)/shard_map/while/body/eval_jaxpr/pallas_call | solution.py:55
  450.3 14.9 %eval_jaxpr.17 = bf16[8,272,128]{2,1,0:T(8,128)(2,1)} custom-call(bf16[8,272,128]{2,1,0:T(8,128)(2,1)} %reshape.677.x_ref), custom_call_target="tpu_custom_call" | custom-call | bytes 1114112 | tf_op jit(solution)/shard_map/while/body/eval_jaxpr/pallas_call | solution.py:55
  470.0 15.1 %collective-permute-start = (bf16[32,2048]{1,0:T(8,128)(2,1)S(1)}, bf16[32,2048]{1,0:T(8,128)(2,1)S(1)}, u32[]{:S(2)}, u32[]{:S(2)}) collective-permute-start(bf16[32,2048]{1,0:T(8,128)(2,1)S(1)} %fusion.124), channel_id=1, source_target_pairs={{0,32},{32,64},{64,96},{96,128},{128,160},{160,192},{192,224},{1,3... | collective-permute-start | bytes 393224 | tf_op jit(solution)/shard_map/while/body/eval_jaxpr/ppermute | solution.py:21
  513.4 14.9 %eval_jaxpr.17 = bf16[8,272,128]{2,1,0:T(8,128)(2,1)} custom-call(bf16[8,272,128]{2,1,0:T(8,128)(2,1)} %reshape.677.x_ref), custom_call_target="tpu_custom_call" | custom-call | bytes 1114112 | tf_op jit(solution)/shard_map/while/body/eval_jaxpr/pallas_call | solution.py:55
  571.7 14.9 %eval_jaxpr.17 = bf16[8,272,128]{2,1,0:T(8,128)(2,1)} custom-call(bf16[8,272,128]{2,1,0:T(8,128)(2,1)} %reshape.677.x_ref), custom_call_target="tpu_custom_call" | custom-call | bytes 1114112 | tf_op jit(solution)/shard_map/while/body/eval_jaxpr/pallas_call | solution.py:55
  630.2 14.9 %eval_jaxpr.17 = bf16[8,272,128]{2,1,0:T(8,128)(2,1)} custom-call(bf16[8,272,128]{2,1,0:T(8,128)(2,1)} %reshape.677.x_ref), custom_call_target="tpu_custom_call" | custom-call | bytes 1114112 | tf_op jit(solution)/shard_map/while/body/eval_jaxpr/pallas_call | solution.py:55
  671.3 691.6 %while.40 = (s32[]{:T(128)}, bf16[32,2048]{1,0:T(8,128)(2,1)S(1)}, bf16[11,8,1,17,512]{4,3,1,2,0:T(8,128)(2,1)}, bf16[11,8,1,17,2048]{4,3,1,2,0:T(8,128)(2,1)}, ...) while((s32[]{:T(128)}, bf16[32,2048]{1,0:T(8,128)(2,1)S(1)}, ...), condition=%wide.region_20.21_spmd.clone, body=%wide.region_10.20_spmd.clone.sunk | while | flops 581163648 | bytes 27663024 | solution.py:262
  693.7 14.9 %eval_jaxpr.19 = bf16[8,272,128]{2,1,0:T(8,128)(2,1)} custom-call(bf16[8,272,128]{2,1,0:T(8,128)(2,1)} %reshape.685.x_ref), custom_call_target="tpu_custom_call" | custom-call | bytes 1114112 | tf_op jit(solution)/shard_map/while/body/eval_jaxpr/pallas_call | solution.py:55
  755.2 14.9 %eval_jaxpr.19 = bf16[8,272,128]{2,1,0:T(8,128)(2,1)} custom-call(bf16[8,272,128]{2,1,0:T(8,128)(2,1)} %reshape.685.x_ref), custom_call_target="tpu_custom_call" | custom-call | bytes 1114112 | tf_op jit(solution)/shard_map/while/body/eval_jaxpr/pallas_call | solution.py:55
  816.0 14.9 %eval_jaxpr.19 = bf16[8,272,128]{2,1,0:T(8,128)(2,1)} custom-call(bf16[8,272,128]{2,1,0:T(8,128)(2,1)} %reshape.685.x_ref), custom_call_target="tpu_custom_call" | custom-call | bytes 1114112 | tf_op jit(solution)/shard_map/while/body/eval_jaxpr/pallas_call | solution.py:55
  876.8 14.9 %eval_jaxpr.19 = bf16[8,272,128]{2,1,0:T(8,128)(2,1)} custom-call(bf16[8,272,128]{2,1,0:T(8,128)(2,1)} %reshape.685.x_ref), custom_call_target="tpu_custom_call" | custom-call | bytes 1114112 | tf_op jit(solution)/shard_map/while/body/eval_jaxpr/pallas_call | solution.py:55
  942.9 14.9 %eval_jaxpr.19 = bf16[8,272,128]{2,1,0:T(8,128)(2,1)} custom-call(bf16[8,272,128]{2,1,0:T(8,128)(2,1)} %reshape.685.x_ref), custom_call_target="tpu_custom_call" | custom-call | bytes 1114112 | tf_op jit(solution)/shard_map/while/body/eval_jaxpr/pallas_call | solution.py:55
  1009.3 14.9 %eval_jaxpr.19 = bf16[8,272,128]{2,1,0:T(8,128)(2,1)} custom-call(bf16[8,272,128]{2,1,0:T(8,128)(2,1)} %reshape.685.x_ref), custom_call_target="tpu_custom_call" | custom-call | bytes 1114112 | tf_op jit(solution)/shard_map/while/body/eval_jaxpr/pallas_call | solution.py:55
  1075.5 14.9 %eval_jaxpr.19 = bf16[8,272,128]{2,1,0:T(8,128)(2,1)} custom-call(bf16[8,272,128]{2,1,0:T(8,128)(2,1)} %reshape.685.x_ref), custom_call_target="tpu_custom_call" | custom-call | bytes 1114112 | tf_op jit(solution)/shard_map/while/body/eval_jaxpr/pallas_call | solution.py:55
  1141.7 14.9 %eval_jaxpr.19 = bf16[8,272,128]{2,1,0:T(8,128)(2,1)} custom-call(bf16[8,272,128]{2,1,0:T(8,128)(2,1)} %reshape.685.x_ref), custom_call_target="tpu_custom_call" | custom-call | bytes 1114112 | tf_op jit(solution)/shard_map/while/body/eval_jaxpr/pallas_call | solution.py:55
  1202.5 14.9 %eval_jaxpr.19 = bf16[8,272,128]{2,1,0:T(8,128)(2,1)} custom-call(bf16[8,272,128]{2,1,0:T(8,128)(2,1)} %reshape.685.x_ref), custom_call_target="tpu_custom_call" | custom-call | bytes 1114112 | tf_op jit(solution)/shard_map/while/body/eval_jaxpr/pallas_call | solution.py:55
  (1053 shorter events, 1184.4 us)
Async XLA Ops:
  105.0 17.0 %collective-permute-start = (bf16[32,2048]{1,0:T(8,128)(2,1)S(1)}, bf16[32,2048]{1,0:T(8,128)(2,1)S(1)}, u32[]{:S(2)}, u32[]{:S(2)}) collective-permute-start(bf16[32,2048]{1,0:T(8,128)(2,1)S(1)} %fusion.124), channel_id=1, source_target_pairs={{0,32},{32,64},{64,96},{96,128},{128,160},{160,192},{192,224},{1,3... | collective-permute-start | bytes 393224 | tf_op jit(solution)/shard_map/while/body/eval_jaxpr/ppermute | solution.py:21
  163.4 17.1 %collective-permute-start = (bf16[32,2048]{1,0:T(8,128)(2,1)S(1)}, bf16[32,2048]{1,0:T(8,128)(2,1)S(1)}, u32[]{:S(2)}, u32[]{:S(2)}) collective-permute-start(bf16[32,2048]{1,0:T(8,128)(2,1)S(1)} %fusion.124), channel_id=1, source_target_pairs={{0,32},{32,64},{64,96},{96,128},{128,160},{160,192},{192,224},{1,3... | collective-permute-start | bytes 393224 | tf_op jit(solution)/shard_map/while/body/eval_jaxpr/ppermute | solution.py:21
  285.0 17.1 %collective-permute-start = (bf16[32,2048]{1,0:T(8,128)(2,1)S(1)}, bf16[32,2048]{1,0:T(8,128)(2,1)S(1)}, u32[]{:S(2)}, u32[]{:S(2)}) collective-permute-start(bf16[32,2048]{1,0:T(8,128)(2,1)S(1)} %fusion.124), channel_id=1, source_target_pairs={{0,32},{32,64},{64,96},{96,128},{128,160},{160,192},{192,224},{1,3... | collective-permute-start | bytes 393224 | tf_op jit(solution)/shard_map/while/body/eval_jaxpr/ppermute | solution.py:21
  348.2 17.2 %collective-permute-start = (bf16[32,2048]{1,0:T(8,128)(2,1)S(1)}, bf16[32,2048]{1,0:T(8,128)(2,1)S(1)}, u32[]{:S(2)}, u32[]{:S(2)}) collective-permute-start(bf16[32,2048]{1,0:T(8,128)(2,1)S(1)} %fusion.124), channel_id=1, source_target_pairs={{0,32},{32,64},{64,96},{96,128},{128,160},{160,192},{192,224},{1,3... | collective-permute-start | bytes 393224 | tf_op jit(solution)/shard_map/while/body/eval_jaxpr/ppermute | solution.py:21
  411.5 17.1 %collective-permute-start = (bf16[32,2048]{1,0:T(8,128)(2,1)S(1)}, bf16[32,2048]{1,0:T(8,128)(2,1)S(1)}, u32[]{:S(2)}, u32[]{:S(2)}) collective-permute-start(bf16[32,2048]{1,0:T(8,128)(2,1)S(1)} %fusion.124), channel_id=1, source_target_pairs={{0,32},{32,64},{64,96},{96,128},{128,160},{160,192},{192,224},{1,3... | collective-permute-start | bytes 393224 | tf_op jit(solution)/shard_map/while/body/eval_jaxpr/ppermute | solution.py:21
  470.0 21.7 %collective-permute-start = (bf16[32,2048]{1,0:T(8,128)(2,1)S(1)}, bf16[32,2048]{1,0:T(8,128)(2,1)S(1)}, u32[]{:S(2)}, u32[]{:S(2)}) collective-permute-start(bf16[32,2048]{1,0:T(8,128)(2,1)S(1)} %fusion.124), channel_id=1, source_target_pairs={{0,32},{32,64},{64,96},{96,128},{128,160},{160,192},{192,224},{1,3... | collective-permute-start | bytes 393224 | tf_op jit(solution)/shard_map/while/body/eval_jaxpr/ppermute | solution.py:21
  533.0 17.0 %collective-permute-start = (bf16[32,2048]{1,0:T(8,128)(2,1)S(1)}, bf16[32,2048]{1,0:T(8,128)(2,1)S(1)}, u32[]{:S(2)}, u32[]{:S(2)}) collective-permute-start(bf16[32,2048]{1,0:T(8,128)(2,1)S(1)} %fusion.124), channel_id=1, source_target_pairs={{0,32},{32,64},{64,96},{96,128},{128,160},{160,192},{192,224},{1,3... | collective-permute-start | bytes 393224 | tf_op jit(solution)/shard_map/while/body/eval_jaxpr/ppermute | solution.py:21
  591.3 17.1 %collective-permute-start = (bf16[32,2048]{1,0:T(8,128)(2,1)S(1)}, bf16[32,2048]{1,0:T(8,128)(2,1)S(1)}, u32[]{:S(2)}, u32[]{:S(2)}) collective-permute-start(bf16[32,2048]{1,0:T(8,128)(2,1)S(1)} %fusion.124), channel_id=1, source_target_pairs={{0,32},{32,64},{64,96},{96,128},{128,160},{160,192},{192,224},{1,3... | collective-permute-start | bytes 393224 | tf_op jit(solution)/shard_map/while/body/eval_jaxpr/ppermute | solution.py:21
  649.8 17.1 %collective-permute-start = (bf16[32,2048]{1,0:T(8,128)(2,1)S(1)}, bf16[32,2048]{1,0:T(8,128)(2,1)S(1)}, u32[]{:S(2)}, u32[]{:S(2)}) collective-permute-start(bf16[32,2048]{1,0:T(8,128)(2,1)S(1)} %fusion.124), channel_id=1, source_target_pairs={{0,32},{32,64},{64,96},{96,128},{128,160},{160,192},{192,224},{1,3... | collective-permute-start | bytes 393224 | tf_op jit(solution)/shard_map/while/body/eval_jaxpr/ppermute | solution.py:21
  715.3 17.6 %collective-permute-start.1 = (bf16[32,2048]{1,0:T(8,128)(2,1)S(1)}, bf16[32,2048]{1,0:T(8,128)(2,1)S(1)}, u32[]{:S(2)}, u32[]{:S(2)}) collective-permute-start(bf16[32,2048]{1,0:T(8,128)(2,1)S(1)} %fusion.135), channel_id=1, source_target_pairs={{32,0},{64,32},{96,64},{128,96},{160,128},{192,160},{224,192},{33,... | collective-permute-start | bytes 393224 | tf_op jit(solution)/shard_map/while/body/eval_jaxpr/ppermute | solution.py:21
  776.8 17.0 %collective-permute-start.1 = (bf16[32,2048]{1,0:T(8,128)(2,1)S(1)}, bf16[32,2048]{1,0:T(8,128)(2,1)S(1)}, u32[]{:S(2)}, u32[]{:S(2)}) collective-permute-start(bf16[32,2048]{1,0:T(8,128)(2,1)S(1)} %fusion.135), channel_id=1, source_target_pairs={{32,0},{64,32},{96,64},{128,96},{160,128},{192,160},{224,192},{33,... | collective-permute-start | bytes 393224 | tf_op jit(solution)/shard_map/while/body/eval_jaxpr/ppermute | solution.py:21
  837.6 17.0 %collective-permute-start.1 = (bf16[32,2048]{1,0:T(8,128)(2,1)S(1)}, bf16[32,2048]{1,0:T(8,128)(2,1)S(1)}, u32[]{:S(2)}, u32[]{:S(2)}) collective-permute-start(bf16[32,2048]{1,0:T(8,128)(2,1)S(1)} %fusion.135), channel_id=1, source_target_pairs={{32,0},{64,32},{96,64},{128,96},{160,128},{192,160},{224,192},{33,... | collective-permute-start | bytes 393224 | tf_op jit(solution)/shard_map/while/body/eval_jaxpr/ppermute | solution.py:21
  898.4 17.0 %collective-permute-start.1 = (bf16[32,2048]{1,0:T(8,128)(2,1)S(1)}, bf16[32,2048]{1,0:T(8,128)(2,1)S(1)}, u32[]{:S(2)}, u32[]{:S(2)}) collective-permute-start(bf16[32,2048]{1,0:T(8,128)(2,1)S(1)} %fusion.135), channel_id=1, source_target_pairs={{32,0},{64,32},{96,64},{128,96},{160,128},{192,160},{224,192},{33,... | collective-permute-start | bytes 393224 | tf_op jit(solution)/shard_map/while/body/eval_jaxpr/ppermute | solution.py:21
  964.5 17.2 %collective-permute-start.1 = (bf16[32,2048]{1,0:T(8,128)(2,1)S(1)}, bf16[32,2048]{1,0:T(8,128)(2,1)S(1)}, u32[]{:S(2)}, u32[]{:S(2)}) collective-permute-start(bf16[32,2048]{1,0:T(8,128)(2,1)S(1)} %fusion.135), channel_id=1, source_target_pairs={{32,0},{64,32},{96,64},{128,96},{160,128},{192,160},{224,192},{33,... | collective-permute-start | bytes 393224 | tf_op jit(solution)/shard_map/while/body/eval_jaxpr/ppermute | solution.py:21
  1030.9 17.1 %collective-permute-start.1 = (bf16[32,2048]{1,0:T(8,128)(2,1)S(1)}, bf16[32,2048]{1,0:T(8,128)(2,1)S(1)}, u32[]{:S(2)}, u32[]{:S(2)}) collective-permute-start(bf16[32,2048]{1,0:T(8,128)(2,1)S(1)} %fusion.135), channel_id=1, source_target_pairs={{32,0},{64,32},{96,64},{128,96},{160,128},{192,160},{224,192},{33,... | collective-permute-start | bytes 393224 | tf_op jit(solution)/shard_map/while/body/eval_jaxpr/ppermute | solution.py:21
  1097.2 17.0 %collective-permute-start.1 = (bf16[32,2048]{1,0:T(8,128)(2,1)S(1)}, bf16[32,2048]{1,0:T(8,128)(2,1)S(1)}, u32[]{:S(2)}, u32[]{:S(2)}) collective-permute-start(bf16[32,2048]{1,0:T(8,128)(2,1)S(1)} %fusion.135), channel_id=1, source_target_pairs={{32,0},{64,32},{96,64},{128,96},{160,128},{192,160},{224,192},{33,... | collective-permute-start | bytes 393224 | tf_op jit(solution)/shard_map/while/body/eval_jaxpr/ppermute | solution.py:21
  1163.3 17.0 %collective-permute-start.1 = (bf16[32,2048]{1,0:T(8,128)(2,1)S(1)}, bf16[32,2048]{1,0:T(8,128)(2,1)S(1)}, u32[]{:S(2)}, u32[]{:S(2)}) collective-permute-start(bf16[32,2048]{1,0:T(8,128)(2,1)S(1)} %fusion.135), channel_id=1, source_target_pairs={{32,0},{64,32},{96,64},{128,96},{160,128},{192,160},{224,192},{33,... | collective-permute-start | bytes 393224 | tf_op jit(solution)/shard_map/while/body/eval_jaxpr/ppermute | solution.py:21
  1224.1 17.1 %collective-permute-start.1 = (bf16[32,2048]{1,0:T(8,128)(2,1)S(1)}, bf16[32,2048]{1,0:T(8,128)(2,1)S(1)}, u32[]{:S(2)}, u32[]{:S(2)}) collective-permute-start(bf16[32,2048]{1,0:T(8,128)(2,1)S(1)} %fusion.135), channel_id=1, source_target_pairs={{32,0},{64,32},{96,64},{128,96},{160,128},{192,160},{224,192},{33,... | collective-permute-start | bytes 393224 | tf_op jit(solution)/shard_map/while/body/eval_jaxpr/ppermute | solution.py:21
  1285.0 17.1 %collective-permute-start.1 = (bf16[32,2048]{1,0:T(8,128)(2,1)S(1)}, bf16[32,2048]{1,0:T(8,128)(2,1)S(1)}, u32[]{:S(2)}, u32[]{:S(2)}) collective-permute-start(bf16[32,2048]{1,0:T(8,128)(2,1)S(1)} %fusion.135), channel_id=1, source_target_pairs={{32,0},{64,32},{96,64},{128,96},{160,128},{192,160},{224,192},{33,... | collective-permute-start | bytes 393224 | tf_op jit(solution)/shard_map/while/body/eval_jaxpr/ppermute | solution.py:21
  1346.0 17.0 %collective-permute-start.1 = (bf16[32,2048]{1,0:T(8,128)(2,1)S(1)}, bf16[32,2048]{1,0:T(8,128)(2,1)S(1)}, u32[]{:S(2)}, u32[]{:S(2)}) collective-permute-start(bf16[32,2048]{1,0:T(8,128)(2,1)S(1)} %fusion.135), channel_id=1, source_target_pairs={{32,0},{64,32},{96,64},{128,96},{160,128},{192,160},{224,192},{33,... | collective-permute-start | bytes 393224 | tf_op jit(solution)/shard_map/while/body/eval_jaxpr/ppermute | solution.py:21
  1379.3 15.1 %collective-permute-start.8 = (bf16[512,512]{1,0:T(8,128)(2,1)S(1)}, bf16[512,512]{1,0:T(8,128)(2,1)S(1)}, u32[]{:S(2)}, u32[]{:S(2)}) collective-permute-start(bf16[512,512]{1,0:T(8,128)(2,1)S(1)} %fusion.87), channel_id=1, source_target_pairs={{0,24},{8,0},{16,8},{24,16},{1,25},{9,1},{17,9},{25,17},{2,26},{10... | collective-permute-start | bytes 1572872 | tf_op jit(solution)/shard_map/ppermute | solution.py:80
  1381.5 14.4 collective-permute-start.2
  1395.8 14.2 collective-permute-start.9
  1452.2 18.0 %collective-permute-start.7 = (bf16[512,512]{1,0:T(8,128)(2,1)}, bf16[512,512]{1,0:T(8,128)(2,1)}, u32[]{:S(2)}, u32[]{:S(2)}) collective-permute-start(bf16[512,512]{1,0:T(8,128)(2,1)} %collective-permute-done.6), channel_id=1, source_target_pairs={{0,8},{8,16},{16,24},{24,0},{1,9},{9,17},{17,25},{25,1},{2,10},{10... | collective-permute-start | bytes 1572872 | tf_op jit(solution)/shard_map/ppermute | solution.py:86
  (12 other events, 134.3 us)
